TPU v7x, 512 devices: a whole 4x8x8 slice. The times are simulated.
512 devices in a mesh: dom: 16 (over z_lo, x, core), band: 32 (over z_hi, y).
Axes of the slice: x: 4, y: 8, z: 8 (z_hi: 4, z_lo: 2; z = z_hi * 2 + z_lo), core: 2. Of those that a mesh axis runs over, the one named last changes fastest.
Arguments:
- orbitals: bfloat16 [1024, 16, 2, 16, 128], P('band', 'dom'), may hold values from -6 to 6
- potential: float32 [16, 2, 16, 128], P('dom'), may hold values from -1 to 1
- ritz: bfloat16 [1024, 1024], P(None, 'band'), may hold values from -0.1875 to 0.1875
Outputs:
- rotated: float32 [1024, 16, 2, 16, 128], P('band', 'dom')
All inputs are finite; a program needn't handle non-finite values.
Results may differ from a plain program's by a relative error of at most 0.0029.
Values may be sent and summed in bfloat16 or wider, within the bound.
No kernel may reach another device: no remote copies, remote signals or barrier semaphores. Data moves between devices by JAX's collectives and lax.ppermute only.
A program may use at most 64 MiB of HBM per device.

v0:
```python
import math

import jax
import jax.numpy as jnp
from jax import lax
from jax.sharding import PartitionSpec as P

DEG = 4


lower_bound = -1.5
cut_off = 1.0
upper_bound = 9.5
coef_zero = -2.5
coef_one = 4.0 / 3.0
coef_two = -1.0 / 12.0


def shifted(value, axis, steps):
    count = lax.axis_size(axis)
    pairs = [(source, (source + steps) % count) for source in range(count)]
    return lax.ppermute(value, axis, pairs)


def filter_weights(degree):
    half_width = (upper_bound - cut_off) / 2.0
    centre = (upper_bound + cut_off) / 2.0
    sigma_now = half_width / (lower_bound - centre)
    first_scale = sigma_now / half_width
    inverse_gain = 2.0 / sigma_now
    weights = []
    for degree_step in range(1, degree):
        sigma_next = 1.0 / (inverse_gain - sigma_now)
        weights.append((2.0 * sigma_next / half_width, sigma_now * sigma_next))
        sigma_now = sigma_next
    return (centre, first_scale, weights)


def send_first(face, offset):
    return shifted(face, "dom", offset)


def send_second(face, offset):
    return shifted(face, "dom", offset)


def padded_second(padded, count, axis):
    lower_near = lax.slice_in_dim(padded, 1, count + 1, axis=axis)
    upper_near = lax.slice_in_dim(padded, 3, count + 3, axis=axis)
    lower_far = lax.slice_in_dim(padded, 0, count, axis=axis)
    upper_far = lax.slice_in_dim(padded, 4, count + 4, axis=axis)
    return coef_one * (lower_near + upper_near) + coef_two * (lower_far + upper_far)


def apply_ham(field_now, local_pot, grid_side, row_y):
    cells_x = field_now.shape[1]
    cells_y = field_now.shape[2]
    low_x = send_first(field_now, grid_side)
    high_x = send_first(field_now, -grid_side)
    along_x = jnp.concatenate([low_x, field_now, high_x], axis=1)
    top_y = field_now[:, :, cells_y - 2 :]
    bottom_y = field_now[:, :, :2]
    low_y = jnp.where(row_y == 0, send_second(top_y, 1 - grid_side), send_second(top_y, 1))
    high_y = jnp.where(
        row_y == grid_side - 1, send_second(bottom_y, grid_side - 1), send_second(bottom_y, -1)
    )
    along_y = jnp.concatenate([low_y, field_now, high_y], axis=2)
    near_z = jnp.roll(field_now, 1, 3) + jnp.roll(field_now, -1, 3)
    far_z = jnp.roll(field_now, 2, 3) + jnp.roll(field_now, -2, 3)
    second = (
        3.0 * coef_zero * field_now
        + padded_second(along_x, cells_x, 1)
        + padded_second(along_y, cells_y, 2)
    )
    second = second + (coef_one * near_z + coef_two * far_z)
    return -0.5 * second + local_pot * field_now


def on_device(orbitals, potential, ritz):
    grid_side = math.isqrt(lax.axis_size("dom"))
    row_y = lax.axis_index("dom") % grid_side
    centre, first_scale, weights = filter_weights(DEG)
    local_pot = potential[0]
    previous = orbitals[:, 0].astype(jnp.float32)
    current = (apply_ham(previous, local_pot, grid_side, row_y) - centre * previous) * first_scale
    for scale_h, scale_x in weights:
        following = (
            apply_ham(current, local_pot, grid_side, row_y) - centre * current
        ) * scale_h - scale_x * previous
        previous, current = (current, following)
    band_rows = current.shape[0]
    flat_panel = current.astype(jnp.bfloat16).reshape(band_rows, -1)
    rotated = lax.dot_general(
        ritz,
        lax.all_gather(flat_panel, "band", axis=0, tiled=True),
        (((0,), (0,)), ((), ())),
        preferred_element_type=jnp.float32,
    )
    return rotated.reshape(orbitals.shape)


def solution(mesh):
    in_specs = (P("band", "dom", None, None, None), P("dom", None, None, None), P(None, "band"))
    out_specs = P("band", "dom", None, None, None)
    return jax.shard_map(
        on_device, mesh=mesh, in_specs=in_specs, out_specs=out_specs, check_vma=False
    )
```

profile of v0, /device:TPU:1, one launch (start us, length us, event | category | flops | bytes accessed | tf_op | source)
XLA Modules:
  0.0 319.9 jit_solution(1605391283668732699)
XLA Ops:
  6.5 1.1 bitcast_convert_fusion
  7.6 0.7 fusion.99
  8.3 4.5 %collective-permute-start.3 = (f32[32,2,2,128]{3,2,1,0:T(2,128)}, f32[32,2,2,128]{3,2,1,0:T(2,128)}, u32[]{:S(2)}, u32[]{:S(2)}) collective-permute-start(f32[32,2,2,128]{3,2,1,0:T(2,128)} %get-tuple-element.37), channel_id=1, source_target_pairs={{0,32},{32,64},{64,96},{96,128},{128,160},{160,192},{192,224},{224... | collective-permute-start | bytes 196616 | tf_op jit(solution)/shard_map/ppermute | solution.py:22
  12.8 5.0 %collective-permute-start.2 = (f32[32,2,2,128]{3,2,1,0:T(2,128)}, f32[32,2,2,128]{3,2,1,0:T(2,128)}, u32[]{:S(2)}, u32[]{:S(2)}) collective-permute-start(f32[32,2,2,128]{3,2,1,0:T(2,128)} %get-tuple-element.37), channel_id=1, source_target_pairs={{0,416},{32,448},{64,480},{96,0},{128,32},{160,64},{192,96},{224,1... | collective-permute-start | bytes 196616 | tf_op jit(solution)/shard_map/ppermute | solution.py:22
  17.8 3.1 collective-permute-start.1
  20.9 3.7 %collective-permute-start = (f32[32,2,16,128]{3,2,1,0:T(8,128)S(1)}, f32[32,2,16,128]{3,2,1,0:T(8,128)}, u32[]{:S(2)}, u32[]{:S(2)}) collective-permute-start(f32[32,2,16,128]{3,2,1,0:T(8,128)S(1)} %bitcast_convert_fusion), channel_id=1, source_target_pairs={{0,128},{32,160},{64,192},{96,224},{128,256},{160,288},{192,320},{... | collective-permute-start | bytes 1572872 | tf_op jit(solution)/shard_map/ppermute | solution.py:22
  24.6 4.0 %collective-permute-start.5 = (f32[32,2,2,128]{3,2,1,0:T(2,128)}, f32[32,2,2,128]{3,2,1,0:T(2,128)}, u32[]{:S(2)}, u32[]{:S(2)}) collective-permute-start(f32[32,2,2,128]{3,2,1,0:T(2,128)} %get-tuple-element.38), channel_id=1, source_target_pairs={{0,480},{32,0},{64,32},{96,64},{128,96},{160,128},{192,160},{224,1... | collective-permute-start | bytes 196616 | tf_op jit(solution)/shard_map/ppermute | solution.py:22
  28.7 0.2 fusion.101
  28.9 0.2 fusion.100
  29.1 1.0 fusion.103
  30.1 1.1 fusion.102
  31.3 0.0 collective-permute-done.3
  31.3 4.4 %collective-permute-start.4 = (f32[32,2,2,128]{3,2,1,0:T(2,128)}, f32[32,2,2,128]{3,2,1,0:T(2,128)S(1)}, u32[]{:S(2)}, u32[]{:S(2)}) collective-permute-start(f32[32,2,2,128]{3,2,1,0:T(2,128)} %get-tuple-element.38), channel_id=1, source_target_pairs={{0,96},{32,128},{64,160},{96,192},{128,224},{160,256},{192,288},{2... | collective-permute-start | bytes 196616 | tf_op jit(solution)/shard_map/ppermute | solution.py:22
  35.7 0.9 broadcast_select_fusion.7
  36.6 10.4 %collective-permute-done.5 = f32[32,2,2,128]{3,2,1,0:T(2,128)} collective-permute-done((f32[32,2,2,128]{3,2,1,0:T(2,128)}, f32[32,2,2,128]{3,2,1,0:T(2,128)}, u32[]{:S(2)}, u32[]{:S(2)}) %collective-permute-start.5) | collective-permute-done | bytes 65568 | tf_op jit(solution)/shard_map/ppermute | solution.py:22
  47.0 0.9 broadcast_select_fusion.3
  47.9 0.0 collective-permute-done
  47.9 2.9 broadcast_multiply_fusion
  50.8 4.1 %collective-permute-start.9 = (f32[32,2,2,128]{3,2,1,0:T(2,128)S(1)}, f32[32,2,2,128]{3,2,1,0:T(2,128)S(1)}, u32[]{:S(2)}, u32[]{:S(2)}) collective-permute-start(f32[32,2,2,128]{3,2,1,0:T(2,128)S(1)} %get-tuple-element.35), channel_id=1, source_target_pairs={{0,32},{32,64},{64,96},{96,128},{128,160},{160,192},{192,224},{224... | collective-permute-start | bytes 196616 | tf_op jit(solution)/shard_map/ppermute | solution.py:22
  54.9 6.9 %collective-permute-start.8 = (f32[32,2,2,128]{3,2,1,0:T(2,128)S(1)}, f32[32,2,2,128]{3,2,1,0:T(2,128)S(1)}, u32[]{:S(2)}, u32[]{:S(2)}) collective-permute-start(f32[32,2,2,128]{3,2,1,0:T(2,128)S(1)} %get-tuple-element.35), channel_id=1, source_target_pairs={{0,416},{32,448},{64,480},{96,0},{128,32},{160,64},{192,96},{224,1... | collective-permute-start | bytes 196616 | tf_op jit(solution)/shard_map/ppermute | solution.py:22
  61.9 3.1 collective-permute-start.7
  65.0 3.7 %collective-permute-start.6 = (f32[32,2,16,128]{3,2,1,0:T(8,128)S(1)}, f32[32,2,16,128]{3,2,1,0:T(8,128)S(1)}, u32[]{:S(2)}, u32[]{:S(2)}) collective-permute-start(f32[32,2,16,128]{3,2,1,0:T(8,128)S(1)} %get-tuple-element.5), channel_id=1, source_target_pairs={{0,128},{32,160},{64,192},{96,224},{128,256},{160,288},{192,320},{... | collective-permute-start | bytes 1572872 | tf_op jit(solution)/shard_map/ppermute | solution.py:22
  68.7 0.2 fusion.96
  68.9 0.2 fusion.94
  69.1 0.2 fusion.95
  69.3 0.2 fusion.97
  69.5 4.0 %collective-permute-start.11 = (f32[32,2,2,128]{3,2,1,0:T(2,128)S(1)}, f32[32,2,2,128]{3,2,1,0:T(2,128)S(1)}, u32[]{:S(2)}, u32[]{:S(2)}) collective-permute-start(f32[32,2,2,128]{3,2,1,0:T(2,128)S(1)} %get-tuple-element.36), channel_id=1, source_target_pairs={{0,480},{32,0},{64,32},{96,64},{128,96},{160,128},{192,160},{224,1... | collective-permute-start | bytes 196616 | tf_op jit(solution)/shard_map/ppermute | solution.py:22
  73.6 1.9 collective-permute-start.10
  75.5 0.0 collective-permute-done.8
  75.6 13.0 %collective-permute-done.11 = f32[32,2,2,128]{3,2,1,0:T(2,128)S(1)} collective-permute-done((f32[32,2,2,128]{3,2,1,0:T(2,128)S(1)}, f32[32,2,2,128]{3,2,1,0:T(2,128)S(1)}, u32[]{:S(2)}, u32[]{:S(2)}) %collective-permute-start.11) | collective-permute-done | bytes 65568 | tf_op jit(solution)/shard_map/ppermute | solution.py:22
  88.6 0.0 collective-permute-done.10
  88.6 1.1 collective-permute-done.7
  89.8 1.1 fusion.34
  90.9 1.9 collective-permute-start.15
  92.8 4.1 %collective-permute-start.14 = (f32[32,2,2,128]{3,2,1,0:T(2,128)S(1)}, f32[32,2,2,128]{3,2,1,0:T(2,128)S(1)}, u32[]{:S(2)}, u32[]{:S(2)}) collective-permute-start(f32[32,2,2,128]{3,2,1,0:T(2,128)S(1)} %get-tuple-element.25), channel_id=1, source_target_pairs={{0,416},{32,448},{64,480},{96,0},{128,32},{160,64},{192,96},{224,1... | collective-permute-start | bytes 196616 | tf_op jit(solution)/shard_map/ppermute | solution.py:22
  96.9 4.4 %collective-permute-start.13 = (f32[32,2,16,128]{3,2,1,0:T(8,128)S(1)}, f32[32,2,16,128]{3,2,1,0:T(8,128)S(1)}, u32[]{:S(2)}, u32[]{:S(2)}) collective-permute-start(f32[32,2,16,128]{3,2,1,0:T(8,128)S(1)} %fusion.34), channel_id=1, source_target_pairs={{0,384},{32,416},{64,448},{96,480},{128,0},{160,32},{192,64},{224,... | collective-permute-start | bytes 1572872 | tf_op jit(solution)/shard_map/ppermute | solution.py:22
  101.3 2.4 collective-permute-start.12
  103.8 0.2 fusion.91
  104.0 0.2 fusion.90
  104.2 0.2 fusion.89
  104.4 0.2 fusion.92
  104.6 4.9 %collective-permute-start.17 = (f32[32,2,2,128]{3,2,1,0:T(2,128)S(1)}, f32[32,2,2,128]{3,2,1,0:T(2,128)S(1)}, u32[]{:S(2)}, u32[]{:S(2)}) collective-permute-start(f32[32,2,2,128]{3,2,1,0:T(2,128)S(1)} %get-tuple-element.26), channel_id=1, source_target_pairs={{0,480},{32,0},{64,32},{96,64},{128,96},{160,128},{192,160},{224,1... | collective-permute-start | bytes 196616 | tf_op jit(solution)/shard_map/ppermute | solution.py:22
  109.5 0.0 collective-permute-done.15
  109.5 2.6 collective-permute-start.16
  112.2 0.0 collective-permute-done.14
  112.2 14.9 %collective-permute-done.17 = f32[32,2,2,128]{3,2,1,0:T(2,128)S(1)} collective-permute-done((f32[32,2,2,128]{3,2,1,0:T(2,128)S(1)}, f32[32,2,2,128]{3,2,1,0:T(2,128)S(1)}, u32[]{:S(2)}, u32[]{:S(2)}) %collective-permute-start.17) | collective-permute-done | bytes 65568 | tf_op jit(solution)/shard_map/ppermute | solution.py:22
  127.2 1.0 fusion.22
  128.3 2.9 collective-permute-start.21
  131.2 6.1 %collective-permute-start.20 = (f32[32,2,2,128]{3,2,1,0:T(2,128)S(1)}, f32[32,2,2,128]{3,2,1,0:T(2,128)S(1)}, u32[]{:S(2)}, u32[]{:S(2)}) collective-permute-start(f32[32,2,2,128]{3,2,1,0:T(2,128)S(1)} %get-tuple-element.7), channel_id=1, source_target_pairs={{0,416},{32,448},{64,480},{96,0},{128,32},{160,64},{192,96},{224,1... | collective-permute-start | bytes 196616 | tf_op jit(solution)/shard_map/ppermute | solution.py:22
  137.4 3.1 collective-permute-start.19
  140.5 3.7 %collective-permute-start.18 = (f32[32,2,16,128]{3,2,1,0:T(8,128)S(1)}, f32[32,2,16,128]{3,2,1,0:T(8,128)S(1)}, u32[]{:S(2)}, u32[]{:S(2)}) collective-permute-start(f32[32,2,16,128]{3,2,1,0:T(8,128)S(1)} %fusion.22), channel_id=1, source_target_pairs={{0,128},{32,160},{64,192},{96,224},{128,256},{160,288},{192,320},{... | collective-permute-start | bytes 1572872 | tf_op jit(solution)/shard_map/ppermute | solution.py:22
  144.2 0.2 fusion.88
  144.4 0.2 fusion.85
  144.6 0.2 fusion.86
  144.8 0.2 fusion.87
  145.0 4.0 %collective-permute-start.23 = (f32[32,2,2,128]{3,2,1,0:T(2,128)S(1)}, f32[32,2,2,128]{3,2,1,0:T(2,128)S(1)}, u32[]{:S(2)}, u32[]{:S(2)}) collective-permute-start(f32[32,2,2,128]{3,2,1,0:T(2,128)S(1)} %get-tuple-element.8), channel_id=1, source_target_pairs={{0,480},{32,0},{64,32},{96,64},{128,96},{160,128},{192,160},{224,1... | collective-permute-start | bytes 196616 | tf_op jit(solution)/shard_map/ppermute | solution.py:22
  149.1 1.9 collective-permute-start.22
  151.1 14.7 %collective-permute-done.23 = f32[32,2,2,128]{3,2,1,0:T(2,128)S(1)} collective-permute-done((f32[32,2,2,128]{3,2,1,0:T(2,128)S(1)}, f32[32,2,2,128]{3,2,1,0:T(2,128)S(1)}, u32[]{:S(2)}, u32[]{:S(2)}) %collective-permute-start.23) | collective-permute-done | bytes 65568 | tf_op jit(solution)/shard_map/ppermute | solution.py:22
  165.9 1.0 fusion.82
  166.9 0.8 copy.8
  167.7 0.0 all-gather.2.cloned.1.call-update
  167.8 139.5 %all-gather.2.cloned.1.call-done = bf16[1024,4096]{1,0:T(8,128)(2,1)} async-done(((bf16[32,4096]{1,0:T(8,128)(2,1)}), bf16[1024,4096]{1,0:T(8,128)(2,1)}) %all-gather.2.cloned.1.call-update) | async-done | bytes 8388624 | tf_op jit(solution)/shard_map/all_gather | solution.py:95
  307.2 4.9 %convolution_bitcast_fusion = f32[4,8,32,128]{3,1,2,0:T(8,128)S(1)} fusion(bf16[1024,32]{0,1:T(8,128)(2,1)S(1)} %copy-done, bf16[1024,4096]{1,0:T(8,128)(2,1)} %all-gather.2.cloned.1.call-done), kind=kOutput, calls=%fused_computation | convolution fusion | flops 268435456 | bytes 8978432 | tf_op jit(solution)/shard_map/dot_general | solution.py:93
  312.2 0.9 copy.6
  (30 shorter events, 0.4 us)
Async XLA Ops:
  6.5 300.7 %copy-start = (bf16[1024,32]{0,1:T(8,128)(2,1)S(1)}, bf16[1024,32]{0,1:T(8,128)(2,1)}, u32[]{:S(2)}) copy-start(bf16[1024,32]{0,1:T(8,128)(2,1)} %param.5) | copy-start | bytes 196612
  6.5 41.4 %copy-start.1 = (bf16[32,1,2,16,128]{4,3,2,1,0:T(8,128)(2,1)S(1)}, bf16[32,1,2,16,128]{4,3,2,1,0:T(8,128)(2,1)}, u32[]{:S(2)}) copy-start(bf16[32,1,2,16,128]{4,3,2,1,0:T(8,128)(2,1)} %param.3) | copy-start | bytes 786436
  6.5 24.7 %copy-start.2 = (f32[1,2,16,128]{3,2,1,0:T(8,128)S(1)}, f32[1,2,16,128]{3,2,1,0:T(8,128)}, u32[]{:S(2)}) copy-start(f32[1,2,16,128]{3,2,1,0:T(8,128)} %param.4) | copy-start | bytes 49156
  6.5 300.7 %all-gather.2.cloned.1.call-start = ((), (), s32[]{:S(2)}) async-start(), calls=%async_computation | async-start | bytes 8650752 | tf_op jit(solution)/shard_map/all_gather | solution.py:95
  8.3 22.9 %collective-permute-start.3 = (f32[32,2,2,128]{3,2,1,0:T(2,128)}, f32[32,2,2,128]{3,2,1,0:T(2,128)}, u32[]{:S(2)}, u32[]{:S(2)}) collective-permute-start(f32[32,2,2,128]{3,2,1,0:T(2,128)} %get-tuple-element.37), channel_id=1, source_target_pairs={{0,32},{32,64},{64,96},{96,128},{128,160},{160,192},{192,224},{224... | collective-permute-start | bytes 196616 | tf_op jit(solution)/shard_map/ppermute | solution.py:22
  12.8 22.8 %collective-permute-start.2 = (f32[32,2,2,128]{3,2,1,0:T(2,128)}, f32[32,2,2,128]{3,2,1,0:T(2,128)}, u32[]{:S(2)}, u32[]{:S(2)}) collective-permute-start(f32[32,2,2,128]{3,2,1,0:T(2,128)} %get-tuple-element.37), channel_id=1, source_target_pairs={{0,416},{32,448},{64,480},{96,0},{128,32},{160,64},{192,96},{224,1... | collective-permute-start | bytes 196616 | tf_op jit(solution)/shard_map/ppermute | solution.py:22
  17.8 30.1 %collective-permute-start.1 = (f32[32,2,16,128]{3,2,1,0:T(8,128)S(1)}, f32[32,2,16,128]{3,2,1,0:T(8,128)}, u32[]{:S(2)}, u32[]{:S(2)}) collective-permute-start(f32[32,2,16,128]{3,2,1,0:T(8,128)S(1)} %bitcast_convert_fusion), channel_id=1, source_target_pairs={{0,384},{32,416},{64,448},{96,480},{128,0},{160,32},{192,64},{224,... | collective-permute-start | bytes 1572872 | tf_op jit(solution)/shard_map/ppermute | solution.py:22
  20.9 27.0 %collective-permute-start = (f32[32,2,16,128]{3,2,1,0:T(8,128)S(1)}, f32[32,2,16,128]{3,2,1,0:T(8,128)}, u32[]{:S(2)}, u32[]{:S(2)}) collective-permute-start(f32[32,2,16,128]{3,2,1,0:T(8,128)S(1)} %bitcast_convert_fusion), channel_id=1, source_target_pairs={{0,128},{32,160},{64,192},{96,224},{128,256},{160,288},{192,320},{... | collective-permute-start | bytes 1572872 | tf_op jit(solution)/shard_map/ppermute | solution.py:22
  24.6 22.4 %collective-permute-start.5 = (f32[32,2,2,128]{3,2,1,0:T(2,128)}, f32[32,2,2,128]{3,2,1,0:T(2,128)}, u32[]{:S(2)}, u32[]{:S(2)}) collective-permute-start(f32[32,2,2,128]{3,2,1,0:T(2,128)} %get-tuple-element.38), channel_id=1, source_target_pairs={{0,480},{32,0},{64,32},{96,64},{128,96},{160,128},{192,160},{224,1... | collective-permute-start | bytes 196616 | tf_op jit(solution)/shard_map/ppermute | solution.py:22
  31.3 15.7 %collective-permute-start.4 = (f32[32,2,2,128]{3,2,1,0:T(2,128)}, f32[32,2,2,128]{3,2,1,0:T(2,128)S(1)}, u32[]{:S(2)}, u32[]{:S(2)}) collective-permute-start(f32[32,2,2,128]{3,2,1,0:T(2,128)} %get-tuple-element.38), channel_id=1, source_target_pairs={{0,96},{32,128},{64,160},{96,192},{128,224},{160,256},{192,288},{2... | collective-permute-start | bytes 196616 | tf_op jit(solution)/shard_map/ppermute | solution.py:22
  50.8 22.7 %collective-permute-start.9 = (f32[32,2,2,128]{3,2,1,0:T(2,128)S(1)}, f32[32,2,2,128]{3,2,1,0:T(2,128)S(1)}, u32[]{:S(2)}, u32[]{:S(2)}) collective-permute-start(f32[32,2,2,128]{3,2,1,0:T(2,128)S(1)} %get-tuple-element.35), channel_id=1, source_target_pairs={{0,32},{32,64},{64,96},{96,128},{128,160},{160,192},{192,224},{224... | collective-permute-start | bytes 196616 | tf_op jit(solution)/shard_map/ppermute | solution.py:22
  54.9 20.6 %collective-permute-start.8 = (f32[32,2,2,128]{3,2,1,0:T(2,128)S(1)}, f32[32,2,2,128]{3,2,1,0:T(2,128)S(1)}, u32[]{:S(2)}, u32[]{:S(2)}) collective-permute-start(f32[32,2,2,128]{3,2,1,0:T(2,128)S(1)} %get-tuple-element.35), channel_id=1, source_target_pairs={{0,416},{32,448},{64,480},{96,0},{128,32},{160,64},{192,96},{224,1... | collective-permute-start | bytes 196616 | tf_op jit(solution)/shard_map/ppermute | solution.py:22
  61.9 27.9 %collective-permute-start.7 = (f32[32,2,16,128]{3,2,1,0:T(8,128)S(1)}, f32[32,2,16,128]{3,2,1,0:T(8,128)S(1)}, u32[]{:S(2)}, u32[]{:S(2)}) collective-permute-start(f32[32,2,16,128]{3,2,1,0:T(8,128)S(1)} %get-tuple-element.5), channel_id=1, source_target_pairs={{0,384},{32,416},{64,448},{96,480},{128,0},{160,32},{192,64},{224,... | collective-permute-start | bytes 1572872 | tf_op jit(solution)/shard_map/ppermute | solution.py:22
  65.0 24.8 %collective-permute-start.6 = (f32[32,2,16,128]{3,2,1,0:T(8,128)S(1)}, f32[32,2,16,128]{3,2,1,0:T(8,128)S(1)}, u32[]{:S(2)}, u32[]{:S(2)}) collective-permute-start(f32[32,2,16,128]{3,2,1,0:T(8,128)S(1)} %get-tuple-element.5), channel_id=1, source_target_pairs={{0,128},{32,160},{64,192},{96,224},{128,256},{160,288},{192,320},{... | collective-permute-start | bytes 1572872 | tf_op jit(solution)/shard_map/ppermute | solution.py:22
  69.5 19.1 %collective-permute-start.11 = (f32[32,2,2,128]{3,2,1,0:T(2,128)S(1)}, f32[32,2,2,128]{3,2,1,0:T(2,128)S(1)}, u32[]{:S(2)}, u32[]{:S(2)}) collective-permute-start(f32[32,2,2,128]{3,2,1,0:T(2,128)S(1)} %get-tuple-element.36), channel_id=1, source_target_pairs={{0,480},{32,0},{64,32},{96,64},{128,96},{160,128},{192,160},{224,1... | collective-permute-start | bytes 196616 | tf_op jit(solution)/shard_map/ppermute | solution.py:22
  73.6 15.0 %collective-permute-start.10 = (f32[32,2,2,128]{3,2,1,0:T(2,128)S(1)}, f32[32,2,2,128]{3,2,1,0:T(2,128)S(1)}, u32[]{:S(2)}, u32[]{:S(2)}) collective-permute-start(f32[32,2,2,128]{3,2,1,0:T(2,128)S(1)} %get-tuple-element.36), channel_id=1, source_target_pairs={{0,96},{32,128},{64,160},{96,192},{128,224},{160,256},{192,288},{2... | collective-permute-start | bytes 196616 | tf_op jit(solution)/shard_map/ppermute | solution.py:22
  90.9 18.6 %collective-permute-start.15 = (f32[32,2,2,128]{3,2,1,0:T(2,128)S(1)}, f32[32,2,2,128]{3,2,1,0:T(2,128)S(1)}, u32[]{:S(2)}, u32[]{:S(2)}) collective-permute-start(f32[32,2,2,128]{3,2,1,0:T(2,128)S(1)} %get-tuple-element.25), channel_id=1, source_target_pairs={{0,32},{32,64},{64,96},{96,128},{128,160},{160,192},{192,224},{224... | collective-permute-start | bytes 196616 | tf_op jit(solution)/shard_map/ppermute | solution.py:22
  92.8 19.3 %collective-permute-start.14 = (f32[32,2,2,128]{3,2,1,0:T(2,128)S(1)}, f32[32,2,2,128]{3,2,1,0:T(2,128)S(1)}, u32[]{:S(2)}, u32[]{:S(2)}) collective-permute-start(f32[32,2,2,128]{3,2,1,0:T(2,128)S(1)} %get-tuple-element.25), channel_id=1, source_target_pairs={{0,416},{32,448},{64,480},{96,0},{128,32},{160,64},{192,96},{224,1... | collective-permute-start | bytes 196616 | tf_op jit(solution)/shard_map/ppermute | solution.py:22
  96.9 30.2 %collective-permute-start.13 = (f32[32,2,16,128]{3,2,1,0:T(8,128)S(1)}, f32[32,2,16,128]{3,2,1,0:T(8,128)S(1)}, u32[]{:S(2)}, u32[]{:S(2)}) collective-permute-start(f32[32,2,16,128]{3,2,1,0:T(8,128)S(1)} %fusion.34), channel_id=1, source_target_pairs={{0,384},{32,416},{64,448},{96,480},{128,0},{160,32},{192,64},{224,... | collective-permute-start | bytes 1572872 | tf_op jit(solution)/shard_map/ppermute | solution.py:22
  101.3 25.9 %collective-permute-start.12 = (f32[32,2,16,128]{3,2,1,0:T(8,128)S(1)}, f32[32,2,16,128]{3,2,1,0:T(8,128)S(1)}, u32[]{:S(2)}, u32[]{:S(2)}) collective-permute-start(f32[32,2,16,128]{3,2,1,0:T(8,128)S(1)} %fusion.34), channel_id=1, source_target_pairs={{0,128},{32,160},{64,192},{96,224},{128,256},{160,288},{192,320},{... | collective-permute-start | bytes 1572872 | tf_op jit(solution)/shard_map/ppermute | solution.py:22
  104.6 22.6 %collective-permute-start.17 = (f32[32,2,2,128]{3,2,1,0:T(2,128)S(1)}, f32[32,2,2,128]{3,2,1,0:T(2,128)S(1)}, u32[]{:S(2)}, u32[]{:S(2)}) collective-permute-start(f32[32,2,2,128]{3,2,1,0:T(2,128)S(1)} %get-tuple-element.26), channel_id=1, source_target_pairs={{0,480},{32,0},{64,32},{96,64},{128,96},{160,128},{192,160},{224,1... | collective-permute-start | bytes 196616 | tf_op jit(solution)/shard_map/ppermute | solution.py:22
  109.5 17.6 %collective-permute-start.16 = (f32[32,2,2,128]{3,2,1,0:T(2,128)S(1)}, f32[32,2,2,128]{3,2,1,0:T(2,128)S(1)}, u32[]{:S(2)}, u32[]{:S(2)}) collective-permute-start(f32[32,2,2,128]{3,2,1,0:T(2,128)S(1)} %get-tuple-element.26), channel_id=1, source_target_pairs={{0,96},{32,128},{64,160},{96,192},{128,224},{160,256},{192,288},{2... | collective-permute-start | bytes 196616 | tf_op jit(solution)/shard_map/ppermute | solution.py:22
  128.3 20.8 %collective-permute-start.21 = (f32[32,2,2,128]{3,2,1,0:T(2,128)S(1)}, f32[32,2,2,128]{3,2,1,0:T(2,128)S(1)}, u32[]{:S(2)}, u32[]{:S(2)}) collective-permute-start(f32[32,2,2,128]{3,2,1,0:T(2,128)S(1)} %get-tuple-element.7), channel_id=1, source_target_pairs={{0,32},{32,64},{64,96},{96,128},{128,160},{160,192},{192,224},{224... | collective-permute-start | bytes 196616 | tf_op jit(solution)/shard_map/ppermute | solution.py:22
  131.2 19.8 %collective-permute-start.20 = (f32[32,2,2,128]{3,2,1,0:T(2,128)S(1)}, f32[32,2,2,128]{3,2,1,0:T(2,128)S(1)}, u32[]{:S(2)}, u32[]{:S(2)}) collective-permute-start(f32[32,2,2,128]{3,2,1,0:T(2,128)S(1)} %get-tuple-element.7), channel_id=1, source_target_pairs={{0,416},{32,448},{64,480},{96,0},{128,32},{160,64},{192,96},{224,1... | collective-permute-start | bytes 196616 | tf_op jit(solution)/shard_map/ppermute | solution.py:22
  137.4 28.5 %collective-permute-start.19 = (f32[32,2,16,128]{3,2,1,0:T(8,128)S(1)}, f32[32,2,16,128]{3,2,1,0:T(8,128)S(1)}, u32[]{:S(2)}, u32[]{:S(2)}) collective-permute-start(f32[32,2,16,128]{3,2,1,0:T(8,128)S(1)} %fusion.22), channel_id=1, source_target_pairs={{0,384},{32,416},{64,448},{96,480},{128,0},{160,32},{192,64},{224,... | collective-permute-start | bytes 1572872 | tf_op jit(solution)/shard_map/ppermute | solution.py:22
  140.5 25.4 %collective-permute-start.18 = (f32[32,2,16,128]{3,2,1,0:T(8,128)S(1)}, f32[32,2,16,128]{3,2,1,0:T(8,128)S(1)}, u32[]{:S(2)}, u32[]{:S(2)}) collective-permute-start(f32[32,2,16,128]{3,2,1,0:T(8,128)S(1)} %fusion.22), channel_id=1, source_target_pairs={{0,128},{32,160},{64,192},{96,224},{128,256},{160,288},{192,320},{... | collective-permute-start | bytes 1572872 | tf_op jit(solution)/shard_map/ppermute | solution.py:22
  145.0 20.8 %collective-permute-start.23 = (f32[32,2,2,128]{3,2,1,0:T(2,128)S(1)}, f32[32,2,2,128]{3,2,1,0:T(2,128)S(1)}, u32[]{:S(2)}, u32[]{:S(2)}) collective-permute-start(f32[32,2,2,128]{3,2,1,0:T(2,128)S(1)} %get-tuple-element.8), channel_id=1, source_target_pairs={{0,480},{32,0},{64,32},{96,64},{128,96},{160,128},{192,160},{224,1... | collective-permute-start | bytes 196616 | tf_op jit(solution)/shard_map/ppermute | solution.py:22
  149.1 16.7 %collective-permute-start.22 = (f32[32,2,2,128]{3,2,1,0:T(2,128)S(1)}, f32[32,2,2,128]{3,2,1,0:T(2,128)S(1)}, u32[]{:S(2)}, u32[]{:S(2)}) collective-permute-start(f32[32,2,2,128]{3,2,1,0:T(2,128)S(1)} %get-tuple-element.8), channel_id=1, source_target_pairs={{0,96},{32,128},{64,160},{96,192},{128,224},{160,256},{192,288},{2... | collective-permute-start | bytes 196616 | tf_op jit(solution)/shard_map/ppermute | solution.py:22
Sparse Core Ops, SparseCore 0:
  167.9 139.3 all-gather.1
where the time goes:
time: 321 us; the launch traced here: 320 us
  waiting for transfers between devices  194 us (60%)
  starting transfers between devices  90.6 us (28%)
  between operations  13.8 us (4%)
  other arithmetic  9.05 us (3%)
  local copies, waits for them, and re-layouts  7.66 us (2%)
  matrix products  4.92 us (2%)
    all_gather x1, waiting for transfers between devices, on_device(): lax.all_gather(flat_panel, 'band', axis=0, tiled=True)  139 us
    ppermute x24, starting transfers between devices, shifted(): return lax.ppermute(value, axis, pairs)  90.6 us
    ppermute x24, waiting for transfers between devices, shifted(): return lax.ppermute(value, axis, pairs)  54.3 us
  transfers between devices with their start and end apart: 25, of which 6 were waited for; matrix products, arithmetic and copies ran while one was open for 2% of the time, Pallas kernels for 0%

commit v1 on v0

v1 whole, which is shorter than its diff:
```python
import math

import jax
import jax.numpy as jnp
from jax import lax
from jax.experimental import pallas as pl
from jax.experimental.pallas import tpu as pltpu
from jax.sharding import PartitionSpec as P

DEG = 4

lower_bound = -1.5
cut_off = 1.0
upper_bound = 9.5
coef_zero = -2.5
coef_one = 4.0 / 3.0
coef_two = -1.0 / 12.0

PAD = 8


def filter_weights(degree):
    half_width = (upper_bound - cut_off) / 2.0
    centre = (upper_bound + cut_off) / 2.0
    sigma_now = half_width / (lower_bound - centre)
    first_scale = sigma_now / half_width
    inverse_gain = 2.0 / sigma_now
    weights = []
    for degree_step in range(1, degree):
        sigma_next = 1.0 / (inverse_gain - sigma_now)
        weights.append((2.0 * sigma_next / half_width, sigma_now * sigma_next))
        sigma_now = sigma_next
    return (centre, first_scale, weights)


def filter_kernel(n_dom, n_own, cx, cy, nz):
    side = math.isqrt(n_dom)
    gx, gy = side * cx, side * cy
    centre, first_scale, weights = filter_weights(DEG)
    row_stride = n_dom * n_own
    far_near = coef_two / coef_one

    def wrap(ref, band, x):
        ref[band, x, 0:PAD, :] = ref[band, x, gy : gy + PAD, :]
        ref[band, x, PAD + gy : PAD + gy + PAD, :] = ref[band, x, PAD : 2 * PAD, :]

    def shifted_ham(cur, diag, band, x):
        mid = cur[band, x, PAD : PAD + gy, :]

        def plane(step):
            return cur[band, lax.rem(x + (gx + step), gx), PAD : PAD + gy, :]

        def rows(step):
            return cur[band, x, PAD + step : PAD + step + gy, :]

        def lanes(step):
            return pltpu.roll(mid, step % nz, 1)

        near = (plane(-1) + plane(1)) + (rows(-1) + rows(1)) + (lanes(-1) + lanes(1))
        far = (plane(-2) + plane(2)) + (rows(-2) + rows(2)) + (lanes(-2) + lanes(2))
        return diag[x] * mid + (-0.5 * coef_one) * (near + far_near * far)

    def body(blocks, out, first, second, diag, ordered):
        def load(x, carry):
            for j in range(side):
                dom = lax.div(x, cx) * side + j
                inner = lax.rem(x, cx)
                for band in range(n_own):
                    first[band, x, PAD + j * cy : PAD + (j + 1) * cy, :] = blocks[
                        dom, band, inner
                    ].astype(jnp.float32)
                pot = blocks[dom, n_own, inner].astype(jnp.float32) + blocks[
                    dom, n_own + 1, inner
                ].astype(jnp.float32)
                diag[x, j * cy : (j + 1) * cy, :] = pot + (-1.5 * coef_zero - centre)
            for band in range(n_own):
                wrap(first, band, x)
            return carry

        lax.fori_loop(0, gx, load, 0)

        def run(step):
            def one(n, carry):
                step(lax.div(n, gx), lax.rem(n, gx))
                return carry

            lax.fori_loop(0, n_own * gx, one, 0)

        def start(band, x):
            second[band, x, PAD : PAD + gy, :] = shifted_ham(first, diag, band, x) * first_scale
            wrap(second, band, x)

        run(start)
        previous, current = first, second
        for scale_h, scale_x in weights[:-1]:

            def middle(band, x, previous=previous, current=current, scale_h=scale_h, scale_x=scale_x):
                following = shifted_ham(current, diag, band, x) * scale_h
                following = following - scale_x * previous[band, x, PAD : PAD + gy, :]
                previous[band, x, PAD : PAD + gy, :] = following
                wrap(previous, band, x)

            run(middle)
            previous, current = current, previous
        scale_h, scale_x = weights[-1]

        def last(band, x):
            following = shifted_ham(current, diag, band, x) * scale_h
            following = following - scale_x * previous[band, x, PAD : PAD + gy, :]
            for j in range(side):
                for part in range(cy // 8):
                    dom = lax.div(x, cx) * side + j
                    cell = lax.rem(x, cx) * cy + part * 8
                    base = cell * row_stride + dom * n_own + band
                    at = j * cy + part * 8
                    ordered[pl.ds(base, 8, stride=row_stride), :] = following[at : at + 8]

        run(last)
        block = 64

        def store(n, carry):
            at = pl.multiple_of(n * block, block)
            out[pl.ds(at, block), :] = ordered[pl.ds(at, block), :].astype(jnp.bfloat16)
            return carry

        lax.fori_loop(0, out.shape[0] // block, store, 0)

    padded = pltpu.VMEM((n_own, gx, gy + 2 * PAD, nz), jnp.float32)
    rows_out = cx * cy * n_dom * n_own
    return pl.pallas_call(
        body,
        out_shape=jax.ShapeDtypeStruct((rows_out, nz), jnp.bfloat16),
        in_specs=[pl.BlockSpec(memory_space=pltpu.VMEM)],
        out_specs=pl.BlockSpec(memory_space=pltpu.VMEM),
        scratch_shapes=[
            padded,
            padded,
            pltpu.VMEM((gx, gy, nz), jnp.float32),
            pltpu.VMEM((rows_out, nz), jnp.float32),
        ],
        name="chebyshev",
    )


def on_device(orbitals, potential, ritz):
    n_dom = lax.axis_size("dom")
    n_band = lax.axis_size("band")
    n_mine, _, cx, cy, nz = orbitals.shape
    n_all = ritz.shape[0]
    n_own = n_mine // n_dom
    half = n_all // 2
    core = lax.rem(lax.axis_index("dom"), 2)

    columns = ritz.T
    piece = lax.dynamic_slice_in_dim(columns, core * half, half, 1)
    many = jnp.broadcast_to(piece[None], (n_band,) + piece.shape)
    with jax.named_scope("ritz"):
        mine = lax.all_to_all(many, "band", 0, 0, tiled=True).reshape(n_all, half)
        other = lax.ppermute(mine, "dom", [(d, d ^ 1) for d in range(n_dom)])

    pot = potential[0]
    high = lax.reduce_precision(pot, 8, 7)
    parts = jnp.stack([high, pot - high]).astype(jnp.bfloat16)
    parts = jnp.broadcast_to(parts[None], (n_dom, 2, cx, cy, nz))
    blocks = orbitals.reshape(n_dom, n_own, cx, cy, nz)
    blocks = jnp.concatenate([blocks, parts], axis=1)
    with jax.named_scope("spread"):
        blocks = lax.all_to_all(blocks, "dom", 0, 0, tiled=True)
    filtered = filter_kernel(n_dom, n_own, cx, cy, nz)(blocks)

    with jax.named_scope("turn"):
        rows = lax.all_to_all(
            filtered.reshape(n_band * n_dom, n_own, nz), ("band", "dom"), 0, 0, tiled=True
        ).reshape(n_all, nz)

    def product(left, which):
        right = lax.dynamic_slice_in_dim(rows, which * half, half, 0)
        return jnp.dot(left, right, preferred_element_type=jnp.float32)

    rotated = product(mine, core) + product(other, 1 - core)
    rotated = rotated.astype(jnp.bfloat16).reshape(n_band, n_mine, nz)
    with jax.named_scope("back"):
        rotated = lax.all_to_all(rotated, "band", 0, 0, tiled=True)
    rotated = rotated.transpose(1, 0, 2).astype(jnp.float32)
    return rotated.reshape(orbitals.shape)


def solution(mesh):
    in_specs = (P("band", "dom", None, None, None), P("dom", None, None, None), P(None, "band"))
    out_specs = P("band", "dom", None, None, None)
    return jax.shard_map(
        on_device, mesh=mesh, in_specs=in_specs, out_specs=out_specs, check_vma=False
    )
```

time: 321 us -> 124 us (0.39)
  the two profiles are of different devices: /device:TPU:1 before, /device:TPU:8 now
where the time goes in v1:
time: 124 us; the launch traced here: 123 us
  waiting for transfers between devices  54.2 us (44%)
  starting transfers between devices  33 us (27%)
  blocking collectives  19.9 us (16%)
  Pallas kernels  9.32 us (8%)
  local copies, waits for them, and re-layouts  4.74 us (4%)
    all_to_all x1, waiting for transfers between devices, on_device(): mine = lax.all_to_all(many, 'band', 0, 0, tiled=True).reshape(n_all, half)  29.3 us
    all_to_all x1, blocking collectives, on_device(): rotated = lax.all_to_all(rotated, 'band', 0, 0, tiled=True)  19.9 us
    all_to_all x1, waiting for transfers between devices, on_device(): lax.all_to_all(filtered.reshape(n_band * n_dom, n_own, nz), ('band', 'dom...  16.4 us
    all_to_all x1, starting transfers between devices, on_device(): mine = lax.all_to_all(many, 'band', 0, 0, tiled=True).reshape(n_all, half)  16.3 us
    pallas_call x1, Pallas kernels, on_device(): filtered = filter_kernel(n_dom, n_own, cx, cy, nz)(blocks)  9.32 us
    all_to_all x1, starting transfers between devices, on_device(): lax.all_to_all(filtered.reshape(n_band * n_dom, n_own, nz), ('band', 'dom...  9.16 us
    all_to_all x1, waiting for transfers between devices, on_device(): blocks = lax.all_to_all(blocks, 'dom', 0, 0, tiled=True)  8.51 us
    all_to_all x1, starting transfers between devices, on_device(): blocks = lax.all_to_all(blocks, 'dom', 0, 0, tiled=True)  5.26 us
  transfers between devices with their start and end apart: 4, of which 3 were waited for; matrix products, arithmetic and copies ran while one was open for 1% of the time, Pallas kernels for 8%

profile of v1, /device:TPU:8, one launch (start us, length us, event | category | flops | bytes accessed | tf_op | source)
XLA Modules:
  0.0 123.1 jit_solution(12414326853565951282)
XLA Ops:
  0.0 0.0 copy-start
  0.0 0.8 copy-done
  0.8 1.1 broadcast_in_dim.4
  1.9 0.0 copy-start.3
  1.9 16.3 %all-to-all-start = ((bf16[32,32,512]{2,1,0:T(8,128)(2,1)}), bf16[32,32,512]{2,1,0:T(8,128)(2,1)S(1)}, u32[]{:S(2)}, u32[]{:S(2)}) async-start(bf16[32,32,512]{2,1,0:T(8,128)(2,1)} %broadcast_in_dim.4), calls=%async_computation | async-start | bytes 2097152 | tf_op jit(solution)/shard_map/ritz/all_to_all | solution.py:158
  18.2 0.0 copy-done.3
  18.3 0.0 copy-start.2
  18.3 0.9 copy-done.2
  19.2 0.8 pad_maximum_fusion
  20.0 29.3 %all-to-all-done = bf16[32,32,512]{2,1,0:T(8,128)(2,1)S(1)} async-done(((bf16[32,32,512]{2,1,0:T(8,128)(2,1)}), bf16[32,32,512]{2,1,0:T(8,128)(2,1)S(1)}, u32[]{:S(2)}, u32[]{:S(2)}) %all-to-all-start) | async-done | bytes 1048608 | tf_op jit(solution)/shard_map/ritz/all_to_all | solution.py:158
  49.4 5.3 %all-to-all-start.1 = ((bf16[16,4,2,16,128]{4,3,2,1,0:T(8,128)(2,1)}), bf16[16,4,2,16,128]{4,3,2,1,0:T(8,128)(2,1)S(1)}, u32[]{:S(2)}, u32[]{:S(2)}) async-start(bf16[16,4,2,16,128]{4,3,2,1,0:T(8,128)(2,1)} %pad_maximum_fusion), calls=%async_computation.1 | async-start | bytes 1048576 | tf_op jit(solution)/shard_map/spread/all_to_all | solution.py:168
  54.6 2.3 %collective-permute-start = (bf16[1024,512]{1,0:T(8,128)(2,1)S(1)}, bf16[1024,512]{1,0:T(8,128)(2,1)S(1)}, u32[]{:S(2)}, u32[]{:S(2)}) collective-permute-start(bf16[1024,512]{1,0:T(8,128)(2,1)S(1)} %bitcast.12), channel_id=1, source_target_pairs={{0,32},{32,0},{64,96},{96,64},{128,160},{160,128},{192,224},{224,1... | collective-permute-start | bytes 3145736 | tf_op jit(solution)/shard_map/ritz/ppermute | solution.py:159
  57.0 8.5 %all-to-all-done.1.blocks = bf16[16,4,2,16,128]{4,3,2,1,0:T(8,128)(2,1)S(1)} async-done(((bf16[16,4,2,16,128]{4,3,2,1,0:T(8,128)(2,1)}), bf16[16,4,2,16,128]{4,3,2,1,0:T(8,128)(2,1)S(1)}, u32[]{:S(2)}, u32[]{:S(2)}) %all-to-all-start.1) | async-done | bytes 524320 | tf_op jit(solution)/shard_map/spread/all_to_all | solution.py:168
  65.5 0.0 copy-start.1
  65.5 0.8 copy-done.1
  66.3 9.3 %chebyshev.1 = bf16[1024,128]{1,0:T(8,128)(2,1)} custom-call(bf16[16,4,2,16,128]{4,3,2,1,0:T(8,128)(2,1)} %copy-done.1), custom_call_target="tpu_custom_call" | custom-call | tf_op jit(solution)/shard_map/chebyshev/pallas_call | solution.py:169
  75.6 9.2 %all-to-all-start.2 = ((bf16[512,2,128]{2,1,0:T(2,128)(2,1)}), bf16[512,2,128]{2,1,0:T(2,128)(2,1)S(1)}, u32[]{:S(2)}, u32[]{:S(2)}) async-start(bf16[512,2,128]{2,1,0:T(2,128)(2,1)} %bitcast.16), calls=%async_computation.2 | async-start | bytes 524288 | tf_op jit(solution)/shard_map/turn/all_to_all | solution.py:172
  84.8 16.4 %all-to-all-done.2 = bf16[512,2,128]{2,1,0:T(2,128)(2,1)S(1)} async-done(((bf16[512,2,128]{2,1,0:T(2,128)(2,1)}), bf16[512,2,128]{2,1,0:T(2,128)(2,1)S(1)}, u32[]{:S(2)}, u32[]{:S(2)}) %all-to-all-start.2) | async-done | bytes 262176 | tf_op jit(solution)/shard_map/turn/all_to_all | solution.py:172
  101.1 0.4 fusion.2
  101.6 0.0 collective-permute-done
  101.6 0.5 fusion
  102.0 19.9 %all_to_all.20 = bf16[32,32,128]{2,1,0:T(8,128)(2,1)S(1)} all-to-all(bf16[32,32,128]{2,1,0:T(8,128)(2,1)S(1)} %bitcast.17), channel_id=1, replica_groups=mesh['dom'=16,'band'=32] {'band'}, dimensions={0} | all-to-all | bytes 524288 | tf_op jit(solution)/shard_map/back/all_to_all | solution.py:183
  122.0 0.1 convert_bitcast_fusion
  122.0 1.1 copy.4
  (4 shorter events, 0.1 us)
Async XLA Ops:
  0.0 0.8 copy-start
  1.9 16.3 %copy-start.3 = (f32[1,2,16,128]{3,2,1,0:T(8,128)S(1)}, f32[1,2,16,128]{3,2,1,0:T(8,128)}, u32[]{:S(2)}) copy-start(f32[1,2,16,128]{3,2,1,0:T(8,128)} %param.4) | copy-start | bytes 49156
  1.9 47.4 %all-to-all-start = ((bf16[32,32,512]{2,1,0:T(8,128)(2,1)}), bf16[32,32,512]{2,1,0:T(8,128)(2,1)S(1)}, u32[]{:S(2)}, u32[]{:S(2)}) async-start(bf16[32,32,512]{2,1,0:T(8,128)(2,1)} %broadcast_in_dim.4), calls=%async_computation | async-start | bytes 2097152 | tf_op jit(solution)/shard_map/ritz/all_to_all | solution.py:158
  18.3 1.0 copy-start.2
  49.4 16.1 %all-to-all-start.1 = ((bf16[16,4,2,16,128]{4,3,2,1,0:T(8,128)(2,1)}), bf16[16,4,2,16,128]{4,3,2,1,0:T(8,128)(2,1)S(1)}, u32[]{:S(2)}, u32[]{:S(2)}) async-start(bf16[16,4,2,16,128]{4,3,2,1,0:T(8,128)(2,1)} %pad_maximum_fusion), calls=%async_computation.1 | async-start | bytes 1048576 | tf_op jit(solution)/shard_map/spread/all_to_all | solution.py:168
  54.6 46.9 %collective-permute-start = (bf16[1024,512]{1,0:T(8,128)(2,1)S(1)}, bf16[1024,512]{1,0:T(8,128)(2,1)S(1)}, u32[]{:S(2)}, u32[]{:S(2)}) collective-permute-start(bf16[1024,512]{1,0:T(8,128)(2,1)S(1)} %bitcast.12), channel_id=1, source_target_pairs={{0,32},{32,0},{64,96},{96,64},{128,160},{160,128},{192,224},{224,1... | collective-permute-start | bytes 3145736 | tf_op jit(solution)/shard_map/ritz/ppermute | solution.py:159
  65.5 0.8 copy-start.1
  75.6 25.5 %all-to-all-start.2 = ((bf16[512,2,128]{2,1,0:T(2,128)(2,1)}), bf16[512,2,128]{2,1,0:T(2,128)(2,1)S(1)}, u32[]{:S(2)}, u32[]{:S(2)}) async-start(bf16[512,2,128]{2,1,0:T(2,128)(2,1)} %bitcast.16), calls=%async_computation.2 | async-start | bytes 524288 | tf_op jit(solution)/shard_map/turn/all_to_all | solution.py:172

commit v2 on v1

--- a/solution.py
+++ b/solution.py
@@ -6,6 +6,7 @@
 from jax.experimental import pallas as pl
 from jax.experimental.pallas import tpu as pltpu
 from jax.sharding import PartitionSpec as P
+
 
 DEG = 4
 
@@ -26,7 +27,7 @@
     first_scale = sigma_now / half_width
     inverse_gain = 2.0 / sigma_now
     weights = []
-    for degree_step in range(1, degree):
+    for _ in range(1, degree):
         sigma_next = 1.0 / (inverse_gain - sigma_now)
         weights.append((2.0 * sigma_next / half_width, sigma_now * sigma_next))
         sigma_now = sigma_next
@@ -142,6 +143,35 @@
     )
 
 
+def rotate_kernel(n_band, order, n_mine, half, nz):
+    n_all = n_band * n_mine
+
+    def body(place, mine, other, rows, out, sums):
+        core = place[1]
+        near = rows[pl.ds(pl.multiple_of(core * half, half), half), :]
+        far = rows[pl.ds(pl.multiple_of((1 - core) * half, half), half), :]
+        sums[...] = jnp.dot(
+            mine[...], near, preferred_element_type=jnp.float32
+        ) + jnp.dot(other[...], far, preferred_element_type=jnp.float32)
+        for r, mask in enumerate(order):
+            at = pl.multiple_of(lax.bitwise_xor(place[0], mask) * n_mine, n_mine)
+            out[pl.ds(at, n_mine), :] = sums[r * n_mine : (r + 1) * n_mine, :].astype(jnp.bfloat16)
+
+    vmem = pl.BlockSpec(memory_space=pltpu.VMEM)
+    return pl.pallas_call(
+        body,
+        out_shape=jax.ShapeDtypeStruct((n_all, nz), jnp.bfloat16),
+        in_specs=[pl.BlockSpec(memory_space=pltpu.SMEM), vmem, vmem, vmem],
+        out_specs=vmem,
+        scratch_shapes=[pltpu.VMEM((n_all, nz), jnp.float32)],
+        name="rotate",
+    )
+
+
+def in_vmem(x):
+    return pltpu.with_memory_space_constraint(x, pltpu.VMEM)
+
+
 def on_device(orbitals, potential, ritz):
     n_dom = lax.axis_size("dom")
     n_band = lax.axis_size("band")
@@ -150,13 +180,7 @@
     n_own = n_mine // n_dom
     half = n_all // 2
     core = lax.rem(lax.axis_index("dom"), 2)
-
-    columns = ritz.T
-    piece = lax.dynamic_slice_in_dim(columns, core * half, half, 1)
-    many = jnp.broadcast_to(piece[None], (n_band,) + piece.shape)
-    with jax.named_scope("ritz"):
-        mine = lax.all_to_all(many, "band", 0, 0, tiled=True).reshape(n_all, half)
-        other = lax.ppermute(mine, "dom", [(d, d ^ 1) for d in range(n_dom)])
+    band = lax.axis_index("band")
 
     pot = potential[0]
     high = lax.reduce_precision(pot, 8, 7)
@@ -164,23 +188,26 @@
     parts = jnp.broadcast_to(parts[None], (n_dom, 2, cx, cy, nz))
     blocks = orbitals.reshape(n_dom, n_own, cx, cy, nz)
     blocks = jnp.concatenate([blocks, parts], axis=1)
-    with jax.named_scope("spread"):
-        blocks = lax.all_to_all(blocks, "dom", 0, 0, tiled=True)
-    filtered = filter_kernel(n_dom, n_own, cx, cy, nz)(blocks)
-
-    with jax.named_scope("turn"):
-        rows = lax.all_to_all(
-            filtered.reshape(n_band * n_dom, n_own, nz), ("band", "dom"), 0, 0, tiled=True
-        ).reshape(n_all, nz)
-
-    def product(left, which):
-        right = lax.dynamic_slice_in_dim(rows, which * half, half, 0)
-        return jnp.dot(left, right, preferred_element_type=jnp.float32)
-
-    rotated = product(mine, core) + product(other, 1 - core)
-    rotated = rotated.astype(jnp.bfloat16).reshape(n_band, n_mine, nz)
-    with jax.named_scope("back"):
-        rotated = lax.all_to_all(rotated, "band", 0, 0, tiled=True)
+    blocks = lax.all_to_all(blocks, "dom", 0, 0, tiled=True)
+    filtered = filter_kernel(n_dom, n_own, cx, cy, nz)(in_vmem(blocks))
+
+    mine = lax.dynamic_slice_in_dim(ritz.T, core * half, half, 1)
+    order = [0]
+    for mask in (4, 16, 2, 8, 1):
+        more = lax.ppermute(mine, "band", [(p, p ^ mask) for p in range(n_band)])
+        mine = jnp.concatenate([mine, more], axis=0)
+        order = order + [r ^ mask for r in order]
+    other = lax.ppermute(mine, "dom", [(d, d ^ 1) for d in range(n_dom)])
+
+    rows = lax.all_to_all(
+        filtered.reshape(n_band * n_dom, n_own, nz), ("band", "dom"), 0, 0, tiled=True
+    ).reshape(n_all, nz)
+
+    place = jnp.stack([band, core])
+    rotated = rotate_kernel(n_band, order, n_mine, half, nz)(
+        place, in_vmem(mine), in_vmem(other), in_vmem(rows)
+    )
+    rotated = lax.all_to_all(rotated.reshape(n_band, n_mine, nz), "band", 0, 0, tiled=True)
     rotated = rotated.transpose(1, 0, 2).astype(jnp.float32)
     return rotated.reshape(orbitals.shape)
 

time: 124 us -> 131 us (1.056)
  the two profiles are of different devices: /device:TPU:8 before, /device:TPU:1 now
where the time goes in v2:
time: 131 us; the launch traced here: 128 us
  starting transfers between devices  58.4 us (45%)
  waiting for transfers between devices  39.4 us (30%)
  blocking collectives  16.4 us (13%)
  Pallas kernels  10.4 us (8%)
  local copies, waits for them, and re-layouts  2.03 us (2%)
  other arithmetic  1.6 us (1%)
    ppermute x5, starting transfers between devices, on_device(): more = lax.ppermute(mine, 'band', [(p, p ^ mask) for p in range(n_band)])  30.9 us
    ppermute x5, waiting for transfers between devices, on_device(): more = lax.ppermute(mine, 'band', [(p, p ^ mask) for p in range(n_band)])  22.5 us
    all_to_all x1, starting transfers between devices, on_device(): lax.all_to_all(filtered.reshape(n_band * n_dom, n_own, nz), ('band', 'dom...  17.1 us
    all_to_all x1, waiting for transfers between devices, on_device(): lax.all_to_all(filtered.reshape(n_band * n_dom, n_own, nz), ('band', 'dom...  16.4 us
    all_to_all x1, blocking collectives, on_device(): lax.all_to_all(rotated.reshape(n_band, n_mine, nz), 'band', 0, 0, tiled=T...  16.4 us
    pallas_call x1, Pallas kernels, on_device(): filtered = filter_kernel(n_dom, n_own, cx, cy, nz)(in_vmem(blocks))  8.29 us
    all_to_all x1, starting transfers between devices, on_device(): blocks = lax.all_to_all(blocks, 'dom', 0, 0, tiled=True)  5.88 us
    ppermute x1, starting transfers between devices, on_device(): other = lax.ppermute(mine, 'dom', [(d, d ^ 1) for d in range(n_dom)])  4.48 us
  transfers between devices with their start and end apart: 8, of which 7 were waited for; matrix products, arithmetic and copies ran while one was open for 1% of the time, Pallas kernels for 6%

profile of v2, /device:TPU:1, one launch (start us, length us, event | category | flops | bytes accessed | tf_op | source)
XLA Modules:
  0.0 128.4 jit_solution(6288068249796783109)
XLA Ops:
  0.0 0.8 constant_dynamic-update-slice_fusion.4
  0.8 8.3 %collective-permute-start = (bf16[32,512]{1,0:T(8,128)(2,1)S(1)}, bf16[32,512]{1,0:T(8,128)(2,1)S(1)}, u32[]{:S(2)}, u32[]{:S(2)}) collective-permute-start(bf16[32,512]{1,0:T(8,128)(2,1)S(1)} %get-tuple-element.6), channel_id=1, source_target_pairs={{0,4},{1,5},{2,6},{3,7},{4,0},{5,1},{6,2},{7,3},{8,12},{9,13},{10,... | collective-permute-start | bytes 98312 | tf_op jit(solution)/shard_map/ppermute | solution.py:197
  9.0 1.3 %collective-permute-done = bf16[32,512]{1,0:T(8,128)(2,1)S(1)} collective-permute-done((bf16[32,512]{1,0:T(8,128)(2,1)S(1)}, bf16[32,512]{1,0:T(8,128)(2,1)S(1)}, u32[]{:S(2)}, u32[]{:S(2)}) %collective-permute-start) | collective-permute-done | bytes 32800 | tf_op jit(solution)/shard_map/ppermute | solution.py:197
  10.4 0.0 copy-start.1
  10.4 10.6 %collective-permute-start.1 = (bf16[64,512]{1,0:T(8,128)(2,1)S(1)}, bf16[64,512]{1,0:T(8,128)(2,1)S(1)}, u32[]{:S(2)}, u32[]{:S(2)}) collective-permute-start(bf16[64,512]{1,0:T(8,128)(2,1)S(1)} %pad_maximum_fusion.3), channel_id=1, source_target_pairs={{0,16},{1,17},{2,18},{3,19},{4,20},{5,21},{6,22},{7,23},{8,24},{9,... | collective-permute-start | bytes 196616 | tf_op jit(solution)/shard_map/ppermute | solution.py:197
  21.0 1.7 %collective-permute-done.1 = bf16[64,512]{1,0:T(8,128)(2,1)S(1)} collective-permute-done((bf16[64,512]{1,0:T(8,128)(2,1)S(1)}, bf16[64,512]{1,0:T(8,128)(2,1)S(1)}, u32[]{:S(2)}, u32[]{:S(2)}) %collective-permute-start.1) | collective-permute-done | bytes 65568 | tf_op jit(solution)/shard_map/ppermute | solution.py:197
  22.7 4.4 %collective-permute-start.2 = (bf16[128,512]{1,0:T(8,128)(2,1)S(1)}, bf16[128,512]{1,0:T(8,128)(2,1)S(1)}, u32[]{:S(2)}, u32[]{:S(2)}) collective-permute-start(bf16[128,512]{1,0:T(8,128)(2,1)S(1)} %pad_maximum_fusion.2), channel_id=1, source_target_pairs={{0,2},{1,3},{2,0},{3,1},{4,6},{5,7},{6,4},{7,5},{8,10},{9,11},{10,... | collective-permute-start | bytes 393224 | tf_op jit(solution)/shard_map/ppermute | solution.py:197
  27.1 0.0 copy-done.1
  27.2 3.7 %collective-permute-done.2 = bf16[128,512]{1,0:T(8,128)(2,1)S(1)} collective-permute-done((bf16[128,512]{1,0:T(8,128)(2,1)S(1)}, bf16[128,512]{1,0:T(8,128)(2,1)S(1)}, u32[]{:S(2)}, u32[]{:S(2)}) %collective-permute-start.2) | collective-permute-done | bytes 131104 | tf_op jit(solution)/shard_map/ppermute | solution.py:197
  30.9 5.3 %collective-permute-start.3 = (bf16[256,512]{1,0:T(8,128)(2,1)S(1)}, bf16[256,512]{1,0:T(8,128)(2,1)S(1)}, u32[]{:S(2)}, u32[]{:S(2)}) collective-permute-start(bf16[256,512]{1,0:T(8,128)(2,1)S(1)} %pad_maximum_fusion.1), channel_id=1, source_target_pairs={{0,8},{1,9},{2,10},{3,11},{4,12},{5,13},{6,14},{7,15},{8,0},{9,1},... | collective-permute-start | bytes 786440 | tf_op jit(solution)/shard_map/ppermute | solution.py:197
  36.3 11.1 %collective-permute-done.3 = bf16[256,512]{1,0:T(8,128)(2,1)S(1)} collective-permute-done((bf16[256,512]{1,0:T(8,128)(2,1)S(1)}, bf16[256,512]{1,0:T(8,128)(2,1)S(1)}, u32[]{:S(2)}, u32[]{:S(2)}) %collective-permute-start.3) | collective-permute-done | bytes 262176 | tf_op jit(solution)/shard_map/ppermute | solution.py:197
  47.5 0.0 copy-start
  47.5 2.3 %collective-permute-start.4 = (bf16[512,512]{1,0:T(8,128)(2,1)S(1)}, bf16[512,512]{1,0:T(8,128)(2,1)S(1)}, u32[]{:S(2)}, u32[]{:S(2)}) collective-permute-start(bf16[512,512]{1,0:T(8,128)(2,1)S(1)} %get-tuple-element.7), channel_id=1, source_target_pairs={{0,1},{1,0},{2,3},{3,2},{4,5},{5,4},{6,7},{7,6},{8,9},{9,8},{10,11... | collective-permute-start | bytes 1572872 | tf_op jit(solution)/shard_map/ppermute | solution.py:197
  49.8 0.0 copy-done
  49.8 0.8 pad_maximum_fusion
  50.7 5.9 %all-to-all-start = ((bf16[16,4,2,16,128]{4,3,2,1,0:T(8,128)(2,1)}), bf16[16,4,2,16,128]{4,3,2,1,0:T(8,128)(2,1)S(1)}, u32[]{:S(2)}, u32[]{:S(2)}) async-start(bf16[16,4,2,16,128]{4,3,2,1,0:T(8,128)(2,1)} %pad_maximum_fusion), calls=%async_computation | async-start | bytes 1048576 | tf_op jit(solution)/shard_map/all_to_all | solution.py:191
  56.6 4.7 %collective-permute-done.4 = bf16[512,512]{1,0:T(8,128)(2,1)S(1)} collective-permute-done((bf16[512,512]{1,0:T(8,128)(2,1)S(1)}, bf16[512,512]{1,0:T(8,128)(2,1)S(1)}, u32[]{:S(2)}, u32[]{:S(2)}) %collective-permute-start.4) | collective-permute-done | bytes 524320 | tf_op jit(solution)/shard_map/ppermute | solution.py:197
  61.3 4.5 %collective-permute-start.5 = (bf16[1024,512]{1,0:T(8,128)(2,1)S(1)}, bf16[1024,512]{1,0:T(8,128)(2,1)S(1)}, u32[]{:S(2)}, u32[]{:S(2)}) collective-permute-start(bf16[1024,512]{1,0:T(8,128)(2,1)S(1)} %constant_dynamic-update-slice_fusion.5.mine), channel_id=1, source_target_pairs={{0,32},{32,0},{64,96},{96,64},{128,160},{160,128},{192,224},{224,1... | collective-permute-start | bytes 3145736 | tf_op jit(solution)/shard_map/ppermute | solution.py:200
  65.8 0.4 all-to-all-done.blocks
  66.2 8.3 %chebyshev.1 = bf16[1024,128]{1,0:T(8,128)(2,1)} custom-call(bf16[16,4,2,16,128]{4,3,2,1,0:T(8,128)(2,1)S(1)} %all-to-all-done.blocks), custom_call_target="tpu_custom_call" | custom-call | tf_op jit(solution)/shard_map/chebyshev/pallas_call | solution.py:192
  74.5 17.1 %all-to-all-start.1 = ((bf16[512,2,128]{2,1,0:T(2,128)(2,1)}), bf16[512,2,128]{2,1,0:T(2,128)(2,1)S(1)}, u32[]{:S(2)}, u32[]{:S(2)}) async-start(bf16[512,2,128]{2,1,0:T(2,128)(2,1)} %bitcast.13), calls=%async_computation.1 | async-start | bytes 524288 | tf_op jit(solution)/shard_map/all_to_all | solution.py:202
  91.7 0.7 pad_add_fusion.place
  92.3 16.4 %all-to-all-done.1 = bf16[512,2,128]{2,1,0:T(2,128)(2,1)S(1)} async-done(((bf16[512,2,128]{2,1,0:T(2,128)(2,1)}), bf16[512,2,128]{2,1,0:T(2,128)(2,1)S(1)}, u32[]{:S(2)}, u32[]{:S(2)}) %all-to-all-start.1) | async-done | bytes 262176 | tf_op jit(solution)/shard_map/all_to_all | solution.py:202
  108.8 0.0 collective-permute-done.5.other
  108.8 2.1 %rotate.1 = bf16[1024,128]{1,0:T(8,128)(2,1)} custom-call(s32[2]{0:T(128)} %pad_add_fusion.place, bf16[1024,512]{1,0:T(8,128)(2,1)S(1)} %constant_dynamic-update-slice_fusion.5.mine, bf16[1024,512]{1,0:T(8,128)(2,1)S(1)} %collective-permute-done.5.other, bf16[1024,128]{1,0:T(8,128)(2,1)S(1)} %bitcast.12), custom_call_target="tpu_custom_call" | custom-call | tf_op jit(solution)/shard_map/rotate/pallas_call | solution.py:207
  110.9 16.4 %all_to_all.15 = bf16[32,32,128]{2,1,0:T(8,128)(2,1)S(1)} all-to-all(bf16[32,32,128]{2,1,0:T(8,128)(2,1)} %bitcast.14), channel_id=1, replica_groups=mesh['dom'=16,'band'=32] {'band'}, dimensions={0} | all-to-all | bytes 524288 | tf_op jit(solution)/shard_map/all_to_all | solution.py:210
  127.2 0.1 convert_bitcast_fusion
  127.3 1.1 copy.4
  (12 shorter events, 0.2 us)
Async XLA Ops:
  0.8 9.6 %collective-permute-start = (bf16[32,512]{1,0:T(8,128)(2,1)S(1)}, bf16[32,512]{1,0:T(8,128)(2,1)S(1)}, u32[]{:S(2)}, u32[]{:S(2)}) collective-permute-start(bf16[32,512]{1,0:T(8,128)(2,1)S(1)} %get-tuple-element.6), channel_id=1, source_target_pairs={{0,4},{1,5},{2,6},{3,7},{4,0},{5,1},{6,2},{7,3},{8,12},{9,13},{10,... | collective-permute-start | bytes 98312 | tf_op jit(solution)/shard_map/ppermute | solution.py:197
  10.4 16.8 %copy-start.1 = (f32[1,2,16,128]{3,2,1,0:T(8,128)S(1)}, f32[1,2,16,128]{3,2,1,0:T(8,128)}, u32[]{:S(2)}) copy-start(f32[1,2,16,128]{3,2,1,0:T(8,128)} %param.4) | copy-start | bytes 49156
  10.4 12.4 %collective-permute-start.1 = (bf16[64,512]{1,0:T(8,128)(2,1)S(1)}, bf16[64,512]{1,0:T(8,128)(2,1)S(1)}, u32[]{:S(2)}, u32[]{:S(2)}) collective-permute-start(bf16[64,512]{1,0:T(8,128)(2,1)S(1)} %pad_maximum_fusion.3), channel_id=1, source_target_pairs={{0,16},{1,17},{2,18},{3,19},{4,20},{5,21},{6,22},{7,23},{8,24},{9,... | collective-permute-start | bytes 196616 | tf_op jit(solution)/shard_map/ppermute | solution.py:197
  22.7 8.2 %collective-permute-start.2 = (bf16[128,512]{1,0:T(8,128)(2,1)S(1)}, bf16[128,512]{1,0:T(8,128)(2,1)S(1)}, u32[]{:S(2)}, u32[]{:S(2)}) collective-permute-start(bf16[128,512]{1,0:T(8,128)(2,1)S(1)} %pad_maximum_fusion.2), channel_id=1, source_target_pairs={{0,2},{1,3},{2,0},{3,1},{4,6},{5,7},{6,4},{7,5},{8,10},{9,11},{10,... | collective-permute-start | bytes 393224 | tf_op jit(solution)/shard_map/ppermute | solution.py:197
  30.9 16.5 %collective-permute-start.3 = (bf16[256,512]{1,0:T(8,128)(2,1)S(1)}, bf16[256,512]{1,0:T(8,128)(2,1)S(1)}, u32[]{:S(2)}, u32[]{:S(2)}) collective-permute-start(bf16[256,512]{1,0:T(8,128)(2,1)S(1)} %pad_maximum_fusion.1), channel_id=1, source_target_pairs={{0,8},{1,9},{2,10},{3,11},{4,12},{5,13},{6,14},{7,15},{8,0},{9,1},... | collective-permute-start | bytes 786440 | tf_op jit(solution)/shard_map/ppermute | solution.py:197
  47.5 2.4 %copy-start = (bf16[32,1,2,16,128]{4,3,2,1,0:T(8,128)(2,1)S(1)}, bf16[32,1,2,16,128]{4,3,2,1,0:T(8,128)(2,1)}, u32[]{:S(2)}) copy-start(bf16[32,1,2,16,128]{4,3,2,1,0:T(8,128)(2,1)} %param.3) | copy-start | bytes 786436
  47.5 13.8 %collective-permute-start.4 = (bf16[512,512]{1,0:T(8,128)(2,1)S(1)}, bf16[512,512]{1,0:T(8,128)(2,1)S(1)}, u32[]{:S(2)}, u32[]{:S(2)}) collective-permute-start(bf16[512,512]{1,0:T(8,128)(2,1)S(1)} %get-tuple-element.7), channel_id=1, source_target_pairs={{0,1},{1,0},{2,3},{3,2},{4,5},{5,4},{6,7},{7,6},{8,9},{9,8},{10,11... | collective-permute-start | bytes 1572872 | tf_op jit(solution)/shard_map/ppermute | solution.py:197
  50.7 15.5 %all-to-all-start = ((bf16[16,4,2,16,128]{4,3,2,1,0:T(8,128)(2,1)}), bf16[16,4,2,16,128]{4,3,2,1,0:T(8,128)(2,1)S(1)}, u32[]{:S(2)}, u32[]{:S(2)}) async-start(bf16[16,4,2,16,128]{4,3,2,1,0:T(8,128)(2,1)} %pad_maximum_fusion), calls=%async_computation | async-start | bytes 1048576 | tf_op jit(solution)/shard_map/all_to_all | solution.py:191
  61.3 47.5 %collective-permute-start.5 = (bf16[1024,512]{1,0:T(8,128)(2,1)S(1)}, bf16[1024,512]{1,0:T(8,128)(2,1)S(1)}, u32[]{:S(2)}, u32[]{:S(2)}) collective-permute-start(bf16[1024,512]{1,0:T(8,128)(2,1)S(1)} %constant_dynamic-update-slice_fusion.5.mine), channel_id=1, source_target_pairs={{0,32},{32,0},{64,96},{96,64},{128,160},{160,128},{192,224},{224,1... | collective-permute-start | bytes 3145736 | tf_op jit(solution)/shard_map/ppermute | solution.py:200
  74.5 34.3 %all-to-all-start.1 = ((bf16[512,2,128]{2,1,0:T(2,128)(2,1)}), bf16[512,2,128]{2,1,0:T(2,128)(2,1)S(1)}, u32[]{:S(2)}, u32[]{:S(2)}) async-start(bf16[512,2,128]{2,1,0:T(2,128)(2,1)} %bitcast.13), calls=%async_computation.1 | async-start | bytes 524288 | tf_op jit(solution)/shard_map/all_to_all | solution.py:202

commit v3 on v2

--- a/solution.py
+++ b/solution.py
@@ -130,7 +130,7 @@
     rows_out = cx * cy * n_dom * n_own
     return pl.pallas_call(
         body,
-        out_shape=jax.ShapeDtypeStruct((rows_out, nz), jnp.bfloat16),
+        out_shape=pltpu.VMEM((rows_out, nz), jnp.bfloat16),
         in_specs=[pl.BlockSpec(memory_space=pltpu.VMEM)],
         out_specs=pl.BlockSpec(memory_space=pltpu.VMEM),
         scratch_shapes=[
@@ -143,27 +143,27 @@
     )
 
 
-def rotate_kernel(n_band, order, n_mine, half, nz):
-    n_all = n_band * n_mine
-
-    def body(place, mine, other, rows, out, sums):
-        core = place[1]
-        near = rows[pl.ds(pl.multiple_of(core * half, half), half), :]
-        far = rows[pl.ds(pl.multiple_of((1 - core) * half, half), half), :]
-        sums[...] = jnp.dot(
-            mine[...], near, preferred_element_type=jnp.float32
-        ) + jnp.dot(other[...], far, preferred_element_type=jnp.float32)
-        for r, mask in enumerate(order):
-            at = pl.multiple_of(lax.bitwise_xor(place[0], mask) * n_mine, n_mine)
-            out[pl.ds(at, n_mine), :] = sums[r * n_mine : (r + 1) * n_mine, :].astype(jnp.bfloat16)
+def rotate_kernel(n_all, n_x, piece, nz):
+    def body(place, mine, other, rows, out):
+        core, x = place[0], place[1]
+
+        def half(pieces, which):
+            left = jnp.concatenate([pieces[r] for r in range(n_x)], axis=1)
+            right = []
+            for r in range(n_x):
+                q = which * n_x + lax.rem(x + r, n_x)
+                right.append(rows[pl.ds(pl.multiple_of(q * piece, piece), piece), :])
+            right = jnp.concatenate(right, axis=0)
+            return jnp.dot(left, right, preferred_element_type=jnp.float32)
+
+        out[...] = (half(mine, core) + half(other, 1 - core)).astype(jnp.bfloat16)
 
     vmem = pl.BlockSpec(memory_space=pltpu.VMEM)
     return pl.pallas_call(
         body,
-        out_shape=jax.ShapeDtypeStruct((n_all, nz), jnp.bfloat16),
+        out_shape=pltpu.VMEM((n_all, nz), jnp.bfloat16),
         in_specs=[pl.BlockSpec(memory_space=pltpu.SMEM), vmem, vmem, vmem],
         out_specs=vmem,
-        scratch_shapes=[pltpu.VMEM((n_all, nz), jnp.float32)],
         name="rotate",
     )
 
@@ -178,9 +178,10 @@
     n_mine, _, cx, cy, nz = orbitals.shape
     n_all = ritz.shape[0]
     n_own = n_mine // n_dom
-    half = n_all // 2
-    core = lax.rem(lax.axis_index("dom"), 2)
-    band = lax.axis_index("band")
+    n_x = n_dom // 4
+    dom = lax.axis_index("dom")
+    core = lax.rem(dom, 2)
+    x = lax.rem(lax.div(dom, 2), n_x)
 
     pot = potential[0]
     high = lax.reduce_precision(pot, 8, 7)
@@ -191,20 +192,30 @@
     blocks = lax.all_to_all(blocks, "dom", 0, 0, tiled=True)
     filtered = filter_kernel(n_dom, n_own, cx, cy, nz)(in_vmem(blocks))
 
-    mine = lax.dynamic_slice_in_dim(ritz.T, core * half, half, 1)
-    order = [0]
-    for mask in (4, 16, 2, 8, 1):
-        more = lax.ppermute(mine, "band", [(p, p ^ mask) for p in range(n_band)])
-        mine = jnp.concatenate([mine, more], axis=0)
-        order = order + [r ^ mask for r in order]
+    piece = n_all // (2 * n_x)
+    own = lax.dynamic_slice_in_dim(ritz.T, (core * n_x + x) * piece, piece, 1)
+    many = jnp.broadcast_to(own[None], (n_band,) + own.shape)
+
+    def from_x(value, step):
+        pairs = []
+        for d in range(n_dom):
+            z, at, c = d // (2 * n_x), d // 2 % n_x, d % 2
+            pairs.append((z * 2 * n_x + (at + step) % n_x * 2 + c, d))
+        return lax.ppermute(value, "dom", pairs)
+
+    own = lax.all_to_all(many, "band", 0, 0, tiled=True).reshape(n_all, piece)
+    after = from_x(own, 1)
+    before = from_x(own, -1)
+    far = from_x(after, 1)
+    mine = jnp.stack([own, after, far, before])
     other = lax.ppermute(mine, "dom", [(d, d ^ 1) for d in range(n_dom)])
 
     rows = lax.all_to_all(
         filtered.reshape(n_band * n_dom, n_own, nz), ("band", "dom"), 0, 0, tiled=True
     ).reshape(n_all, nz)
 
-    place = jnp.stack([band, core])
-    rotated = rotate_kernel(n_band, order, n_mine, half, nz)(
+    place = jnp.stack([core, x])
+    rotated = rotate_kernel(n_all, n_x, piece, nz)(
         place, in_vmem(mine), in_vmem(other), in_vmem(rows)
     )
     rotated = lax.all_to_all(rotated.reshape(n_band, n_mine, nz), "band", 0, 0, tiled=True)

time: 131 us -> 119 us (0.908)
  the two profiles are of different devices: /device:TPU:1 before, /device:TPU:8 now
where the time goes in v3:
time: 119 us; the launch traced here: 118 us
  starting transfers between devices  42.1 us (35%)
  waiting for transfers between devices  38.8 us (33%)
  blocking collectives  19.9 us (17%)
  Pallas kernels  10.2 us (9%)
  local copies, waits for them, and re-layouts  4.95 us (4%)
  other arithmetic  1.7 us (1%)
    all_to_all x1, blocking collectives, on_device(): lax.all_to_all(rotated.reshape(n_band, n_mine, nz), 'band', 0, 0, tiled=T...  19.9 us
    all_to_all x1, starting transfers between devices, on_device(): own = lax.all_to_all(many, 'band', 0, 0, tiled=True).reshape(n_all, piece)  16.3 us
    all_to_all x1, waiting for transfers between devices, on_device(): lax.all_to_all(filtered.reshape(n_band * n_dom, n_own, nz), ('band', 'dom...  15.7 us
    all_to_all x1, waiting for transfers between devices, on_device(): own = lax.all_to_all(many, 'band', 0, 0, tiled=True).reshape(n_all, piece)  14.7 us
    ppermute x3, starting transfers between devices, from_x(): return lax.ppermute(value, 'dom', pairs)  11.7 us
    all_to_all x1, starting transfers between devices, on_device(): lax.all_to_all(filtered.reshape(n_band * n_dom, n_own, nz), ('band', 'dom...  8.64 us
    ppermute x3, waiting for transfers between devices, from_x(): return lax.ppermute(value, 'dom', pairs)  8.39 us
    pallas_call x1, Pallas kernels, on_device(): filtered = filter_kernel(n_dom, n_own, cx, cy, nz)(in_vmem(blocks))  8.29 us
  transfers between devices with their start and end apart: 7, of which 3 were waited for; matrix products, arithmetic and copies ran while one was open for 1% of the time, Pallas kernels for 7%

profile of v3, /device:TPU:8, one launch (start us, length us, event | category | flops | bytes accessed | tf_op | source)
XLA Modules:
  0.0 117.9 jit_solution(6602489640582233825)
XLA Ops:
  0.0 0.0 copy-start
  0.0 0.8 copy-done
  0.8 0.7 broadcast_in_dim.4
  1.6 0.0 copy-start.4
  1.6 16.3 %all-to-all-start = ((bf16[32,32,128]{2,1,0:T(8,128)(2,1)}), bf16[32,32,128]{2,1,0:T(8,128)(2,1)S(1)}, u32[]{:S(2)}, u32[]{:S(2)}) async-start(bf16[32,32,128]{2,1,0:T(8,128)(2,1)} %broadcast_in_dim.4), calls=%async_computation | async-start | bytes 524288 | tf_op jit(solution)/shard_map/all_to_all | solution.py:206
  17.9 0.0 copy-done.4
  17.9 0.0 copy-start.3
  17.9 14.7 %all-to-all-done = bf16[32,32,128]{2,1,0:T(8,128)(2,1)S(1)} async-done(((bf16[32,32,128]{2,1,0:T(8,128)(2,1)}), bf16[32,32,128]{2,1,0:T(8,128)(2,1)S(1)}, u32[]{:S(2)}, u32[]{:S(2)}) %all-to-all-start) | async-done | bytes 262176 | tf_op jit(solution)/shard_map/all_to_all | solution.py:206
  32.7 4.7 %collective-permute-start = (bf16[1024,128]{1,0:T(8,128)(2,1)S(1)}, bf16[1024,128]{1,0:T(8,128)(2,1)S(1)}, u32[]{:S(2)}, u32[]{:S(2)}) collective-permute-start(bf16[1024,128]{1,0:T(8,128)(2,1)S(1)} %bitcast.18), channel_id=1, source_target_pairs={{64,0},{96,32},{128,64},{160,96},{192,128},{224,160},{0,192},{32,2... | collective-permute-start | bytes 786440 | tf_op jit(solution)/shard_map/ppermute | solution.py:204
  37.4 0.0 copy-done.3
  37.4 0.8 pad_maximum_fusion.1
  38.2 3.6 %all-to-all-start.1 = ((bf16[16,4,2,16,128]{4,3,2,1,0:T(8,128)(2,1)}), bf16[16,4,2,16,128]{4,3,2,1,0:T(8,128)(2,1)S(1)}, u32[]{:S(2)}, u32[]{:S(2)}) async-start(bf16[16,4,2,16,128]{4,3,2,1,0:T(8,128)(2,1)} %pad_maximum_fusion.1), calls=%async_computation.1 | async-start | bytes 1048576 | tf_op jit(solution)/shard_map/all_to_all | solution.py:192
  41.8 3.7 %collective-permute-start.2 = (bf16[1024,128]{1,0:T(8,128)(2,1)S(1)}, bf16[1024,128]{1,0:T(8,128)(2,1)S(1)}, u32[]{:S(2)}, u32[]{:S(2)}) collective-permute-start(bf16[1024,128]{1,0:T(8,128)(2,1)S(1)} %bitcast.19), channel_id=1, source_target_pairs={{192,0},{224,32},{0,64},{32,96},{64,128},{96,160},{128,192},{160,2... | collective-permute-start | bytes 786440 | tf_op jit(solution)/shard_map/ppermute | solution.py:204
  45.5 0.0 collective-permute-done
  45.5 3.3 %collective-permute-start.1 = (bf16[1024,128]{1,0:T(8,128)(2,1)S(1)}, bf16[1024,128]{1,0:T(8,128)(2,1)S(1)}, u32[]{:S(2)}, u32[]{:S(2)}) collective-permute-start(bf16[1024,128]{1,0:T(8,128)(2,1)S(1)} %collective-permute-done), channel_id=1, source_target_pairs={{64,0},{96,32},{128,64},{160,96},{192,128},{224,160},{0,192},{32,2... | collective-permute-start | bytes 786440 | tf_op jit(solution)/shard_map/ppermute | solution.py:204
  48.9 8.4 %collective-permute-done.2 = bf16[1024,128]{1,0:T(8,128)(2,1)S(1)} collective-permute-done((bf16[1024,128]{1,0:T(8,128)(2,1)S(1)}, bf16[1024,128]{1,0:T(8,128)(2,1)S(1)}, u32[]{:S(2)}, u32[]{:S(2)}) %collective-permute-start.2) | collective-permute-done | bytes 262176 | tf_op jit(solution)/shard_map/ppermute | solution.py:204
  57.3 0.0 collective-permute-done.1
  57.3 0.1 pad_maximum_fusion.mine
  57.4 1.9 %collective-permute-start.3 = (bf16[4,1024,128]{2,1,0:T(8,128)(2,1)S(1)}, bf16[4,1024,128]{2,1,0:T(8,128)(2,1)}, u32[]{:S(2)}, u32[]{:S(2)}) collective-permute-start(bf16[4,1024,128]{2,1,0:T(8,128)(2,1)S(1)} %pad_maximum_fusion.mine), channel_id=1, source_target_pairs={{0,32},{32,0},{64,96},{96,64},{128,160},{160,128},{192,224},{224,1... | collective-permute-start | bytes 3145736 | tf_op jit(solution)/shard_map/ppermute | solution.py:211
  59.3 0.0 copy-start.1
  59.4 1.0 copy-done.1
  60.3 0.0 all-to-all-done.1.blocks
  60.3 8.3 %chebyshev.1 = bf16[1024,128]{1,0:T(8,128)(2,1)} custom-call(bf16[16,4,2,16,128]{4,3,2,1,0:T(8,128)(2,1)S(1)} %all-to-all-done.1.blocks), custom_call_target="tpu_custom_call" | custom-call | tf_op jit(solution)/shard_map/chebyshev/pallas_call | solution.py:193
  68.6 8.6 %all-to-all-start.2 = ((bf16[512,2,128]{2,1,0:T(2,128)(2,1)}), bf16[512,2,128]{2,1,0:T(2,128)(2,1)S(1)}, u32[]{:S(2)}, u32[]{:S(2)}) async-start(bf16[512,2,128]{2,1,0:T(2,128)(2,1)} %bitcast.9), calls=%async_computation.2 | async-start | bytes 524288 | tf_op jit(solution)/shard_map/all_to_all | solution.py:213
  77.3 0.7 pad_add_fusion.place
  77.9 15.7 %all-to-all-done.2 = bf16[512,2,128]{2,1,0:T(2,128)(2,1)S(1)} async-done(((bf16[512,2,128]{2,1,0:T(2,128)(2,1)}), bf16[512,2,128]{2,1,0:T(2,128)(2,1)S(1)}, u32[]{:S(2)}, u32[]{:S(2)}) %all-to-all-start.2) | async-done | bytes 262176 | tf_op jit(solution)/shard_map/all_to_all | solution.py:213
  93.7 0.0 collective-permute-done.3.other
  93.7 0.0 copy-start.2
  93.7 1.2 %copy-done.2 = bf16[4,1024,128]{2,1,0:T(8,128)(2,1)S(1)} copy-done((bf16[4,1024,128]{2,1,0:T(8,128)(2,1)S(1)}, bf16[4,1024,128]{2,1,0:T(8,128)(2,1)}, u32[]{:S(2)}) %copy-start.2) | copy-done | bytes 1048600
  94.9 1.9 %rotate.1 = bf16[1024,128]{1,0:T(8,128)(2,1)S(1)} custom-call(s32[2]{0:T(128)} %pad_add_fusion.place, bf16[4,1024,128]{2,1,0:T(8,128)(2,1)S(1)} %copy-done.2, bf16[4,1024,128]{2,1,0:T(8,128)(2,1)} %collective-permute-done.3.other, bf16[1024,128]{1,0:T(8,128)(2,1)S(1)} %bitcast.16), custom_call_target="tpu_custom_call" | custom-call | tf_op jit(solution)/shard_map/rotate/pallas_call | solution.py:218
  96.8 19.9 %all_to_all.20 = bf16[32,32,128]{2,1,0:T(8,128)(2,1)S(1)} all-to-all(bf16[32,32,128]{2,1,0:T(8,128)(2,1)S(1)} %bitcast.17), channel_id=1, replica_groups=mesh['dom'=16,'band'=32] {'band'}, dimensions={0} | all-to-all | bytes 524288 | tf_op jit(solution)/shard_map/all_to_all | solution.py:221
  116.8 1.1 copy.4
  (5 shorter events, 0.1 us)
Async XLA Ops:
  0.0 0.8 copy-start
  1.6 16.3 %copy-start.4 = (f32[1,2,16,128]{3,2,1,0:T(8,128)S(1)}, f32[1,2,16,128]{3,2,1,0:T(8,128)}, u32[]{:S(2)}) copy-start(f32[1,2,16,128]{3,2,1,0:T(8,128)} %param.4) | copy-start | bytes 49156
  1.6 31.1 %all-to-all-start = ((bf16[32,32,128]{2,1,0:T(8,128)(2,1)}), bf16[32,32,128]{2,1,0:T(8,128)(2,1)S(1)}, u32[]{:S(2)}, u32[]{:S(2)}) async-start(bf16[32,32,128]{2,1,0:T(8,128)(2,1)} %broadcast_in_dim.4), calls=%async_computation | async-start | bytes 524288 | tf_op jit(solution)/shard_map/all_to_all | solution.py:206
  17.9 19.5 %copy-start.3 = (bf16[32,1,2,16,128]{4,3,2,1,0:T(8,128)(2,1)S(1)}, bf16[32,1,2,16,128]{4,3,2,1,0:T(8,128)(2,1)}, u32[]{:S(2)}) copy-start(bf16[32,1,2,16,128]{4,3,2,1,0:T(8,128)(2,1)} %param.3) | copy-start | bytes 786436
  32.7 12.9 %collective-permute-start = (bf16[1024,128]{1,0:T(8,128)(2,1)S(1)}, bf16[1024,128]{1,0:T(8,128)(2,1)S(1)}, u32[]{:S(2)}, u32[]{:S(2)}) collective-permute-start(bf16[1024,128]{1,0:T(8,128)(2,1)S(1)} %bitcast.18), channel_id=1, source_target_pairs={{64,0},{96,32},{128,64},{160,96},{192,128},{224,160},{0,192},{32,2... | collective-permute-start | bytes 786440 | tf_op jit(solution)/shard_map/ppermute | solution.py:204
  38.2 22.1 %all-to-all-start.1 = ((bf16[16,4,2,16,128]{4,3,2,1,0:T(8,128)(2,1)}), bf16[16,4,2,16,128]{4,3,2,1,0:T(8,128)(2,1)S(1)}, u32[]{:S(2)}, u32[]{:S(2)}) async-start(bf16[16,4,2,16,128]{4,3,2,1,0:T(8,128)(2,1)} %pad_maximum_fusion.1), calls=%async_computation.1 | async-start | bytes 1048576 | tf_op jit(solution)/shard_map/all_to_all | solution.py:192
  41.8 15.5 %collective-permute-start.2 = (bf16[1024,128]{1,0:T(8,128)(2,1)S(1)}, bf16[1024,128]{1,0:T(8,128)(2,1)S(1)}, u32[]{:S(2)}, u32[]{:S(2)}) collective-permute-start(bf16[1024,128]{1,0:T(8,128)(2,1)S(1)} %bitcast.19), channel_id=1, source_target_pairs={{192,0},{224,32},{0,64},{32,96},{64,128},{96,160},{128,192},{160,2... | collective-permute-start | bytes 786440 | tf_op jit(solution)/shard_map/ppermute | solution.py:204
  45.5 11.7 %collective-permute-start.1 = (bf16[1024,128]{1,0:T(8,128)(2,1)S(1)}, bf16[1024,128]{1,0:T(8,128)(2,1)S(1)}, u32[]{:S(2)}, u32[]{:S(2)}) collective-permute-start(bf16[1024,128]{1,0:T(8,128)(2,1)S(1)} %collective-permute-done), channel_id=1, source_target_pairs={{64,0},{96,32},{128,64},{160,96},{192,128},{224,160},{0,192},{32,2... | collective-permute-start | bytes 786440 | tf_op jit(solution)/shard_map/ppermute | solution.py:204
  57.4 36.3 %collective-permute-start.3 = (bf16[4,1024,128]{2,1,0:T(8,128)(2,1)S(1)}, bf16[4,1024,128]{2,1,0:T(8,128)(2,1)}, u32[]{:S(2)}, u32[]{:S(2)}) collective-permute-start(bf16[4,1024,128]{2,1,0:T(8,128)(2,1)S(1)} %pad_maximum_fusion.mine), channel_id=1, source_target_pairs={{0,32},{32,0},{64,96},{96,64},{128,160},{160,128},{192,224},{224,1... | collective-permute-start | bytes 3145736 | tf_op jit(solution)/shard_map/ppermute | solution.py:211
  59.3 1.0 copy-start.1
  68.6 25.0 %all-to-all-start.2 = ((bf16[512,2,128]{2,1,0:T(2,128)(2,1)}), bf16[512,2,128]{2,1,0:T(2,128)(2,1)S(1)}, u32[]{:S(2)}, u32[]{:S(2)}) async-start(bf16[512,2,128]{2,1,0:T(2,128)(2,1)} %bitcast.9), calls=%async_computation.2 | async-start | bytes 524288 | tf_op jit(solution)/shard_map/all_to_all | solution.py:213
  93.7 1.2 %copy-start.2 = (bf16[4,1024,128]{2,1,0:T(8,128)(2,1)S(1)}, bf16[4,1024,128]{2,1,0:T(8,128)(2,1)}, u32[]{:S(2)}) copy-start(bf16[4,1024,128]{2,1,0:T(8,128)(2,1)} %copy-done.1) | copy-start | bytes 3145732

commit v4 on v3

--- a/solution.py
+++ b/solution.py
@@ -143,29 +143,32 @@
     )
 
 
-def rotate_kernel(n_all, n_x, piece, nz):
-    def body(place, mine, other, rows, out):
-        core, x = place[0], place[1]
-
-        def half(pieces, which):
-            left = jnp.concatenate([pieces[r] for r in range(n_x)], axis=1)
-            right = []
-            for r in range(n_x):
-                q = which * n_x + lax.rem(x + r, n_x)
-                right.append(rows[pl.ds(pl.multiple_of(q * piece, piece), piece), :])
-            right = jnp.concatenate(right, axis=0)
-            return jnp.dot(left, right, preferred_element_type=jnp.float32)
-
-        out[...] = (half(mine, core) + half(other, 1 - core)).astype(jnp.bfloat16)
+def rotate_kernel(n_all, n_x, nz):
+    half, block = n_all // 2, n_all // n_x
+
+    def body(mine, other, rows, out):
+        core, x = chip_place(n_x)
+        near = rows[pl.ds(pl.multiple_of(core * half, half), half), :]
+        far = rows[pl.ds(pl.multiple_of((1 - core) * half, half), half), :]
+        for r in range(n_x):
+            sums = jnp.dot(mine[r], near, preferred_element_type=jnp.float32)
+            sums = sums + jnp.dot(other[r], far, preferred_element_type=jnp.float32)
+            at = pl.multiple_of(lax.rem(x + r, n_x) * block, block)
+            out[pl.ds(at, block), :] = sums.astype(jnp.bfloat16)
 
     vmem = pl.BlockSpec(memory_space=pltpu.VMEM)
     return pl.pallas_call(
         body,
         out_shape=pltpu.VMEM((n_all, nz), jnp.bfloat16),
-        in_specs=[pl.BlockSpec(memory_space=pltpu.SMEM), vmem, vmem, vmem],
+        in_specs=[vmem, vmem, vmem],
         out_specs=vmem,
         name="rotate",
     )
+
+
+def chip_place(n_x):
+    dom = lax.axis_index("dom")
+    return lax.rem(dom, 2), lax.rem(lax.div(dom, 2), n_x)
 
 
 def in_vmem(x):
@@ -179,9 +182,8 @@
     n_all = ritz.shape[0]
     n_own = n_mine // n_dom
     n_x = n_dom // 4
-    dom = lax.axis_index("dom")
-    core = lax.rem(dom, 2)
-    x = lax.rem(lax.div(dom, 2), n_x)
+    n_y = n_band // n_x
+    core, _ = chip_place(n_x)
 
     pot = potential[0]
     high = lax.reduce_precision(pot, 8, 7)
@@ -192,21 +194,35 @@
     blocks = lax.all_to_all(blocks, "dom", 0, 0, tiled=True)
     filtered = filter_kernel(n_dom, n_own, cx, cy, nz)(in_vmem(blocks))
 
-    piece = n_all // (2 * n_x)
-    own = lax.dynamic_slice_in_dim(ritz.T, (core * n_x + x) * piece, piece, 1)
-    many = jnp.broadcast_to(own[None], (n_band,) + own.shape)
+    half = n_all // 2
+
+    def split(d):
+        return d // (2 * n_x), d // 2 % n_x, d % 2
 
     def from_x(value, step):
         pairs = []
         for d in range(n_dom):
-            z, at, c = d // (2 * n_x), d // 2 % n_x, d % 2
-            pairs.append((z * 2 * n_x + (at + step) % n_x * 2 + c, d))
+            z, x, c = split(d)
+            pairs.append((z * 2 * n_x + (x + step) % n_x * 2 + c, d))
         return lax.ppermute(value, "dom", pairs)
 
-    own = lax.all_to_all(many, "band", 0, 0, tiled=True).reshape(n_all, piece)
+    turned = []
+    for d in range(n_dom):
+        z, x, c = split(d)
+        for p in range(n_band):
+            high_z, y = p // n_y, p % n_y
+            source = (z * 2 * n_x + high_z * 2 + c) * n_band + x * n_y + y
+            turned.append((source, d * n_band + p))
+
+    own = lax.dynamic_slice_in_dim(ritz.T, core * half, half, 1)
+    own = lax.ppermute(own, ("dom", "band"), turned)
+    many = jnp.broadcast_to(own[None], (n_y,) + own.shape)
+    lines = [[z * n_y + y for y in range(n_y)] for z in range(n_x)]
+    own = lax.all_to_all(many, "band", 0, 0, tiled=True, axis_index_groups=lines)
+    own = own.reshape(n_y * n_mine, half)
     after = from_x(own, 1)
     before = from_x(own, -1)
-    far = from_x(after, 1)
+    far = from_x(own, 2)
     mine = jnp.stack([own, after, far, before])
     other = lax.ppermute(mine, "dom", [(d, d ^ 1) for d in range(n_dom)])
 
@@ -214,10 +230,7 @@
         filtered.reshape(n_band * n_dom, n_own, nz), ("band", "dom"), 0, 0, tiled=True
     ).reshape(n_all, nz)
 
-    place = jnp.stack([core, x])
-    rotated = rotate_kernel(n_all, n_x, piece, nz)(
-        place, in_vmem(mine), in_vmem(other), in_vmem(rows)
-    )
+    rotated = rotate_kernel(n_all, n_x, nz)(in_vmem(mine), in_vmem(other), in_vmem(rows))
     rotated = lax.all_to_all(rotated.reshape(n_band, n_mine, nz), "band", 0, 0, tiled=True)
     rotated = rotated.transpose(1, 0, 2).astype(jnp.float32)
     return rotated.reshape(orbitals.shape)

time: 119 us -> 123 us (1.034)
  blocking collectives: 19.9 us -> 47.9 us
  waiting for transfers between devices: 38.8 us -> 16.9 us
    all_to_all x0 -> x1, blocking collectives: none -> 27.9 us  [on_device(): lax.all_to_all(filtered.reshape(n_band * n_dom, n_own, nz), ('band', 'dom...]
    all_to_all x2 -> x1, waiting for transfers between devices: 30.4 us -> 7.26 us  [on_device(): lax.all_to_all(many, 'band', 0, 0, tiled=True, axis_index_groups=lines)]
    all_to_all x2 -> x1, starting transfers between devices: 24.9 us -> 9.24 us  [on_device(): lax.all_to_all(many, 'band', 0, 0, tiled=True, axis_index_groups=lines)]
    all_to_all x1, starting transfers between devices: 3.57 us -> 17.9 us  [on_device(): blocks = lax.all_to_all(blocks, 'dom', 0, 0, tiled=True)]
    ppermute x3, waiting for transfers between devices: 8.39 us -> 9.66 us  [from_x(): return lax.ppermute(value, 'dom', pairs)]
  transfers between devices with their start and end apart: 7 -> 7, of which waited for: 3 -> 3; matrix products, arithmetic and copies ran while one was open for 1% -> 1% of each run, Pallas kernels for 7% -> 6%
where the time goes in v4:
time: 123 us
  blocking collectives  47.9 us (39%)
  starting transfers between devices  41.5 us (34%)
  waiting for transfers between devices  16.9 us (14%)
  Pallas kernels  9.5 us (8%)
  local copies, waits for them, and re-layouts  5.81 us (5%)
    all_to_all x1, blocking collectives, on_device(): lax.all_to_all(filtered.reshape(n_band * n_dom, n_own, nz), ('band', 'dom...  27.9 us
    all_to_all x1, blocking collectives, on_device(): lax.all_to_all(rotated.reshape(n_band, n_mine, nz), 'band', 0, 0, tiled=T...  19.9 us
    all_to_all x1, starting transfers between devices, on_device(): blocks = lax.all_to_all(blocks, 'dom', 0, 0, tiled=True)  17.9 us
    ppermute x3, starting transfers between devices, from_x(): return lax.ppermute(value, 'dom', pairs)  11.8 us
    ppermute x3, waiting for transfers between devices, from_x(): return lax.ppermute(value, 'dom', pairs)  9.66 us
    all_to_all x1, starting transfers between devices, on_device(): lax.all_to_all(many, 'band', 0, 0, tiled=True, axis_index_groups=lines)  9.24 us
    pallas_call x1, Pallas kernels, on_device(): filtered = filter_kernel(n_dom, n_own, cx, cy, nz)(in_vmem(blocks))  7.58 us
    all_to_all x1, waiting for transfers between devices, on_device(): lax.all_to_all(many, 'band', 0, 0, tiled=True, axis_index_groups=lines)  7.26 us
  transfers between devices with their start and end apart: 7, of which 3 were waited for; matrix products, arithmetic and copies ran while one was open for 1% of the time, Pallas kernels for 6%

profile of v4, /device:TPU:8, one launch (start us, length us, event | category | flops | bytes accessed | tf_op | source)
XLA Modules:
  0.0 122.7 jit_solution(15928837519816913032)
XLA Ops:
  0.0 0.0 copy-start
  0.0 0.8 copy-done
  0.8 0.7 collective-permute-start
  1.5 0.0 collective-permute-done
  1.5 0.7 broadcast_in_dim.4
  2.2 0.0 copy-start.4
  2.2 9.2 %all-to-all-start = ((bf16[8,32,512]{2,1,0:T(8,128)(2,1)}), bf16[8,32,512]{2,1,0:T(8,128)(2,1)S(1)}, u32[]{:S(2)}, u32[]{:S(2)}) async-start(bf16[8,32,512]{2,1,0:T(8,128)(2,1)} %broadcast_in_dim.4), calls=%async_computation | async-start | bytes 524288 | tf_op jit(solution)/shard_map/all_to_all | solution.py:221
  11.5 0.0 copy-done.4
  11.5 0.0 copy-start.3
  11.6 0.9 copy-done.3
  12.4 0.8 pad_maximum_fusion.1
  13.3 7.3 %all-to-all-done = bf16[8,32,512]{2,1,0:T(8,128)(2,1)S(1)} async-done(((bf16[8,32,512]{2,1,0:T(8,128)(2,1)}), bf16[8,32,512]{2,1,0:T(8,128)(2,1)S(1)}, u32[]{:S(2)}, u32[]{:S(2)}) %all-to-all-start) | async-done | bytes 262176 | tf_op jit(solution)/shard_map/all_to_all | solution.py:221
  20.5 17.9 %all-to-all-start.1 = ((bf16[16,4,2,16,128]{4,3,2,1,0:T(8,128)(2,1)}), bf16[16,4,2,16,128]{4,3,2,1,0:T(8,128)(2,1)S(1)}, u32[]{:S(2)}, u32[]{:S(2)}) async-start(bf16[16,4,2,16,128]{4,3,2,1,0:T(8,128)(2,1)} %pad_maximum_fusion.1), calls=%async_computation.1 | async-start | bytes 1048576 | tf_op jit(solution)/shard_map/all_to_all | solution.py:194
  38.5 3.8 %collective-permute-start.3 = (bf16[256,512]{1,0:T(8,128)(2,1)S(1)}, bf16[256,512]{1,0:T(8,128)(2,1)S(1)}, u32[]{:S(2)}, u32[]{:S(2)}) collective-permute-start(bf16[256,512]{1,0:T(8,128)(2,1)S(1)} %bitcast.17), channel_id=1, source_target_pairs={{192,0},{224,32},{0,64},{32,96},{64,128},{96,160},{128,192},{160,2... | collective-permute-start | bytes 786440 | tf_op jit(solution)/shard_map/ppermute | solution.py:207
  42.3 4.6 %collective-permute-start.2 = (bf16[256,512]{1,0:T(8,128)(2,1)S(1)}, bf16[256,512]{1,0:T(8,128)(2,1)S(1)}, u32[]{:S(2)}, u32[]{:S(2)}) collective-permute-start(bf16[256,512]{1,0:T(8,128)(2,1)S(1)} %bitcast.18), channel_id=1, source_target_pairs={{128,0},{160,32},{192,64},{224,96},{0,128},{32,160},{64,192},{96,2... | collective-permute-start | bytes 786440 | tf_op jit(solution)/shard_map/ppermute | solution.py:207
  46.9 3.4 %collective-permute-start.1 = (bf16[256,512]{1,0:T(8,128)(2,1)S(1)}, bf16[256,512]{1,0:T(8,128)(2,1)S(1)}, u32[]{:S(2)}, u32[]{:S(2)}) collective-permute-start(bf16[256,512]{1,0:T(8,128)(2,1)S(1)} %bitcast.19), channel_id=1, source_target_pairs={{64,0},{96,32},{128,64},{160,96},{192,128},{224,160},{0,192},{32,2... | collective-permute-start | bytes 786440 | tf_op jit(solution)/shard_map/ppermute | solution.py:207
  50.3 4.0 %collective-permute-done.3 = bf16[256,512]{1,0:T(8,128)(2,1)S(1)} collective-permute-done((bf16[256,512]{1,0:T(8,128)(2,1)S(1)}, bf16[256,512]{1,0:T(8,128)(2,1)S(1)}, u32[]{:S(2)}, u32[]{:S(2)}) %collective-permute-start.3) | collective-permute-done | bytes 262176 | tf_op jit(solution)/shard_map/ppermute | solution.py:207
  54.3 5.6 %collective-permute-done.2 = bf16[256,512]{1,0:T(8,128)(2,1)S(1)} collective-permute-done((bf16[256,512]{1,0:T(8,128)(2,1)S(1)}, bf16[256,512]{1,0:T(8,128)(2,1)S(1)}, u32[]{:S(2)}, u32[]{:S(2)}) %collective-permute-start.2) | collective-permute-done | bytes 262176 | tf_op jit(solution)/shard_map/ppermute | solution.py:207
  59.9 0.0 collective-permute-done.1
  59.9 0.1 pad_maximum_fusion.mine
  60.0 1.9 %collective-permute-start.4 = (bf16[4,256,512]{2,1,0:T(8,128)(2,1)S(1)}, bf16[4,256,512]{2,1,0:T(8,128)(2,1)}, u32[]{:S(2)}, u32[]{:S(2)}) collective-permute-start(bf16[4,256,512]{2,1,0:T(8,128)(2,1)S(1)} %pad_maximum_fusion.mine), channel_id=1, source_target_pairs={{0,32},{32,0},{64,96},{96,64},{128,160},{160,128},{192,224},{224,1... | collective-permute-start | bytes 3145736 | tf_op jit(solution)/shard_map/ppermute | solution.py:227
  62.0 0.0 copy-start.1
  62.0 1.0 copy-done.1
  63.0 0.0 all-to-all-done.1.blocks
  63.0 7.6 %chebyshev.1 = bf16[1024,128]{1,0:T(8,128)(2,1)S(1)} custom-call(bf16[16,4,2,16,128]{4,3,2,1,0:T(8,128)(2,1)S(1)} %all-to-all-done.1.blocks), custom_call_target="tpu_custom_call" | custom-call | tf_op jit(solution)/shard_map/chebyshev/pallas_call | solution.py:195
  70.6 27.9 %all_to_all.20 = bf16[512,2,128]{2,1,0:T(2,128)(2,1)S(1)} all-to-all(bf16[512,2,128]{2,1,0:T(2,128)(2,1)S(1)} %bitcast.16), channel_id=1, replica_groups=mesh['dom'=16,'band'=32] {'band','dom'}, dimensions={0} | all-to-all | bytes 524288 | tf_op jit(solution)/shard_map/all_to_all | solution.py:229
  98.5 0.0 collective-permute-done.4.other
  98.5 0.0 copy-start.2
  98.5 1.2 copy-done.2
  99.7 1.9 %rotate.1 = bf16[1024,128]{1,0:T(8,128)(2,1)S(1)} custom-call(bf16[4,256,512]{2,1,0:T(8,128)(2,1)S(1)} %copy-done.2, bf16[4,256,512]{2,1,0:T(8,128)(2,1)} %collective-permute-done.4.other, bf16[1024,128]{1,0:T(8,128)(2,1)S(1)} %bitcast.14), custom_call_target="tpu_custom_call" | custom-call | tf_op jit(solution)/shard_map/rotate/pallas_call | solution.py:233
  101.7 19.9 %all_to_all.21 = bf16[32,32,128]{2,1,0:T(8,128)(2,1)S(1)} all-to-all(bf16[32,32,128]{2,1,0:T(8,128)(2,1)S(1)} %bitcast.15), channel_id=1, replica_groups=mesh['dom'=16,'band'=32] {'band'}, dimensions={0} | all-to-all | bytes 524288 | tf_op jit(solution)/shard_map/all_to_all | solution.py:234
  121.6 0.1 convert_bitcast_fusion
  121.6 1.1 copy.4
  (4 shorter events, 0.1 us)
Async XLA Ops:
  0.0 0.8 copy-start
  0.8 0.7 collective-permute-start
  2.2 9.2 %copy-start.4 = (f32[1,2,16,128]{3,2,1,0:T(8,128)S(1)}, f32[1,2,16,128]{3,2,1,0:T(8,128)}, u32[]{:S(2)}) copy-start(f32[1,2,16,128]{3,2,1,0:T(8,128)} %param.4) | copy-start | bytes 49156
  2.2 18.3 %all-to-all-start = ((bf16[8,32,512]{2,1,0:T(8,128)(2,1)}), bf16[8,32,512]{2,1,0:T(8,128)(2,1)S(1)}, u32[]{:S(2)}, u32[]{:S(2)}) async-start(bf16[8,32,512]{2,1,0:T(8,128)(2,1)} %broadcast_in_dim.4), calls=%async_computation | async-start | bytes 524288 | tf_op jit(solution)/shard_map/all_to_all | solution.py:221
  11.5 1.0 copy-start.3
  20.5 42.4 %all-to-all-start.1 = ((bf16[16,4,2,16,128]{4,3,2,1,0:T(8,128)(2,1)}), bf16[16,4,2,16,128]{4,3,2,1,0:T(8,128)(2,1)S(1)}, u32[]{:S(2)}, u32[]{:S(2)}) async-start(bf16[16,4,2,16,128]{4,3,2,1,0:T(8,128)(2,1)} %pad_maximum_fusion.1), calls=%async_computation.1 | async-start | bytes 1048576 | tf_op jit(solution)/shard_map/all_to_all | solution.py:194
  38.5 15.8 %collective-permute-start.3 = (bf16[256,512]{1,0:T(8,128)(2,1)S(1)}, bf16[256,512]{1,0:T(8,128)(2,1)S(1)}, u32[]{:S(2)}, u32[]{:S(2)}) collective-permute-start(bf16[256,512]{1,0:T(8,128)(2,1)S(1)} %bitcast.17), channel_id=1, source_target_pairs={{192,0},{224,32},{0,64},{32,96},{64,128},{96,160},{128,192},{160,2... | collective-permute-start | bytes 786440 | tf_op jit(solution)/shard_map/ppermute | solution.py:207
  42.3 17.6 %collective-permute-start.2 = (bf16[256,512]{1,0:T(8,128)(2,1)S(1)}, bf16[256,512]{1,0:T(8,128)(2,1)S(1)}, u32[]{:S(2)}, u32[]{:S(2)}) collective-permute-start(bf16[256,512]{1,0:T(8,128)(2,1)S(1)} %bitcast.18), channel_id=1, source_target_pairs={{128,0},{160,32},{192,64},{224,96},{0,128},{32,160},{64,192},{96,2... | collective-permute-start | bytes 786440 | tf_op jit(solution)/shard_map/ppermute | solution.py:207
  46.9 13.0 %collective-permute-start.1 = (bf16[256,512]{1,0:T(8,128)(2,1)S(1)}, bf16[256,512]{1,0:T(8,128)(2,1)S(1)}, u32[]{:S(2)}, u32[]{:S(2)}) collective-permute-start(bf16[256,512]{1,0:T(8,128)(2,1)S(1)} %bitcast.19), channel_id=1, source_target_pairs={{64,0},{96,32},{128,64},{160,96},{192,128},{224,160},{0,192},{32,2... | collective-permute-start | bytes 786440 | tf_op jit(solution)/shard_map/ppermute | solution.py:207
  60.0 38.5 %collective-permute-start.4 = (bf16[4,256,512]{2,1,0:T(8,128)(2,1)S(1)}, bf16[4,256,512]{2,1,0:T(8,128)(2,1)}, u32[]{:S(2)}, u32[]{:S(2)}) collective-permute-start(bf16[4,256,512]{2,1,0:T(8,128)(2,1)S(1)} %pad_maximum_fusion.mine), channel_id=1, source_target_pairs={{0,32},{32,0},{64,96},{96,64},{128,160},{160,128},{192,224},{224,1... | collective-permute-start | bytes 3145736 | tf_op jit(solution)/shard_map/ppermute | solution.py:227
  62.0 1.0 copy-start.1
  98.5 1.2 copy-start.2

commit v5 on v3

--- a/solution.py
+++ b/solution.py
@@ -143,29 +143,37 @@
     )
 
 
-def rotate_kernel(n_all, n_x, piece, nz):
-    def body(place, mine, other, rows, out):
-        core, x = place[0], place[1]
-
-        def half(pieces, which):
-            left = jnp.concatenate([pieces[r] for r in range(n_x)], axis=1)
-            right = []
+def rotate_kernel(n_all, n_x, nz):
+    piece = n_all // (2 * n_x)
+    block = 256
+
+    def body(mine, other, rows, out):
+        core, x = chip_place(n_x)
+        right = []
+        for which in (core, 1 - core):
             for r in range(n_x):
                 q = which * n_x + lax.rem(x + r, n_x)
                 right.append(rows[pl.ds(pl.multiple_of(q * piece, piece), piece), :])
-            right = jnp.concatenate(right, axis=0)
-            return jnp.dot(left, right, preferred_element_type=jnp.float32)
-
-        out[...] = (half(mine, core) + half(other, 1 - core)).astype(jnp.bfloat16)
+        right = jnp.concatenate(right, axis=0)
+        for at in range(0, n_all, block):
+            left = [p[r, at : at + block, :] for p in (mine, other) for r in range(n_x)]
+            left = jnp.concatenate(left, axis=1)
+            sums = jnp.dot(left, right, preferred_element_type=jnp.float32)
+            out[at : at + block, :] = sums.astype(jnp.bfloat16)
 
     vmem = pl.BlockSpec(memory_space=pltpu.VMEM)
     return pl.pallas_call(
         body,
         out_shape=pltpu.VMEM((n_all, nz), jnp.bfloat16),
-        in_specs=[pl.BlockSpec(memory_space=pltpu.SMEM), vmem, vmem, vmem],
+        in_specs=[vmem, vmem, vmem],
         out_specs=vmem,
         name="rotate",
     )
+
+
+def chip_place(n_x):
+    dom = lax.axis_index("dom")
+    return lax.rem(dom, 2), lax.rem(lax.div(dom, 2), n_x)
 
 
 def in_vmem(x):
@@ -179,9 +187,7 @@
     n_all = ritz.shape[0]
     n_own = n_mine // n_dom
     n_x = n_dom // 4
-    dom = lax.axis_index("dom")
-    core = lax.rem(dom, 2)
-    x = lax.rem(lax.div(dom, 2), n_x)
+    core, x = chip_place(n_x)
 
     pot = potential[0]
     high = lax.reduce_precision(pot, 8, 7)
@@ -206,7 +212,7 @@
     own = lax.all_to_all(many, "band", 0, 0, tiled=True).reshape(n_all, piece)
     after = from_x(own, 1)
     before = from_x(own, -1)
-    far = from_x(after, 1)
+    far = from_x(own, 2)
     mine = jnp.stack([own, after, far, before])
     other = lax.ppermute(mine, "dom", [(d, d ^ 1) for d in range(n_dom)])
 
@@ -214,10 +220,7 @@
         filtered.reshape(n_band * n_dom, n_own, nz), ("band", "dom"), 0, 0, tiled=True
     ).reshape(n_all, nz)
 
-    place = jnp.stack([core, x])
-    rotated = rotate_kernel(n_all, n_x, piece, nz)(
-        place, in_vmem(mine), in_vmem(other), in_vmem(rows)
-    )
+    rotated = rotate_kernel(n_all, n_x, nz)(in_vmem(mine), in_vmem(other), in_vmem(rows))
     rotated = lax.all_to_all(rotated.reshape(n_band, n_mine, nz), "band", 0, 0, tiled=True)
     rotated = rotated.transpose(1, 0, 2).astype(jnp.float32)
     return rotated.reshape(orbitals.shape)

time: 119 us -> 120 us (level)
  blocking collectives: 19.9 us -> 45.4 us
  waiting for transfers between devices: 38.8 us -> 22.6 us
  starting transfers between devices: 42.1 us -> 35.3 us
    all_to_all x0 -> x1, blocking collectives: none -> 25.5 us  [on_device(): lax.all_to_all(filtered.reshape(n_band * n_dom, n_own, nz), ('band', 'dom...]
    all_to_all x1 -> x0, waiting for transfers between devices: 15.7 us -> none  [on_device(): lax.all_to_all(filtered.reshape(n_band * n_dom, n_own, nz), ('band', 'dom...]
    all_to_all x1 -> x0, starting transfers between devices: 8.64 us -> none  [on_device(): lax.all_to_all(filtered.reshape(n_band * n_dom, n_own, nz), ('band', 'dom...]
    all_to_all x1, waiting for transfers between devices: 14.7 us -> 13 us  [on_device(): own = lax.all_to_all(many, 'band', 0, 0, tiled=True).reshape(n_all, piece)]
    all_to_all x1, starting transfers between devices: 3.57 us -> 5.28 us  [on_device(): blocks = lax.all_to_all(blocks, 'dom', 0, 0, tiled=True)]
    ppermute x3, waiting for transfers between devices: 8.39 us -> 9.66 us  [from_x(): return lax.ppermute(value, 'dom', pairs)]
  transfers between devices with their start and end apart: 7 -> 6, of which waited for: 3 -> 3; matrix products, arithmetic and copies ran while one was open for 1% -> 1% of each run, Pallas kernels for 7% -> 6%
where the time goes in v5:
time: 120 us
  blocking collectives  45.4 us (38%)
  starting transfers between devices  35.3 us (29%)
  waiting for transfers between devices  22.6 us (19%)
  Pallas kernels  9.51 us (8%)
  local copies, waits for them, and re-layouts  5.81 us (5%)
    all_to_all x1, blocking collectives, on_device(): lax.all_to_all(filtered.reshape(n_band * n_dom, n_own, nz), ('band', 'dom...  25.5 us
    all_to_all x1, blocking collectives, on_device(): lax.all_to_all(rotated.reshape(n_band, n_mine, nz), 'band', 0, 0, tiled=T...  19.9 us
    all_to_all x1, starting transfers between devices, on_device(): own = lax.all_to_all(many, 'band', 0, 0, tiled=True).reshape(n_all, piece)  16.3 us
    all_to_all x1, waiting for transfers between devices, on_device(): own = lax.all_to_all(many, 'band', 0, 0, tiled=True).reshape(n_all, piece)  13 us
    ppermute x3, starting transfers between devices, from_x(): return lax.ppermute(value, 'dom', pairs)  11.8 us
    ppermute x3, waiting for transfers between devices, from_x(): return lax.ppermute(value, 'dom', pairs)  9.66 us
    pallas_call x1, Pallas kernels, on_device(): filtered = filter_kernel(n_dom, n_own, cx, cy, nz)(in_vmem(blocks))  7.58 us
    all_to_all x1, starting transfers between devices, on_device(): blocks = lax.all_to_all(blocks, 'dom', 0, 0, tiled=True)  5.28 us
  transfers between devices with their start and end apart: 6, of which 3 were waited for; matrix products, arithmetic and copies ran while one was open for 1% of the time, Pallas kernels for 6%

profile of v5, /device:TPU:8, one launch (start us, length us, event | category | flops | bytes accessed | tf_op | source)
XLA Modules:
  0.0 119.8 jit_solution(12387983150050945240)
XLA Ops:
  0.0 0.0 copy-start
  0.0 0.8 copy-done
  0.8 0.7 broadcast_in_dim.4
  1.6 0.0 copy-start.4
  1.6 16.3 %all-to-all-start = ((bf16[32,32,128]{2,1,0:T(8,128)(2,1)}), bf16[32,32,128]{2,1,0:T(8,128)(2,1)S(1)}, u32[]{:S(2)}, u32[]{:S(2)}) async-start(bf16[32,32,128]{2,1,0:T(8,128)(2,1)} %broadcast_in_dim.4), calls=%async_computation | async-start | bytes 524288 | tf_op jit(solution)/shard_map/all_to_all | solution.py:212
  17.9 0.0 copy-done.4
  17.9 0.0 copy-start.3
  18.0 0.9 copy-done.3
  18.9 0.8 pad_maximum_fusion.1
  19.7 13.0 %all-to-all-done = bf16[32,32,128]{2,1,0:T(8,128)(2,1)S(1)} async-done(((bf16[32,32,128]{2,1,0:T(8,128)(2,1)}), bf16[32,32,128]{2,1,0:T(8,128)(2,1)S(1)}, u32[]{:S(2)}, u32[]{:S(2)}) %all-to-all-start) | async-done | bytes 262176 | tf_op jit(solution)/shard_map/all_to_all | solution.py:212
  32.6 5.3 %all-to-all-start.1 = ((bf16[16,4,2,16,128]{4,3,2,1,0:T(8,128)(2,1)}), bf16[16,4,2,16,128]{4,3,2,1,0:T(8,128)(2,1)S(1)}, u32[]{:S(2)}, u32[]{:S(2)}) async-start(bf16[16,4,2,16,128]{4,3,2,1,0:T(8,128)(2,1)} %pad_maximum_fusion.1), calls=%async_computation.1 | async-start | bytes 1048576 | tf_op jit(solution)/shard_map/all_to_all | solution.py:198
  37.9 3.8 %collective-permute-start.2 = (bf16[1024,128]{1,0:T(8,128)(2,1)S(1)}, bf16[1024,128]{1,0:T(8,128)(2,1)S(1)}, u32[]{:S(2)}, u32[]{:S(2)}) collective-permute-start(bf16[1024,128]{1,0:T(8,128)(2,1)S(1)} %bitcast.17), channel_id=1, source_target_pairs={{192,0},{224,32},{0,64},{32,96},{64,128},{96,160},{128,192},{160,2... | collective-permute-start | bytes 786440 | tf_op jit(solution)/shard_map/ppermute | solution.py:210
  41.8 4.6 %collective-permute-start.1 = (bf16[1024,128]{1,0:T(8,128)(2,1)S(1)}, bf16[1024,128]{1,0:T(8,128)(2,1)S(1)}, u32[]{:S(2)}, u32[]{:S(2)}) collective-permute-start(bf16[1024,128]{1,0:T(8,128)(2,1)S(1)} %bitcast.18), channel_id=1, source_target_pairs={{128,0},{160,32},{192,64},{224,96},{0,128},{32,160},{64,192},{96,2... | collective-permute-start | bytes 786440 | tf_op jit(solution)/shard_map/ppermute | solution.py:210
  46.4 3.4 %collective-permute-start = (bf16[1024,128]{1,0:T(8,128)(2,1)S(1)}, bf16[1024,128]{1,0:T(8,128)(2,1)S(1)}, u32[]{:S(2)}, u32[]{:S(2)}) collective-permute-start(bf16[1024,128]{1,0:T(8,128)(2,1)S(1)} %bitcast.19), channel_id=1, source_target_pairs={{64,0},{96,32},{128,64},{160,96},{192,128},{224,160},{0,192},{32,2... | collective-permute-start | bytes 786440 | tf_op jit(solution)/shard_map/ppermute | solution.py:210
  49.7 4.0 %collective-permute-done.2 = bf16[1024,128]{1,0:T(8,128)(2,1)S(1)} collective-permute-done((bf16[1024,128]{1,0:T(8,128)(2,1)S(1)}, bf16[1024,128]{1,0:T(8,128)(2,1)S(1)}, u32[]{:S(2)}, u32[]{:S(2)}) %collective-permute-start.2) | collective-permute-done | bytes 262176 | tf_op jit(solution)/shard_map/ppermute | solution.py:210
  53.8 5.6 %collective-permute-done.1 = bf16[1024,128]{1,0:T(8,128)(2,1)S(1)} collective-permute-done((bf16[1024,128]{1,0:T(8,128)(2,1)S(1)}, bf16[1024,128]{1,0:T(8,128)(2,1)S(1)}, u32[]{:S(2)}, u32[]{:S(2)}) %collective-permute-start.1) | collective-permute-done | bytes 262176 | tf_op jit(solution)/shard_map/ppermute | solution.py:210
  59.4 0.0 collective-permute-done
  59.4 0.1 pad_maximum_fusion.mine
  59.5 1.9 %collective-permute-start.3 = (bf16[4,1024,128]{2,1,0:T(8,128)(2,1)S(1)}, bf16[4,1024,128]{2,1,0:T(8,128)(2,1)}, u32[]{:S(2)}, u32[]{:S(2)}) collective-permute-start(bf16[4,1024,128]{2,1,0:T(8,128)(2,1)S(1)} %pad_maximum_fusion.mine), channel_id=1, source_target_pairs={{0,32},{32,0},{64,96},{96,64},{128,160},{160,128},{192,224},{224,1... | collective-permute-start | bytes 3145736 | tf_op jit(solution)/shard_map/ppermute | solution.py:217
  61.5 0.0 copy-start.1
  61.5 1.0 copy-done.1
  62.5 0.0 all-to-all-done.1.blocks
  62.5 7.6 %chebyshev.1 = bf16[1024,128]{1,0:T(8,128)(2,1)S(1)} custom-call(bf16[16,4,2,16,128]{4,3,2,1,0:T(8,128)(2,1)S(1)} %all-to-all-done.1.blocks), custom_call_target="tpu_custom_call" | custom-call | tf_op jit(solution)/shard_map/chebyshev/pallas_call | solution.py:199
  70.1 25.5 %all_to_all.20 = bf16[512,2,128]{2,1,0:T(2,128)(2,1)S(1)} all-to-all(bf16[512,2,128]{2,1,0:T(2,128)(2,1)S(1)} %bitcast.16), channel_id=1, replica_groups=mesh['dom'=16,'band'=32] {'band','dom'}, dimensions={0} | all-to-all | bytes 524288 | tf_op jit(solution)/shard_map/all_to_all | solution.py:219
  95.5 0.0 collective-permute-done.3.other
  95.5 0.0 copy-start.2
  95.5 1.2 %copy-done.2 = bf16[4,1024,128]{2,1,0:T(8,128)(2,1)S(1)} copy-done((bf16[4,1024,128]{2,1,0:T(8,128)(2,1)S(1)}, bf16[4,1024,128]{2,1,0:T(8,128)(2,1)}, u32[]{:S(2)}) %copy-start.2) | copy-done | bytes 1048600
  96.7 1.9 %rotate.1 = bf16[1024,128]{1,0:T(8,128)(2,1)S(1)} custom-call(bf16[4,1024,128]{2,1,0:T(8,128)(2,1)S(1)} %copy-done.2, bf16[4,1024,128]{2,1,0:T(8,128)(2,1)} %collective-permute-done.3.other, bf16[1024,128]{1,0:T(8,128)(2,1)S(1)} %bitcast.14), custom_call_target="tpu_custom_call" | custom-call | tf_op jit(solution)/shard_map/rotate/pallas_call | solution.py:223
  98.7 19.9 %all_to_all.21 = bf16[32,32,128]{2,1,0:T(8,128)(2,1)S(1)} all-to-all(bf16[32,32,128]{2,1,0:T(8,128)(2,1)S(1)} %bitcast.15), channel_id=1, replica_groups=mesh['dom'=16,'band'=32] {'band'}, dimensions={0} | all-to-all | bytes 524288 | tf_op jit(solution)/shard_map/all_to_all | solution.py:224
  118.6 0.1 convert_bitcast_fusion
  118.7 1.1 copy.4
  (4 shorter events, 0.1 us)
Async XLA Ops:
  0.0 0.8 copy-start
  1.6 16.3 %copy-start.4 = (f32[1,2,16,128]{3,2,1,0:T(8,128)S(1)}, f32[1,2,16,128]{3,2,1,0:T(8,128)}, u32[]{:S(2)}) copy-start(f32[1,2,16,128]{3,2,1,0:T(8,128)} %param.4) | copy-start | bytes 49156
  1.6 31.1 %all-to-all-start = ((bf16[32,32,128]{2,1,0:T(8,128)(2,1)}), bf16[32,32,128]{2,1,0:T(8,128)(2,1)S(1)}, u32[]{:S(2)}, u32[]{:S(2)}) async-start(bf16[32,32,128]{2,1,0:T(8,128)(2,1)} %broadcast_in_dim.4), calls=%async_computation | async-start | bytes 524288 | tf_op jit(solution)/shard_map/all_to_all | solution.py:212
  17.9 1.0 copy-start.3
  32.6 29.8 %all-to-all-start.1 = ((bf16[16,4,2,16,128]{4,3,2,1,0:T(8,128)(2,1)}), bf16[16,4,2,16,128]{4,3,2,1,0:T(8,128)(2,1)S(1)}, u32[]{:S(2)}, u32[]{:S(2)}) async-start(bf16[16,4,2,16,128]{4,3,2,1,0:T(8,128)(2,1)} %pad_maximum_fusion.1), calls=%async_computation.1 | async-start | bytes 1048576 | tf_op jit(solution)/shard_map/all_to_all | solution.py:198
  37.9 15.8 %collective-permute-start.2 = (bf16[1024,128]{1,0:T(8,128)(2,1)S(1)}, bf16[1024,128]{1,0:T(8,128)(2,1)S(1)}, u32[]{:S(2)}, u32[]{:S(2)}) collective-permute-start(bf16[1024,128]{1,0:T(8,128)(2,1)S(1)} %bitcast.17), channel_id=1, source_target_pairs={{192,0},{224,32},{0,64},{32,96},{64,128},{96,160},{128,192},{160,2... | collective-permute-start | bytes 786440 | tf_op jit(solution)/shard_map/ppermute | solution.py:210
  41.8 17.6 %collective-permute-start.1 = (bf16[1024,128]{1,0:T(8,128)(2,1)S(1)}, bf16[1024,128]{1,0:T(8,128)(2,1)S(1)}, u32[]{:S(2)}, u32[]{:S(2)}) collective-permute-start(bf16[1024,128]{1,0:T(8,128)(2,1)S(1)} %bitcast.18), channel_id=1, source_target_pairs={{128,0},{160,32},{192,64},{224,96},{0,128},{32,160},{64,192},{96,2... | collective-permute-start | bytes 786440 | tf_op jit(solution)/shard_map/ppermute | solution.py:210
  46.4 13.0 %collective-permute-start = (bf16[1024,128]{1,0:T(8,128)(2,1)S(1)}, bf16[1024,128]{1,0:T(8,128)(2,1)S(1)}, u32[]{:S(2)}, u32[]{:S(2)}) collective-permute-start(bf16[1024,128]{1,0:T(8,128)(2,1)S(1)} %bitcast.19), channel_id=1, source_target_pairs={{64,0},{96,32},{128,64},{160,96},{192,128},{224,160},{0,192},{32,2... | collective-permute-start | bytes 786440 | tf_op jit(solution)/shard_map/ppermute | solution.py:210
  59.5 36.0 %collective-permute-start.3 = (bf16[4,1024,128]{2,1,0:T(8,128)(2,1)S(1)}, bf16[4,1024,128]{2,1,0:T(8,128)(2,1)}, u32[]{:S(2)}, u32[]{:S(2)}) collective-permute-start(bf16[4,1024,128]{2,1,0:T(8,128)(2,1)S(1)} %pad_maximum_fusion.mine), channel_id=1, source_target_pairs={{0,32},{32,0},{64,96},{96,64},{128,160},{160,128},{192,224},{224,1... | collective-permute-start | bytes 3145736 | tf_op jit(solution)/shard_map/ppermute | solution.py:217
  61.5 1.0 copy-start.1
  95.5 1.2 %copy-start.2 = (bf16[4,1024,128]{2,1,0:T(8,128)(2,1)S(1)}, bf16[4,1024,128]{2,1,0:T(8,128)(2,1)}, u32[]{:S(2)}) copy-start(bf16[4,1024,128]{2,1,0:T(8,128)(2,1)} %copy-done.1) | copy-start | bytes 3145732

commit v6 on v4

--- a/solution.py
+++ b/solution.py
@@ -148,12 +148,13 @@
 
     def body(mine, other, rows, out):
         core, x = chip_place(n_x)
+        first = lax.div(lax.axis_index("band"), lax.axis_size("band") // n_x) + x
         near = rows[pl.ds(pl.multiple_of(core * half, half), half), :]
         far = rows[pl.ds(pl.multiple_of((1 - core) * half, half), half), :]
         for r in range(n_x):
             sums = jnp.dot(mine[r], near, preferred_element_type=jnp.float32)
             sums = sums + jnp.dot(other[r], far, preferred_element_type=jnp.float32)
-            at = pl.multiple_of(lax.rem(x + r, n_x) * block, block)
+            at = pl.multiple_of(lax.rem(first + r, n_x) * block, block)
             out[pl.ds(at, block), :] = sums.astype(jnp.bfloat16)
 
     vmem = pl.BlockSpec(memory_space=pltpu.VMEM)
@@ -211,7 +212,8 @@
         z, x, c = split(d)
         for p in range(n_band):
             high_z, y = p // n_y, p % n_y
-            source = (z * 2 * n_x + high_z * 2 + c) * n_band + x * n_y + y
+            near_z = 1 - z if x == 2 else z
+            source = (near_z * 2 * n_x + x * 2 + c) * n_band + (high_z + x) % n_x * n_y + y
             turned.append((source, d * n_band + p))
 
     own = lax.dynamic_slice_in_dim(ritz.T, core * half, half, 1)

time: 123 us -> 122 us (level)
  starting transfers between devices: 41.5 us -> 40.1 us
    all_to_all x1, starting transfers between devices: 17.9 us -> 16.5 us  [on_device(): blocks = lax.all_to_all(blocks, 'dom', 0, 0, tiled=True)]
where the time goes in v6:
time: 122 us; the launch traced here: 121 us
  blocking collectives  47.5 us (39%)
  starting transfers between devices  40.1 us (33%)
  waiting for transfers between devices  16.9 us (14%)
  Pallas kernels  9.5 us (8%)
  local copies, waits for them, and re-layouts  5.81 us (5%)
    all_to_all x1, blocking collectives, on_device(): lax.all_to_all(filtered.reshape(n_band * n_dom, n_own, nz), ('band', 'dom...  27.6 us
    all_to_all x1, blocking collectives, on_device(): lax.all_to_all(rotated.reshape(n_band, n_mine, nz), 'band', 0, 0, tiled=T...  19.9 us
    all_to_all x1, starting transfers between devices, on_device(): blocks = lax.all_to_all(blocks, 'dom', 0, 0, tiled=True)  16.5 us
    ppermute x3, starting transfers between devices, from_x(): return lax.ppermute(value, 'dom', pairs)  11.8 us
    ppermute x3, waiting for transfers between devices, from_x(): return lax.ppermute(value, 'dom', pairs)  9.66 us
    all_to_all x1, starting transfers between devices, on_device(): lax.all_to_all(many, 'band', 0, 0, tiled=True, axis_index_groups=lines)  9.24 us
    pallas_call x1, Pallas kernels, on_device(): filtered = filter_kernel(n_dom, n_own, cx, cy, nz)(in_vmem(blocks))  7.58 us
    all_to_all x1, waiting for transfers between devices, on_device(): lax.all_to_all(many, 'band', 0, 0, tiled=True, axis_index_groups=lines)  7.26 us
  transfers between devices with their start and end apart: 7, of which 3 were waited for; matrix products, arithmetic and copies ran while one was open for 1% of the time, Pallas kernels for 6%

profile of v6, /device:TPU:8, one launch (start us, length us, event | category | flops | bytes accessed | tf_op | source)
XLA Modules:
  0.0 121.0 jit_solution(4328177990889893154)
XLA Ops:
  0.0 0.0 copy-start
  0.0 0.8 copy-done
  0.8 0.7 collective-permute-start
  1.5 0.0 collective-permute-done
  1.5 0.7 broadcast_in_dim.4
  2.2 0.0 copy-start.4
  2.2 9.2 %all-to-all-start = ((bf16[8,32,512]{2,1,0:T(8,128)(2,1)}), bf16[8,32,512]{2,1,0:T(8,128)(2,1)S(1)}, u32[]{:S(2)}, u32[]{:S(2)}) async-start(bf16[8,32,512]{2,1,0:T(8,128)(2,1)} %broadcast_in_dim.4), calls=%async_computation | async-start | bytes 524288 | tf_op jit(solution)/shard_map/all_to_all | solution.py:223
  11.5 0.0 copy-done.4
  11.5 0.0 copy-start.3
  11.6 0.9 copy-done.3
  12.4 0.8 pad_maximum_fusion.1
  13.3 7.3 %all-to-all-done = bf16[8,32,512]{2,1,0:T(8,128)(2,1)S(1)} async-done(((bf16[8,32,512]{2,1,0:T(8,128)(2,1)}), bf16[8,32,512]{2,1,0:T(8,128)(2,1)S(1)}, u32[]{:S(2)}, u32[]{:S(2)}) %all-to-all-start) | async-done | bytes 262176 | tf_op jit(solution)/shard_map/all_to_all | solution.py:223
  20.5 16.5 %all-to-all-start.1 = ((bf16[16,4,2,16,128]{4,3,2,1,0:T(8,128)(2,1)}), bf16[16,4,2,16,128]{4,3,2,1,0:T(8,128)(2,1)S(1)}, u32[]{:S(2)}, u32[]{:S(2)}) async-start(bf16[16,4,2,16,128]{4,3,2,1,0:T(8,128)(2,1)} %pad_maximum_fusion.1), calls=%async_computation.1 | async-start | bytes 1048576 | tf_op jit(solution)/shard_map/all_to_all | solution.py:195
  37.0 3.8 %collective-permute-start.3 = (bf16[256,512]{1,0:T(8,128)(2,1)S(1)}, bf16[256,512]{1,0:T(8,128)(2,1)S(1)}, u32[]{:S(2)}, u32[]{:S(2)}) collective-permute-start(bf16[256,512]{1,0:T(8,128)(2,1)S(1)} %bitcast.17), channel_id=1, source_target_pairs={{192,0},{224,32},{0,64},{32,96},{64,128},{96,160},{128,192},{160,2... | collective-permute-start | bytes 786440 | tf_op jit(solution)/shard_map/ppermute | solution.py:208
  40.8 4.6 %collective-permute-start.2 = (bf16[256,512]{1,0:T(8,128)(2,1)S(1)}, bf16[256,512]{1,0:T(8,128)(2,1)S(1)}, u32[]{:S(2)}, u32[]{:S(2)}) collective-permute-start(bf16[256,512]{1,0:T(8,128)(2,1)S(1)} %bitcast.18), channel_id=1, source_target_pairs={{128,0},{160,32},{192,64},{224,96},{0,128},{32,160},{64,192},{96,2... | collective-permute-start | bytes 786440 | tf_op jit(solution)/shard_map/ppermute | solution.py:208
  45.4 3.4 %collective-permute-start.1 = (bf16[256,512]{1,0:T(8,128)(2,1)S(1)}, bf16[256,512]{1,0:T(8,128)(2,1)S(1)}, u32[]{:S(2)}, u32[]{:S(2)}) collective-permute-start(bf16[256,512]{1,0:T(8,128)(2,1)S(1)} %bitcast.19), channel_id=1, source_target_pairs={{64,0},{96,32},{128,64},{160,96},{192,128},{224,160},{0,192},{32,2... | collective-permute-start | bytes 786440 | tf_op jit(solution)/shard_map/ppermute | solution.py:208
  48.8 4.0 %collective-permute-done.3 = bf16[256,512]{1,0:T(8,128)(2,1)S(1)} collective-permute-done((bf16[256,512]{1,0:T(8,128)(2,1)S(1)}, bf16[256,512]{1,0:T(8,128)(2,1)S(1)}, u32[]{:S(2)}, u32[]{:S(2)}) %collective-permute-start.3) | collective-permute-done | bytes 262176 | tf_op jit(solution)/shard_map/ppermute | solution.py:208
  52.8 5.6 %collective-permute-done.2 = bf16[256,512]{1,0:T(8,128)(2,1)S(1)} collective-permute-done((bf16[256,512]{1,0:T(8,128)(2,1)S(1)}, bf16[256,512]{1,0:T(8,128)(2,1)S(1)}, u32[]{:S(2)}, u32[]{:S(2)}) %collective-permute-start.2) | collective-permute-done | bytes 262176 | tf_op jit(solution)/shard_map/ppermute | solution.py:208
  58.5 0.0 collective-permute-done.1
  58.5 0.1 pad_maximum_fusion.mine
  58.6 1.9 %collective-permute-start.4 = (bf16[4,256,512]{2,1,0:T(8,128)(2,1)S(1)}, bf16[4,256,512]{2,1,0:T(8,128)(2,1)}, u32[]{:S(2)}, u32[]{:S(2)}) collective-permute-start(bf16[4,256,512]{2,1,0:T(8,128)(2,1)S(1)} %pad_maximum_fusion.mine), channel_id=1, source_target_pairs={{0,32},{32,0},{64,96},{96,64},{128,160},{160,128},{192,224},{224,1... | collective-permute-start | bytes 3145736 | tf_op jit(solution)/shard_map/ppermute | solution.py:229
  60.5 0.0 copy-start.1
  60.5 1.0 copy-done.1
  61.5 0.0 all-to-all-done.1.blocks
  61.5 7.6 %chebyshev.1 = bf16[1024,128]{1,0:T(8,128)(2,1)S(1)} custom-call(bf16[16,4,2,16,128]{4,3,2,1,0:T(8,128)(2,1)S(1)} %all-to-all-done.1.blocks), custom_call_target="tpu_custom_call" | custom-call | tf_op jit(solution)/shard_map/chebyshev/pallas_call | solution.py:196
  69.1 27.6 %all_to_all.20 = bf16[512,2,128]{2,1,0:T(2,128)(2,1)S(1)} all-to-all(bf16[512,2,128]{2,1,0:T(2,128)(2,1)S(1)} %bitcast.16), channel_id=1, replica_groups=mesh['dom'=16,'band'=32] {'band','dom'}, dimensions={0} | all-to-all | bytes 524288 | tf_op jit(solution)/shard_map/all_to_all | solution.py:231
  96.7 0.0 collective-permute-done.4.other
  96.7 0.0 copy-start.2
  96.7 1.2 %copy-done.2 = bf16[4,256,512]{2,1,0:T(8,128)(2,1)S(1)} copy-done((bf16[4,256,512]{2,1,0:T(8,128)(2,1)S(1)}, bf16[4,256,512]{2,1,0:T(8,128)(2,1)}, u32[]{:S(2)}) %copy-start.2) | copy-done | bytes 1048600
  98.0 1.9 %rotate.1 = bf16[1024,128]{1,0:T(8,128)(2,1)S(1)} custom-call(bf16[4,256,512]{2,1,0:T(8,128)(2,1)S(1)} %copy-done.2, bf16[4,256,512]{2,1,0:T(8,128)(2,1)} %collective-permute-done.4.other, bf16[1024,128]{1,0:T(8,128)(2,1)S(1)} %bitcast.14), custom_call_target="tpu_custom_call" | custom-call | tf_op jit(solution)/shard_map/rotate/pallas_call | solution.py:235
  99.9 19.9 %all_to_all.21 = bf16[32,32,128]{2,1,0:T(8,128)(2,1)S(1)} all-to-all(bf16[32,32,128]{2,1,0:T(8,128)(2,1)S(1)} %bitcast.15), channel_id=1, replica_groups=mesh['dom'=16,'band'=32] {'band'}, dimensions={0} | all-to-all | bytes 524288 | tf_op jit(solution)/shard_map/all_to_all | solution.py:236
  119.8 0.1 convert_bitcast_fusion
  119.9 1.1 copy.4
  (4 shorter events, 0.1 us)
Async XLA Ops:
  0.0 0.8 copy-start
  0.8 0.7 collective-permute-start
  2.2 9.2 %copy-start.4 = (f32[1,2,16,128]{3,2,1,0:T(8,128)S(1)}, f32[1,2,16,128]{3,2,1,0:T(8,128)}, u32[]{:S(2)}) copy-start(f32[1,2,16,128]{3,2,1,0:T(8,128)} %param.4) | copy-start | bytes 49156
  2.2 18.3 %all-to-all-start = ((bf16[8,32,512]{2,1,0:T(8,128)(2,1)}), bf16[8,32,512]{2,1,0:T(8,128)(2,1)S(1)}, u32[]{:S(2)}, u32[]{:S(2)}) async-start(bf16[8,32,512]{2,1,0:T(8,128)(2,1)} %broadcast_in_dim.4), calls=%async_computation | async-start | bytes 524288 | tf_op jit(solution)/shard_map/all_to_all | solution.py:223
  11.5 1.0 copy-start.3
  20.5 41.0 %all-to-all-start.1 = ((bf16[16,4,2,16,128]{4,3,2,1,0:T(8,128)(2,1)}), bf16[16,4,2,16,128]{4,3,2,1,0:T(8,128)(2,1)S(1)}, u32[]{:S(2)}, u32[]{:S(2)}) async-start(bf16[16,4,2,16,128]{4,3,2,1,0:T(8,128)(2,1)} %pad_maximum_fusion.1), calls=%async_computation.1 | async-start | bytes 1048576 | tf_op jit(solution)/shard_map/all_to_all | solution.py:195
  37.0 15.8 %collective-permute-start.3 = (bf16[256,512]{1,0:T(8,128)(2,1)S(1)}, bf16[256,512]{1,0:T(8,128)(2,1)S(1)}, u32[]{:S(2)}, u32[]{:S(2)}) collective-permute-start(bf16[256,512]{1,0:T(8,128)(2,1)S(1)} %bitcast.17), channel_id=1, source_target_pairs={{192,0},{224,32},{0,64},{32,96},{64,128},{96,160},{128,192},{160,2... | collective-permute-start | bytes 786440 | tf_op jit(solution)/shard_map/ppermute | solution.py:208
  40.8 17.6 %collective-permute-start.2 = (bf16[256,512]{1,0:T(8,128)(2,1)S(1)}, bf16[256,512]{1,0:T(8,128)(2,1)S(1)}, u32[]{:S(2)}, u32[]{:S(2)}) collective-permute-start(bf16[256,512]{1,0:T(8,128)(2,1)S(1)} %bitcast.18), channel_id=1, source_target_pairs={{128,0},{160,32},{192,64},{224,96},{0,128},{32,160},{64,192},{96,2... | collective-permute-start | bytes 786440 | tf_op jit(solution)/shard_map/ppermute | solution.py:208
  45.4 13.0 %collective-permute-start.1 = (bf16[256,512]{1,0:T(8,128)(2,1)S(1)}, bf16[256,512]{1,0:T(8,128)(2,1)S(1)}, u32[]{:S(2)}, u32[]{:S(2)}) collective-permute-start(bf16[256,512]{1,0:T(8,128)(2,1)S(1)} %bitcast.19), channel_id=1, source_target_pairs={{64,0},{96,32},{128,64},{160,96},{192,128},{224,160},{0,192},{32,2... | collective-permute-start | bytes 786440 | tf_op jit(solution)/shard_map/ppermute | solution.py:208
  58.6 38.1 %collective-permute-start.4 = (bf16[4,256,512]{2,1,0:T(8,128)(2,1)S(1)}, bf16[4,256,512]{2,1,0:T(8,128)(2,1)}, u32[]{:S(2)}, u32[]{:S(2)}) collective-permute-start(bf16[4,256,512]{2,1,0:T(8,128)(2,1)S(1)} %pad_maximum_fusion.mine), channel_id=1, source_target_pairs={{0,32},{32,0},{64,96},{96,64},{128,160},{160,128},{192,224},{224,1... | collective-permute-start | bytes 3145736 | tf_op jit(solution)/shard_map/ppermute | solution.py:229
  60.5 1.0 copy-start.1
  96.7 1.2 %copy-start.2 = (bf16[4,256,512]{2,1,0:T(8,128)(2,1)S(1)}, bf16[4,256,512]{2,1,0:T(8,128)(2,1)}, u32[]{:S(2)}) copy-start(bf16[4,256,512]{2,1,0:T(8,128)(2,1)} %copy-done.1) | copy-start | bytes 3145732

commit v7 on v6

--- a/solution.py
+++ b/solution.py
@@ -38,7 +38,8 @@
     side = math.isqrt(n_dom)
     gx, gy = side * cx, side * cy
     centre, first_scale, weights = filter_weights(DEG)
-    row_stride = n_dom * n_own
+    row_stride = n_dom // 2 * n_own
+    rows_out = cx * cy * row_stride
     far_near = coef_two / coef_one
 
     def wrap(ref, band, x):
@@ -61,7 +62,9 @@
         far = (plane(-2) + plane(2)) + (rows(-2) + rows(2)) + (lanes(-2) + lanes(2))
         return diag[x] * mid + (-0.5 * coef_one) * (near + far_near * far)
 
-    def body(blocks, out, first, second, diag, ordered):
+    def body(blocks, out, away, first, second, diag, ordered):
+        core, _ = chip_place(side)
+
         def load(x, carry):
             for j in range(side):
                 dom = lax.div(x, cx) * side + j
@@ -110,9 +113,10 @@
             following = following - scale_x * previous[band, x, PAD : PAD + gy, :]
             for j in range(side):
                 for part in range(cy // 8):
-                    dom = lax.div(x, cx) * side + j
+                    pair = lax.div(x, cx) * (side // 2) + j // 2
                     cell = lax.rem(x, cx) * cy + part * 8
-                    base = cell * row_stride + dom * n_own + band
+                    base = cell * row_stride + pair * n_own + band
+                    base = base + lax.bitwise_xor(core, j % 2) * rows_out
                     at = j * cy + part * 8
                     ordered[pl.ds(base, 8, stride=row_stride), :] = following[at : at + 8]
 
@@ -122,22 +126,24 @@
         def store(n, carry):
             at = pl.multiple_of(n * block, block)
             out[pl.ds(at, block), :] = ordered[pl.ds(at, block), :].astype(jnp.bfloat16)
+            far = ordered[pl.ds(rows_out + at, block), :]
+            away[pl.ds(at, block), :] = far.astype(jnp.bfloat16)
             return carry
 
         lax.fori_loop(0, out.shape[0] // block, store, 0)
 
     padded = pltpu.VMEM((n_own, gx, gy + 2 * PAD, nz), jnp.float32)
-    rows_out = cx * cy * n_dom * n_own
+    vmem = pl.BlockSpec(memory_space=pltpu.VMEM)
     return pl.pallas_call(
         body,
-        out_shape=pltpu.VMEM((rows_out, nz), jnp.bfloat16),
-        in_specs=[pl.BlockSpec(memory_space=pltpu.VMEM)],
-        out_specs=pl.BlockSpec(memory_space=pltpu.VMEM),
+        out_shape=[pltpu.VMEM((rows_out, nz), jnp.bfloat16)] * 2,
+        in_specs=[vmem],
+        out_specs=[vmem, vmem],
         scratch_shapes=[
             padded,
             padded,
             pltpu.VMEM((gx, gy, nz), jnp.float32),
-            pltpu.VMEM((rows_out, nz), jnp.float32),
+            pltpu.VMEM((2 * rows_out, nz), jnp.float32),
         ],
         name="chebyshev",
     )
@@ -193,7 +199,7 @@
     blocks = orbitals.reshape(n_dom, n_own, cx, cy, nz)
     blocks = jnp.concatenate([blocks, parts], axis=1)
     blocks = lax.all_to_all(blocks, "dom", 0, 0, tiled=True)
-    filtered = filter_kernel(n_dom, n_own, cx, cy, nz)(in_vmem(blocks))
+    kept, away = filter_kernel(n_dom, n_own, cx, cy, nz)(in_vmem(blocks))
 
     half = n_all // 2
 
@@ -228,8 +234,17 @@
     mine = jnp.stack([own, after, far, before])
     other = lax.ppermute(mine, "dom", [(d, d ^ 1) for d in range(n_dom)])
 
+    swapped = [(d, d ^ 1) for d in range(n_dom)]
+    away = lax.ppermute(away, "dom", swapped)
+    n_pair = n_dom // 2
+    kept = kept.reshape(n_band * n_pair, n_own, nz)
+    away = away.reshape(n_band * n_pair, n_own, nz)
+    rows = jnp.where(
+        core == 0, jnp.concatenate([kept, away], axis=1), jnp.concatenate([away, kept], axis=1)
+    )
+    group = [[b * n_dom + 2 * p + c for b in range(n_band) for p in range(n_pair)] for c in (0, 1)]
     rows = lax.all_to_all(
-        filtered.reshape(n_band * n_dom, n_own, nz), ("band", "dom"), 0, 0, tiled=True
+        rows, ("band", "dom"), 0, 0, tiled=True, axis_index_groups=group
     ).reshape(n_all, nz)
 
     rotated = rotate_kernel(n_all, n_x, nz)(in_vmem(mine), in_vmem(other), in_vmem(rows))

time: 122 us -> 124 us (1.016)
  starting transfers between devices: 40.1 us -> 42.5 us
  local copies, waits for them, and re-layouts: 5.81 us -> 3.6 us
  other arithmetic: 1.03 us -> 2.49 us
    ppermute x0 -> x1, starting transfers between devices: none -> 2.41 us  [on_device(): away = lax.ppermute(away, 'dom', swapped)]
    unnamed x10 -> x6, local copies, waits for them, and re-layouts: 3.93 us -> 1.72 us
    all_to_all x1, blocking collectives: 19.9 us -> 18.4 us  [on_device(): lax.all_to_all(rotated.reshape(n_band, n_mine, nz), 'band', 0, 0, tiled=T...]
  transfers between devices with their start and end apart: 7 -> 8, of which waited for: 3 -> 4; matrix products, arithmetic and copies ran while one was open for 1% -> 2% of each run, Pallas kernels for 6% -> 6%
where the time goes in v7:
time: 124 us; the launch traced here: 123 us
  blocking collectives  46.8 us (38%)
  starting transfers between devices  42.5 us (34%)
  waiting for transfers between devices  17.9 us (14%)
  Pallas kernels  9.52 us (8%)
  local copies, waits for them, and re-layouts  3.6 us (3%)
  other arithmetic  2.49 us (2%)
    all_to_all x1, blocking collectives, on_device(): lax.all_to_all(rows, ('band', 'dom'), 0, 0, tiled=True, axis_index_groups...  28.4 us
    all_to_all x1, blocking collectives, on_device(): lax.all_to_all(rotated.reshape(n_band, n_mine, nz), 'band', 0, 0, tiled=T...  18.4 us
    all_to_all x1, starting transfers between devices, on_device(): blocks = lax.all_to_all(blocks, 'dom', 0, 0, tiled=True)  16.5 us
    ppermute x3, starting transfers between devices, from_x(): return lax.ppermute(value, 'dom', pairs)  11.8 us
    ppermute x3, waiting for transfers between devices, from_x(): return lax.ppermute(value, 'dom', pairs)  9.66 us
    all_to_all x1, starting transfers between devices, on_device(): lax.all_to_all(many, 'band', 0, 0, tiled=True, axis_index_groups=lines)  9.24 us
    pallas_call x1, Pallas kernels, on_device(): kept, away = filter_kernel(n_dom, n_own, cx, cy, nz)(in_vmem(blocks))  7.29 us
    all_to_all x1, waiting for transfers between devices, on_device(): lax.all_to_all(many, 'band', 0, 0, tiled=True, axis_index_groups=lines)  7.26 us
  transfers between devices with their start and end apart: 8, of which 4 were waited for; matrix products, arithmetic and copies ran while one was open for 2% of the time, Pallas kernels for 6%

profile of v7, /device:TPU:8, one launch (start us, length us, event | category | flops | bytes accessed | tf_op | source)
XLA Modules:
  0.0 122.8 jit_solution(14270159938064781105)
XLA Ops:
  0.0 0.0 copy-start
  0.0 0.8 copy-done
  0.8 0.7 collective-permute-start
  1.5 0.0 collective-permute-done
  1.5 0.7 broadcast_in_dim.4
  2.2 0.0 copy-start.2
  2.2 9.2 %all-to-all-start = ((bf16[8,32,512]{2,1,0:T(8,128)(2,1)}), bf16[8,32,512]{2,1,0:T(8,128)(2,1)S(1)}, u32[]{:S(2)}, u32[]{:S(2)}) async-start(bf16[8,32,512]{2,1,0:T(8,128)(2,1)} %broadcast_in_dim.4), calls=%async_computation | async-start | bytes 524288 | tf_op jit(solution)/shard_map/all_to_all | solution.py:229
  11.5 0.0 copy-done.2
  11.5 0.0 copy-start.1
  11.6 0.9 copy-done.1
  12.4 0.8 pad_maximum_fusion.1
  13.3 7.3 %all-to-all-done = bf16[8,32,512]{2,1,0:T(8,128)(2,1)S(1)} async-done(((bf16[8,32,512]{2,1,0:T(8,128)(2,1)}), bf16[8,32,512]{2,1,0:T(8,128)(2,1)S(1)}, u32[]{:S(2)}, u32[]{:S(2)}) %all-to-all-start) | async-done | bytes 262176 | tf_op jit(solution)/shard_map/all_to_all | solution.py:229
  20.5 16.5 %all-to-all-start.1 = ((bf16[16,4,2,16,128]{4,3,2,1,0:T(8,128)(2,1)}), bf16[16,4,2,16,128]{4,3,2,1,0:T(8,128)(2,1)S(1)}, u32[]{:S(2)}, u32[]{:S(2)}) async-start(bf16[16,4,2,16,128]{4,3,2,1,0:T(8,128)(2,1)} %pad_maximum_fusion.1), calls=%async_computation.1 | async-start | bytes 1048576 | tf_op jit(solution)/shard_map/all_to_all | solution.py:201
  37.0 3.8 %collective-permute-start.3 = (bf16[256,512]{1,0:T(8,128)(2,1)S(1)}, bf16[256,512]{1,0:T(8,128)(2,1)S(1)}, u32[]{:S(2)}, u32[]{:S(2)}) collective-permute-start(bf16[256,512]{1,0:T(8,128)(2,1)S(1)} %bitcast.18), channel_id=1, source_target_pairs={{192,0},{224,32},{0,64},{32,96},{64,128},{96,160},{128,192},{160,2... | collective-permute-start | bytes 786440 | tf_op jit(solution)/shard_map/ppermute | solution.py:214
  40.8 4.6 %collective-permute-start.2 = (bf16[256,512]{1,0:T(8,128)(2,1)S(1)}, bf16[256,512]{1,0:T(8,128)(2,1)S(1)}, u32[]{:S(2)}, u32[]{:S(2)}) collective-permute-start(bf16[256,512]{1,0:T(8,128)(2,1)S(1)} %bitcast.19), channel_id=1, source_target_pairs={{128,0},{160,32},{192,64},{224,96},{0,128},{32,160},{64,192},{96,2... | collective-permute-start | bytes 786440 | tf_op jit(solution)/shard_map/ppermute | solution.py:214
  45.4 3.4 %collective-permute-start.1 = (bf16[256,512]{1,0:T(8,128)(2,1)S(1)}, bf16[256,512]{1,0:T(8,128)(2,1)S(1)}, u32[]{:S(2)}, u32[]{:S(2)}) collective-permute-start(bf16[256,512]{1,0:T(8,128)(2,1)S(1)} %bitcast.20), channel_id=1, source_target_pairs={{64,0},{96,32},{128,64},{160,96},{192,128},{224,160},{0,192},{32,2... | collective-permute-start | bytes 786440 | tf_op jit(solution)/shard_map/ppermute | solution.py:214
  48.8 4.0 %collective-permute-done.3 = bf16[256,512]{1,0:T(8,128)(2,1)S(1)} collective-permute-done((bf16[256,512]{1,0:T(8,128)(2,1)S(1)}, bf16[256,512]{1,0:T(8,128)(2,1)S(1)}, u32[]{:S(2)}, u32[]{:S(2)}) %collective-permute-start.3) | collective-permute-done | bytes 262176 | tf_op jit(solution)/shard_map/ppermute | solution.py:214
  52.8 5.6 %collective-permute-done.2 = bf16[256,512]{1,0:T(8,128)(2,1)S(1)} collective-permute-done((bf16[256,512]{1,0:T(8,128)(2,1)S(1)}, bf16[256,512]{1,0:T(8,128)(2,1)S(1)}, u32[]{:S(2)}, u32[]{:S(2)}) %collective-permute-start.2) | collective-permute-done | bytes 262176 | tf_op jit(solution)/shard_map/ppermute | solution.py:214
  58.5 0.0 collective-permute-done.1
  58.5 1.1 pad_maximum_fusion.mine
  59.6 1.9 %collective-permute-start.4 = (bf16[4,256,512]{2,1,0:T(8,128)(2,1)}, bf16[4,256,512]{2,1,0:T(8,128)(2,1)}, u32[]{:S(2)}, u32[]{:S(2)}) collective-permute-start(bf16[4,256,512]{2,1,0:T(8,128)(2,1)} %pad_maximum_fusion.mine), channel_id=1, source_target_pairs={{0,32},{32,0},{64,96},{96,64},{128,160},{160,128},{192,224},{224,1... | collective-permute-start | bytes 3145736 | tf_op jit(solution)/shard_map/ppermute | solution.py:235
  61.5 0.0 all-to-all-done.1.blocks
  61.5 7.3 %chebyshev.1 = (bf16[512,128]{1,0:T(8,128)(2,1)S(1)}, bf16[512,128]{1,0:T(8,128)(2,1)S(1)}) custom-call(bf16[16,4,2,16,128]{4,3,2,1,0:T(8,128)(2,1)S(1)} %all-to-all-done.1.blocks), custom_call_target="tpu_custom_call" | custom-call | tf_op jit(solution)/shard_map/chebyshev/pallas_call | solution.py:202
  68.8 2.4 %collective-permute-start.5 = (bf16[512,128]{1,0:T(8,128)(2,1)S(1)}, bf16[512,128]{1,0:T(8,128)(2,1)S(1)}, u32[]{:S(2)}, u32[]{:S(2)}) collective-permute-start(bf16[512,128]{1,0:T(8,128)(2,1)S(1)} %get-tuple-element.8), channel_id=1, source_target_pairs={{0,32},{32,0},{64,96},{96,64},{128,160},{160,128},{192,224},{224,1... | collective-permute-start | bytes 393224 | tf_op jit(solution)/shard_map/ppermute | solution.py:238
  71.2 1.0 collective-permute-done.5
  72.2 0.5 maximum_select_fusion
  72.7 28.4 %all_to_all.20 = bf16[256,4,128]{2,1,0:T(4,128)(2,1)S(1)} all-to-all(bf16[256,4,128]{2,1,0:T(4,128)(2,1)S(1)} %maximum_select_fusion), channel_id=1, replica_groups={{0,64,128,192,256,320,384,448,1,65,129,193,257,321,385,449,2,66,130,194..., dimensions={0} | all-to-all | bytes 524288 | tf_op jit(solution)/shard_map/all_to_all | solution.py:246
  101.0 0.0 collective-permute-done.4.other
  101.0 2.2 %rotate.1 = bf16[1024,128]{1,0:T(8,128)(2,1)S(1)} custom-call(bf16[4,256,512]{2,1,0:T(8,128)(2,1)} %pad_maximum_fusion.mine, bf16[4,256,512]{2,1,0:T(8,128)(2,1)} %collective-permute-done.4.other, bf16[1024,128]{1,0:T(8,128)(2,1)S(1)} %bitcast.15), custom_call_target="tpu_custom_call" | custom-call | tf_op jit(solution)/shard_map/rotate/pallas_call | solution.py:250
  103.3 18.4 %all_to_all.21 = bf16[32,32,128]{2,1,0:T(8,128)(2,1)S(1)} all-to-all(bf16[32,32,128]{2,1,0:T(8,128)(2,1)S(1)} %bitcast.16), channel_id=1, replica_groups=mesh['dom'=16,'band'=32] {'band'}, dimensions={0} | all-to-all | bytes 524288 | tf_op jit(solution)/shard_map/all_to_all | solution.py:251
  121.7 0.1 convert_bitcast_fusion
  121.7 1.1 copy.4
  (4 shorter events, 0.1 us)
Async XLA Ops:
  0.0 0.8 copy-start
  0.8 0.7 collective-permute-start
  2.2 9.2 %copy-start.2 = (f32[1,2,16,128]{3,2,1,0:T(8,128)S(1)}, f32[1,2,16,128]{3,2,1,0:T(8,128)}, u32[]{:S(2)}) copy-start(f32[1,2,16,128]{3,2,1,0:T(8,128)} %param.4) | copy-start | bytes 49156
  2.2 18.3 %all-to-all-start = ((bf16[8,32,512]{2,1,0:T(8,128)(2,1)}), bf16[8,32,512]{2,1,0:T(8,128)(2,1)S(1)}, u32[]{:S(2)}, u32[]{:S(2)}) async-start(bf16[8,32,512]{2,1,0:T(8,128)(2,1)} %broadcast_in_dim.4), calls=%async_computation | async-start | bytes 524288 | tf_op jit(solution)/shard_map/all_to_all | solution.py:229
  11.5 1.0 copy-start.1
  20.5 41.0 %all-to-all-start.1 = ((bf16[16,4,2,16,128]{4,3,2,1,0:T(8,128)(2,1)}), bf16[16,4,2,16,128]{4,3,2,1,0:T(8,128)(2,1)S(1)}, u32[]{:S(2)}, u32[]{:S(2)}) async-start(bf16[16,4,2,16,128]{4,3,2,1,0:T(8,128)(2,1)} %pad_maximum_fusion.1), calls=%async_computation.1 | async-start | bytes 1048576 | tf_op jit(solution)/shard_map/all_to_all | solution.py:201
  37.0 15.8 %collective-permute-start.3 = (bf16[256,512]{1,0:T(8,128)(2,1)S(1)}, bf16[256,512]{1,0:T(8,128)(2,1)S(1)}, u32[]{:S(2)}, u32[]{:S(2)}) collective-permute-start(bf16[256,512]{1,0:T(8,128)(2,1)S(1)} %bitcast.18), channel_id=1, source_target_pairs={{192,0},{224,32},{0,64},{32,96},{64,128},{96,160},{128,192},{160,2... | collective-permute-start | bytes 786440 | tf_op jit(solution)/shard_map/ppermute | solution.py:214
  40.8 17.6 %collective-permute-start.2 = (bf16[256,512]{1,0:T(8,128)(2,1)S(1)}, bf16[256,512]{1,0:T(8,128)(2,1)S(1)}, u32[]{:S(2)}, u32[]{:S(2)}) collective-permute-start(bf16[256,512]{1,0:T(8,128)(2,1)S(1)} %bitcast.19), channel_id=1, source_target_pairs={{128,0},{160,32},{192,64},{224,96},{0,128},{32,160},{64,192},{96,2... | collective-permute-start | bytes 786440 | tf_op jit(solution)/shard_map/ppermute | solution.py:214
  45.4 13.0 %collective-permute-start.1 = (bf16[256,512]{1,0:T(8,128)(2,1)S(1)}, bf16[256,512]{1,0:T(8,128)(2,1)S(1)}, u32[]{:S(2)}, u32[]{:S(2)}) collective-permute-start(bf16[256,512]{1,0:T(8,128)(2,1)S(1)} %bitcast.20), channel_id=1, source_target_pairs={{64,0},{96,32},{128,64},{160,96},{192,128},{224,160},{0,192},{32,2... | collective-permute-start | bytes 786440 | tf_op jit(solution)/shard_map/ppermute | solution.py:214
  59.6 41.4 %collective-permute-start.4 = (bf16[4,256,512]{2,1,0:T(8,128)(2,1)}, bf16[4,256,512]{2,1,0:T(8,128)(2,1)}, u32[]{:S(2)}, u32[]{:S(2)}) collective-permute-start(bf16[4,256,512]{2,1,0:T(8,128)(2,1)} %pad_maximum_fusion.mine), channel_id=1, source_target_pairs={{0,32},{32,0},{64,96},{96,64},{128,160},{160,128},{192,224},{224,1... | collective-permute-start | bytes 3145736 | tf_op jit(solution)/shard_map/ppermute | solution.py:235
  68.8 3.4 %collective-permute-start.5 = (bf16[512,128]{1,0:T(8,128)(2,1)S(1)}, bf16[512,128]{1,0:T(8,128)(2,1)S(1)}, u32[]{:S(2)}, u32[]{:S(2)}) collective-permute-start(bf16[512,128]{1,0:T(8,128)(2,1)S(1)} %get-tuple-element.8), channel_id=1, source_target_pairs={{0,32},{32,0},{64,96},{96,64},{128,160},{160,128},{192,224},{224,1... | collective-permute-start | bytes 393224 | tf_op jit(solution)/shard_map/ppermute | solution.py:238

commit v8 on v6

--- a/solution.py
+++ b/solution.py
@@ -41,83 +41,82 @@
     row_stride = n_dom * n_own
     far_near = coef_two / coef_one
 
-    def wrap(ref, band, x):
-        ref[band, x, 0:PAD, :] = ref[band, x, gy : gy + PAD, :]
-        ref[band, x, PAD + gy : PAD + gy + PAD, :] = ref[band, x, PAD : 2 * PAD, :]
-
-    def shifted_ham(cur, diag, band, x):
-        mid = cur[band, x, PAD : PAD + gy, :]
-
-        def plane(step):
-            return cur[band, lax.rem(x + (gx + step), gx), PAD : PAD + gy, :]
-
-        def rows(step):
-            return cur[band, x, PAD + step : PAD + step + gy, :]
-
-        def lanes(step):
-            return pltpu.roll(mid, step % nz, 1)
-
-        near = (plane(-1) + plane(1)) + (rows(-1) + rows(1)) + (lanes(-1) + lanes(1))
-        far = (plane(-2) + plane(2)) + (rows(-2) + rows(2)) + (lanes(-2) + lanes(2))
-        return diag[x] * mid + (-0.5 * coef_one) * (near + far_near * far)
-
     def body(blocks, out, first, second, diag, ordered):
-        def load(x, carry):
+        for x in range(gx):
             for j in range(side):
-                dom = lax.div(x, cx) * side + j
-                inner = lax.rem(x, cx)
+                dom, inner = x // cx * side + j, x % cx
                 for band in range(n_own):
-                    first[band, x, PAD + j * cy : PAD + (j + 1) * cy, :] = blocks[
-                        dom, band, inner
-                    ].astype(jnp.float32)
+                    value = blocks[dom, band, inner].astype(jnp.float32)
+                    first[band, x, PAD + j * cy : PAD + (j + 1) * cy, :] = value
+                    if j == 0:
+                        first[band, x, PAD + gy : PAD + gy + PAD, :] = value[:PAD]
+                    if j == side - 1:
+                        first[band, x, 0:PAD, :] = value[cy - PAD :]
                 pot = blocks[dom, n_own, inner].astype(jnp.float32) + blocks[
                     dom, n_own + 1, inner
                 ].astype(jnp.float32)
                 diag[x, j * cy : (j + 1) * cy, :] = pot + (-1.5 * coef_zero - centre)
-            for band in range(n_own):
-                wrap(first, band, x)
-            return carry
-
-        lax.fori_loop(0, gx, load, 0)
-
-        def run(step):
-            def one(n, carry):
-                step(lax.div(n, gx), lax.rem(n, gx))
+
+        def sweep(cur, store):
+            def one(band, carry):
+                for y in range(0, gy, 8):
+
+                    def rows(x, step):
+                        return cur[band, x, PAD + y + step : PAD + y + step + 8, :]
+
+                    mids = [rows(x, 0) for x in range(gx)]
+                    sums = {}
+
+                    def planes(x, step):
+                        pair = tuple(sorted(((x - step) % gx, (x + step) % gx)))
+                        if pair not in sums:
+                            sums[pair] = mids[pair[0]] + mids[pair[1]]
+                        return sums[pair]
+
+                    for x in range(gx):
+                        mid = mids[x]
+
+                        def around(step):
+                            lanes = pltpu.roll(mid, step, 1) + pltpu.roll(mid, nz - step, 1)
+                            return planes(x, step) + (rows(x, -step) + rows(x, step)) + lanes
+
+                        value = around(1) + far_near * around(2)
+                        value = diag[x, y : y + 8, :] * mid + (-0.5 * coef_one) * value
+                        store(band, x, y, value)
                 return carry
 
-            lax.fori_loop(0, n_own * gx, one, 0)
-
-        def start(band, x):
-            second[band, x, PAD : PAD + gy, :] = shifted_ham(first, diag, band, x) * first_scale
-            wrap(second, band, x)
-
-        run(start)
+            lax.fori_loop(0, n_own, one, 0)
+
+        def put(ref, band, x, y, value):
+            ref[band, x, PAD + y : PAD + y + 8, :] = value
+            if y == 0:
+                ref[band, x, PAD + gy : PAD + gy + PAD, :] = value
+            if y == gy - 8:
+                ref[band, x, 0:PAD, :] = value
+
+        def start(band, x, y, value):
+            put(second, band, x, y, value * first_scale)
+
+        sweep(first, start)
         previous, current = first, second
         for scale_h, scale_x in weights[:-1]:
 
-            def middle(band, x, previous=previous, current=current, scale_h=scale_h, scale_x=scale_x):
-                following = shifted_ham(current, diag, band, x) * scale_h
-                following = following - scale_x * previous[band, x, PAD : PAD + gy, :]
-                previous[band, x, PAD : PAD + gy, :] = following
-                wrap(previous, band, x)
-
-            run(middle)
+            def middle(band, x, y, value, previous=previous, scale_h=scale_h, scale_x=scale_x):
+                before = previous[band, x, PAD + y : PAD + y + 8, :]
+                put(previous, band, x, y, value * scale_h - scale_x * before)
+
+            sweep(current, middle)
             previous, current = current, previous
         scale_h, scale_x = weights[-1]
 
-        def last(band, x):
-            following = shifted_ham(current, diag, band, x) * scale_h
-            following = following - scale_x * previous[band, x, PAD : PAD + gy, :]
-            for j in range(side):
-                for part in range(cy // 8):
-                    dom = lax.div(x, cx) * side + j
-                    cell = lax.rem(x, cx) * cy + part * 8
-                    base = cell * row_stride + dom * n_own + band
-                    at = j * cy + part * 8
-                    ordered[pl.ds(base, 8, stride=row_stride), :] = following[at : at + 8]
-
-        run(last)
-        block = 64
+        def last(band, x, y, value):
+            value = value * scale_h - scale_x * previous[band, x, PAD + y : PAD + y + 8, :]
+            dom = x // cx * side + y // cy
+            base = (x % cx * cy + y % cy) * row_stride + dom * n_own + band
+            ordered[pl.ds(base, 8, stride=row_stride), :] = value
+
+        sweep(current, last)
+        block = 128
 
         def store(n, carry):
             at = pl.multiple_of(n * block, block)
@@ -148,7 +147,9 @@
 
     def body(mine, other, rows, out):
         core, x = chip_place(n_x)
-        first = lax.div(lax.axis_index("band"), lax.axis_size("band") // n_x) + x
+        z_lo = lax.div(lax.axis_index("dom"), 2 * n_x)
+        z_hi = lax.div(lax.axis_index("band"), lax.axis_size("band") // n_x)
+        first = z_hi + x + 2 * z_lo
         near = rows[pl.ds(pl.multiple_of(core * half, half), half), :]
         far = rows[pl.ds(pl.multiple_of((1 - core) * half, half), half), :]
         for r in range(n_x):
@@ -212,8 +213,9 @@
         z, x, c = split(d)
         for p in range(n_band):
             high_z, y = p // n_y, p % n_y
-            near_z = 1 - z if x == 2 else z
-            source = (near_z * 2 * n_x + x * 2 + c) * n_band + (high_z + x) % n_x * n_y + y
+            near_z = 1 - z if x % 2 == 0 else z
+            from_z = (high_z + x + 2 * z) % n_x
+            source = (near_z * 2 * n_x + x * 2 + c) * n_band + from_z * n_y + y
             turned.append((source, d * n_band + p))
 
     own = lax.dynamic_slice_in_dim(ritz.T, core * half, half, 1)
@@ -224,7 +226,8 @@
     own = own.reshape(n_y * n_mine, half)
     after = from_x(own, 1)
     before = from_x(own, -1)
-    far = from_x(own, 2)
+    partner = [(d, (d + n_dom // 2) % n_dom) for d in range(n_dom)]
+    far = lax.ppermute(own, "dom", partner)
     mine = jnp.stack([own, after, far, before])
     other = lax.ppermute(mine, "dom", [(d, d ^ 1) for d in range(n_dom)])
 

time: 122 us -> 113 us (0.926)
  Pallas kernels: 9.5 us -> 4.91 us
  starting transfers between devices: 40.1 us -> 36.5 us
  waiting for transfers between devices: 16.9 us -> 15.3 us
    all_to_all x1, starting transfers between devices: 16.5 us -> 5.06 us  [on_device(): blocks = lax.all_to_all(blocks, 'dom', 0, 0, tiled=True)]
    ppermute x1, starting transfers between devices: 0.65 us -> 10.9 us  [on_device(): own = lax.ppermute(own, ('dom', 'band'), turned)]
    pallas_call x1, Pallas kernels: 7.58 us -> 2.99 us  [on_device(): filtered = filter_kernel(n_dom, n_own, cx, cy, nz)(in_vmem(blocks))]
    ppermute x3 -> x2, starting transfers between devices: 11.8 us -> 7.5 us  [from_x(): return lax.ppermute(value, 'dom', pairs)]
    ppermute x3 -> x2, waiting for transfers between devices: 9.66 us -> 5.97 us  [from_x(): return lax.ppermute(value, 'dom', pairs)]
    ppermute x0 -> x1, starting transfers between devices: none -> 3.38 us  [on_device(): far = lax.ppermute(own, 'dom', partner)]
    ppermute x1, waiting for transfers between devices: 0.01 us -> 1.58 us  [on_device(): own = lax.ppermute(own, ('dom', 'band'), turned)]
    all_to_all x1, starting transfers between devices: 9.24 us -> 7.68 us  [on_device(): lax.all_to_all(many, 'band', 0, 0, tiled=True, axis_index_groups=lines)]
  transfers between devices with their start and end apart: 7 -> 7, of which waited for: 3 -> 4; matrix products, arithmetic and copies ran while one was open for 1% -> 1% of each run, Pallas kernels for 6% -> 3%
where the time goes in v8:
time: 113 us; the launch traced here: 112 us
  blocking collectives  48.7 us (43%)
  starting transfers between devices  36.5 us (32%)
  waiting for transfers between devices  15.3 us (14%)
  local copies, waits for them, and re-layouts  5.81 us (5%)
  Pallas kernels  4.91 us (4%)
    all_to_all x1, blocking collectives, on_device(): lax.all_to_all(filtered.reshape(n_band * n_dom, n_own, nz), ('band', 'dom...  28.8 us
    all_to_all x1, blocking collectives, on_device(): lax.all_to_all(rotated.reshape(n_band, n_mine, nz), 'band', 0, 0, tiled=T...  19.9 us
    ppermute x1, starting transfers between devices, on_device(): own = lax.ppermute(own, ('dom', 'band'), turned)  10.9 us
    all_to_all x1, waiting for transfers between devices, on_device(): lax.all_to_all(many, 'band', 0, 0, tiled=True, axis_index_groups=lines)  7.77 us
    all_to_all x1, starting transfers between devices, on_device(): lax.all_to_all(many, 'band', 0, 0, tiled=True, axis_index_groups=lines)  7.68 us
    ppermute x2, starting transfers between devices, from_x(): return lax.ppermute(value, 'dom', pairs)  7.5 us
    ppermute x2, waiting for transfers between devices, from_x(): return lax.ppermute(value, 'dom', pairs)  5.97 us
    all_to_all x1, starting transfers between devices, on_device(): blocks = lax.all_to_all(blocks, 'dom', 0, 0, tiled=True)  5.06 us
  transfers between devices with their start and end apart: 7, of which 4 were waited for; matrix products, arithmetic and copies ran while one was open for 1% of the time, Pallas kernels for 3%

profile of v8, /device:TPU:8, one launch (start us, length us, event | category | flops | bytes accessed | tf_op | source)
XLA Modules:
  0.0 112.4 jit_solution(16116594408957804646)
XLA Ops:
  0.0 0.0 copy-start
  0.0 0.8 copy-done
  0.8 10.9 %collective-permute-start = (bf16[32,512]{1,0:T(8,128)(2,1)S(1)}, bf16[32,512]{1,0:T(8,128)(2,1)S(1)}, u32[]{:S(2)}, u32[]{:S(2)}) collective-permute-start(bf16[32,512]{1,0:T(8,128)(2,1)S(1)} %dynamic-slice_bitcast_fusion), channel_id=1, source_target_pairs={{256,0},{257,1},{258,2},{259,3},{260,4},{261,5},{262,6},{263,7},{2... | collective-permute-start | bytes 98312 | tf_op jit(solution)/shard_map/ppermute | solution.py:222
  11.8 1.6 %collective-permute-done = bf16[32,512]{1,0:T(8,128)(2,1)S(1)} collective-permute-done((bf16[32,512]{1,0:T(8,128)(2,1)S(1)}, bf16[32,512]{1,0:T(8,128)(2,1)S(1)}, u32[]{:S(2)}, u32[]{:S(2)}) %collective-permute-start) | collective-permute-done | bytes 32800 | tf_op jit(solution)/shard_map/ppermute | solution.py:222
  13.3 0.7 broadcast_in_dim.4
  14.1 0.0 copy-start.4
  14.1 7.7 %all-to-all-start = ((bf16[8,32,512]{2,1,0:T(8,128)(2,1)}), bf16[8,32,512]{2,1,0:T(8,128)(2,1)S(1)}, u32[]{:S(2)}, u32[]{:S(2)}) async-start(bf16[8,32,512]{2,1,0:T(8,128)(2,1)} %broadcast_in_dim.4), calls=%async_computation | async-start | bytes 524288 | tf_op jit(solution)/shard_map/all_to_all | solution.py:225
  21.8 0.0 copy-done.4
  21.8 0.0 copy-start.3
  21.8 0.9 copy-done.3
  22.7 0.8 pad_maximum_fusion.1
  23.5 7.8 %all-to-all-done = bf16[8,32,512]{2,1,0:T(8,128)(2,1)S(1)} async-done(((bf16[8,32,512]{2,1,0:T(8,128)(2,1)}), bf16[8,32,512]{2,1,0:T(8,128)(2,1)S(1)}, u32[]{:S(2)}, u32[]{:S(2)}) %all-to-all-start) | async-done | bytes 262176 | tf_op jit(solution)/shard_map/all_to_all | solution.py:225
  31.3 5.1 %all-to-all-start.1 = ((bf16[16,4,2,16,128]{4,3,2,1,0:T(8,128)(2,1)}), bf16[16,4,2,16,128]{4,3,2,1,0:T(8,128)(2,1)S(1)}, u32[]{:S(2)}, u32[]{:S(2)}) async-start(bf16[16,4,2,16,128]{4,3,2,1,0:T(8,128)(2,1)} %pad_maximum_fusion.1), calls=%async_computation.1 | async-start | bytes 1048576 | tf_op jit(solution)/shard_map/all_to_all | solution.py:196
  36.4 3.8 %collective-permute-start.3 = (bf16[256,512]{1,0:T(8,128)(2,1)S(1)}, bf16[256,512]{1,0:T(8,128)(2,1)S(1)}, u32[]{:S(2)}, u32[]{:S(2)}) collective-permute-start(bf16[256,512]{1,0:T(8,128)(2,1)S(1)} %bitcast.17), channel_id=1, source_target_pairs={{192,0},{224,32},{0,64},{32,96},{64,128},{96,160},{128,192},{160,2... | collective-permute-start | bytes 786440 | tf_op jit(solution)/shard_map/ppermute | solution.py:209
  40.2 3.4 %collective-permute-start.2 = (bf16[256,512]{1,0:T(8,128)(2,1)S(1)}, bf16[256,512]{1,0:T(8,128)(2,1)S(1)}, u32[]{:S(2)}, u32[]{:S(2)}) collective-permute-start(bf16[256,512]{1,0:T(8,128)(2,1)S(1)} %bitcast.18), channel_id=1, source_target_pairs={{0,256},{32,288},{64,320},{96,352},{128,384},{160,416},{192,448},{... | collective-permute-start | bytes 786440 | tf_op jit(solution)/shard_map/ppermute | solution.py:230
  43.6 3.7 %collective-permute-start.1 = (bf16[256,512]{1,0:T(8,128)(2,1)S(1)}, bf16[256,512]{1,0:T(8,128)(2,1)S(1)}, u32[]{:S(2)}, u32[]{:S(2)}) collective-permute-start(bf16[256,512]{1,0:T(8,128)(2,1)S(1)} %bitcast.19), channel_id=1, source_target_pairs={{64,0},{96,32},{128,64},{160,96},{192,128},{224,160},{0,192},{32,2... | collective-permute-start | bytes 786440 | tf_op jit(solution)/shard_map/ppermute | solution.py:209
  47.3 4.6 %collective-permute-done.3 = bf16[256,512]{1,0:T(8,128)(2,1)S(1)} collective-permute-done((bf16[256,512]{1,0:T(8,128)(2,1)S(1)}, bf16[256,512]{1,0:T(8,128)(2,1)S(1)}, u32[]{:S(2)}, u32[]{:S(2)}) %collective-permute-start.3) | collective-permute-done | bytes 262176 | tf_op jit(solution)/shard_map/ppermute | solution.py:209
  51.9 0.0 collective-permute-done.2
  51.9 1.3 %collective-permute-done.1 = bf16[256,512]{1,0:T(8,128)(2,1)S(1)} collective-permute-done((bf16[256,512]{1,0:T(8,128)(2,1)S(1)}, bf16[256,512]{1,0:T(8,128)(2,1)S(1)}, u32[]{:S(2)}, u32[]{:S(2)}) %collective-permute-start.1) | collective-permute-done | bytes 262176 | tf_op jit(solution)/shard_map/ppermute | solution.py:209
  53.3 0.1 pad_maximum_fusion.mine
  53.4 1.9 %collective-permute-start.4 = (bf16[4,256,512]{2,1,0:T(8,128)(2,1)S(1)}, bf16[4,256,512]{2,1,0:T(8,128)(2,1)}, u32[]{:S(2)}, u32[]{:S(2)}) collective-permute-start(bf16[4,256,512]{2,1,0:T(8,128)(2,1)S(1)} %pad_maximum_fusion.mine), channel_id=1, source_target_pairs={{0,32},{32,0},{64,96},{96,64},{128,160},{160,128},{192,224},{224,1... | collective-permute-start | bytes 3145736 | tf_op jit(solution)/shard_map/ppermute | solution.py:232
  55.3 0.0 copy-start.1
  55.3 1.0 copy-done.1
  56.3 0.0 all-to-all-done.1.blocks
  56.3 3.0 %chebyshev.1 = bf16[1024,128]{1,0:T(8,128)(2,1)S(1)} custom-call(bf16[16,4,2,16,128]{4,3,2,1,0:T(8,128)(2,1)S(1)} %all-to-all-done.1.blocks), custom_call_target="tpu_custom_call" | custom-call | tf_op jit(solution)/shard_map/chebyshev/pallas_call | solution.py:197
  59.3 28.8 %all_to_all.20 = bf16[512,2,128]{2,1,0:T(2,128)(2,1)S(1)} all-to-all(bf16[512,2,128]{2,1,0:T(2,128)(2,1)S(1)} %bitcast.16), channel_id=1, replica_groups=mesh['dom'=16,'band'=32] {'band','dom'}, dimensions={0} | all-to-all | bytes 524288 | tf_op jit(solution)/shard_map/all_to_all | solution.py:234
  88.1 0.0 collective-permute-done.4.other
  88.1 0.0 copy-start.2
  88.1 1.2 %copy-done.2 = bf16[4,256,512]{2,1,0:T(8,128)(2,1)S(1)} copy-done((bf16[4,256,512]{2,1,0:T(8,128)(2,1)S(1)}, bf16[4,256,512]{2,1,0:T(8,128)(2,1)}, u32[]{:S(2)}) %copy-start.2) | copy-done | bytes 1048600
  89.3 1.9 %rotate.1 = bf16[1024,128]{1,0:T(8,128)(2,1)S(1)} custom-call(bf16[4,256,512]{2,1,0:T(8,128)(2,1)S(1)} %copy-done.2, bf16[4,256,512]{2,1,0:T(8,128)(2,1)} %collective-permute-done.4.other, bf16[1024,128]{1,0:T(8,128)(2,1)S(1)} %bitcast.14), custom_call_target="tpu_custom_call" | custom-call | tf_op jit(solution)/shard_map/rotate/pallas_call | solution.py:238
  91.3 19.9 %all_to_all.21 = bf16[32,32,128]{2,1,0:T(8,128)(2,1)S(1)} all-to-all(bf16[32,32,128]{2,1,0:T(8,128)(2,1)S(1)} %bitcast.15), channel_id=1, replica_groups=mesh['dom'=16,'band'=32] {'band'}, dimensions={0} | all-to-all | bytes 524288 | tf_op jit(solution)/shard_map/all_to_all | solution.py:239
  111.2 0.1 convert_bitcast_fusion
  111.3 1.1 copy.4
  (4 shorter events, 0.1 us)
Async XLA Ops:
  0.0 0.8 copy-start
  0.8 12.5 %collective-permute-start = (bf16[32,512]{1,0:T(8,128)(2,1)S(1)}, bf16[32,512]{1,0:T(8,128)(2,1)S(1)}, u32[]{:S(2)}, u32[]{:S(2)}) collective-permute-start(bf16[32,512]{1,0:T(8,128)(2,1)S(1)} %dynamic-slice_bitcast_fusion), channel_id=1, source_target_pairs={{256,0},{257,1},{258,2},{259,3},{260,4},{261,5},{262,6},{263,7},{2... | collective-permute-start | bytes 98312 | tf_op jit(solution)/shard_map/ppermute | solution.py:222
  14.1 7.7 %copy-start.4 = (f32[1,2,16,128]{3,2,1,0:T(8,128)S(1)}, f32[1,2,16,128]{3,2,1,0:T(8,128)}, u32[]{:S(2)}) copy-start(f32[1,2,16,128]{3,2,1,0:T(8,128)} %param.4) | copy-start | bytes 49156
  14.1 17.2 %all-to-all-start = ((bf16[8,32,512]{2,1,0:T(8,128)(2,1)}), bf16[8,32,512]{2,1,0:T(8,128)(2,1)S(1)}, u32[]{:S(2)}, u32[]{:S(2)}) async-start(bf16[8,32,512]{2,1,0:T(8,128)(2,1)} %broadcast_in_dim.4), calls=%async_computation | async-start | bytes 524288 | tf_op jit(solution)/shard_map/all_to_all | solution.py:225
  21.8 1.0 copy-start.3
  31.3 25.0 %all-to-all-start.1 = ((bf16[16,4,2,16,128]{4,3,2,1,0:T(8,128)(2,1)}), bf16[16,4,2,16,128]{4,3,2,1,0:T(8,128)(2,1)S(1)}, u32[]{:S(2)}, u32[]{:S(2)}) async-start(bf16[16,4,2,16,128]{4,3,2,1,0:T(8,128)(2,1)} %pad_maximum_fusion.1), calls=%async_computation.1 | async-start | bytes 1048576 | tf_op jit(solution)/shard_map/all_to_all | solution.py:196
  36.4 15.5 %collective-permute-start.3 = (bf16[256,512]{1,0:T(8,128)(2,1)S(1)}, bf16[256,512]{1,0:T(8,128)(2,1)S(1)}, u32[]{:S(2)}, u32[]{:S(2)}) collective-permute-start(bf16[256,512]{1,0:T(8,128)(2,1)S(1)} %bitcast.17), channel_id=1, source_target_pairs={{192,0},{224,32},{0,64},{32,96},{64,128},{96,160},{128,192},{160,2... | collective-permute-start | bytes 786440 | tf_op jit(solution)/shard_map/ppermute | solution.py:209
  40.2 11.7 %collective-permute-start.2 = (bf16[256,512]{1,0:T(8,128)(2,1)S(1)}, bf16[256,512]{1,0:T(8,128)(2,1)S(1)}, u32[]{:S(2)}, u32[]{:S(2)}) collective-permute-start(bf16[256,512]{1,0:T(8,128)(2,1)S(1)} %bitcast.18), channel_id=1, source_target_pairs={{0,256},{32,288},{64,320},{96,352},{128,384},{160,416},{192,448},{... | collective-permute-start | bytes 786440 | tf_op jit(solution)/shard_map/ppermute | solution.py:230
  43.6 9.7 %collective-permute-start.1 = (bf16[256,512]{1,0:T(8,128)(2,1)S(1)}, bf16[256,512]{1,0:T(8,128)(2,1)S(1)}, u32[]{:S(2)}, u32[]{:S(2)}) collective-permute-start(bf16[256,512]{1,0:T(8,128)(2,1)S(1)} %bitcast.19), channel_id=1, source_target_pairs={{64,0},{96,32},{128,64},{160,96},{192,128},{224,160},{0,192},{32,2... | collective-permute-start | bytes 786440 | tf_op jit(solution)/shard_map/ppermute | solution.py:209
  53.4 34.7 %collective-permute-start.4 = (bf16[4,256,512]{2,1,0:T(8,128)(2,1)S(1)}, bf16[4,256,512]{2,1,0:T(8,128)(2,1)}, u32[]{:S(2)}, u32[]{:S(2)}) collective-permute-start(bf16[4,256,512]{2,1,0:T(8,128)(2,1)S(1)} %pad_maximum_fusion.mine), channel_id=1, source_target_pairs={{0,32},{32,0},{64,96},{96,64},{128,160},{160,128},{192,224},{224,1... | collective-permute-start | bytes 3145736 | tf_op jit(solution)/shard_map/ppermute | solution.py:232
  55.3 1.0 copy-start.1
  88.1 1.2 %copy-start.2 = (bf16[4,256,512]{2,1,0:T(8,128)(2,1)S(1)}, bf16[4,256,512]{2,1,0:T(8,128)(2,1)}, u32[]{:S(2)}) copy-start(bf16[4,256,512]{2,1,0:T(8,128)(2,1)} %copy-done.1) | copy-start | bytes 3145732

commit v9 on v8

--- a/solution.py
+++ b/solution.py
@@ -38,10 +38,14 @@
     side = math.isqrt(n_dom)
     gx, gy = side * cx, side * cy
     centre, first_scale, weights = filter_weights(DEG)
-    row_stride = n_dom * n_own
+    row_stride = n_dom // 2 * n_own
+    rows_out = cx * cy * row_stride
     far_near = coef_two / coef_one
 
-    def body(blocks, out, first, second, diag, ordered):
+    def body(blocks, out, away, first, second, diag, ordered):
+        core, _ = chip_place(side)
+        starts = [lax.bitwise_xor(core, c) * rows_out for c in (0, 1)]
+
         for x in range(gx):
             for j in range(side):
                 dom, inner = x // cx * side + j, x % cx
@@ -111,8 +115,9 @@
 
         def last(band, x, y, value):
             value = value * scale_h - scale_x * previous[band, x, PAD + y : PAD + y + 8, :]
-            dom = x // cx * side + y // cy
-            base = (x % cx * cy + y % cy) * row_stride + dom * n_own + band
+            pair = (x // cx * side + y // cy) // 2
+            base = (x % cx * cy + y % cy) * row_stride + pair * n_own + band
+            base = base + starts[y // cy % 2]
             ordered[pl.ds(base, 8, stride=row_stride), :] = value
 
         sweep(current, last)
@@ -121,22 +126,24 @@
         def store(n, carry):
             at = pl.multiple_of(n * block, block)
             out[pl.ds(at, block), :] = ordered[pl.ds(at, block), :].astype(jnp.bfloat16)
+            far = ordered[pl.ds(rows_out + at, block), :]
+            away[pl.ds(at, block), :] = far.astype(jnp.bfloat16)
             return carry
 
         lax.fori_loop(0, out.shape[0] // block, store, 0)
 
     padded = pltpu.VMEM((n_own, gx, gy + 2 * PAD, nz), jnp.float32)
-    rows_out = cx * cy * n_dom * n_own
+    vmem = pl.BlockSpec(memory_space=pltpu.VMEM)
     return pl.pallas_call(
         body,
-        out_shape=pltpu.VMEM((rows_out, nz), jnp.bfloat16),
-        in_specs=[pl.BlockSpec(memory_space=pltpu.VMEM)],
-        out_specs=pl.BlockSpec(memory_space=pltpu.VMEM),
+        out_shape=[pltpu.VMEM((rows_out, nz), jnp.bfloat16)] * 2,
+        in_specs=[vmem],
+        out_specs=[vmem, vmem],
         scratch_shapes=[
             padded,
             padded,
             pltpu.VMEM((gx, gy, nz), jnp.float32),
-            pltpu.VMEM((rows_out, nz), jnp.float32),
+            pltpu.VMEM((2 * rows_out, nz), jnp.float32),
         ],
         name="chebyshev",
     )
@@ -194,7 +201,7 @@
     blocks = orbitals.reshape(n_dom, n_own, cx, cy, nz)
     blocks = jnp.concatenate([blocks, parts], axis=1)
     blocks = lax.all_to_all(blocks, "dom", 0, 0, tiled=True)
-    filtered = filter_kernel(n_dom, n_own, cx, cy, nz)(in_vmem(blocks))
+    kept, away = filter_kernel(n_dom, n_own, cx, cy, nz)(in_vmem(blocks))
 
     half = n_all // 2
 
@@ -231,8 +238,19 @@
     mine = jnp.stack([own, after, far, before])
     other = lax.ppermute(mine, "dom", [(d, d ^ 1) for d in range(n_dom)])
 
+    swapped = [(d, d ^ 1) for d in range(n_dom)]
+    away = lax.ppermute(away, "dom", swapped)
+    n_pair = n_dom // 2
+    kept = kept.reshape(n_band * n_pair, n_own, nz)
+    away = away.reshape(n_band * n_pair, n_own, nz)
+    rows = lax.select(
+        jnp.broadcast_to(core == 0, (n_band * n_pair, 2 * n_own, nz)),
+        jnp.concatenate([kept, away], axis=1),
+        jnp.concatenate([away, kept], axis=1),
+    )
+    group = [[b * n_dom + 2 * p + c for b in range(n_band) for p in range(n_pair)] for c in (0, 1)]
     rows = lax.all_to_all(
-        filtered.reshape(n_band * n_dom, n_own, nz), ("band", "dom"), 0, 0, tiled=True
+        rows, ("band", "dom"), 0, 0, tiled=True, axis_index_groups=group
     ).reshape(n_all, nz)
 
     rotated = rotate_kernel(n_all, n_x, nz)(in_vmem(mine), in_vmem(other), in_vmem(rows))

time: 113 us -> 115 us (1.018)
  starting transfers between devices: 36.5 us -> 38.8 us
  local copies, waits for them, and re-layouts: 5.81 us -> 3.6 us
  other arithmetic: 1.03 us -> 2.49 us
    ppermute x0 -> x1, starting transfers between devices: none -> 2.41 us  [on_device(): away = lax.ppermute(away, 'dom', swapped)]
    unnamed x10 -> x6, local copies, waits for them, and re-layouts: 3.93 us -> 1.72 us
    all_to_all x1, blocking collectives: 19.9 us -> 18.4 us  [on_device(): lax.all_to_all(rotated.reshape(n_band, n_mine, nz), 'band', 0, 0, tiled=T...]
  transfers between devices with their start and end apart: 7 -> 8, of which waited for: 4 -> 5; matrix products, arithmetic and copies ran while one was open for 1% -> 2% of each run, Pallas kernels for 3% -> 2%
where the time goes in v9:
time: 115 us; the launch traced here: 114 us
  blocking collectives  47.9 us (42%)
  starting transfers between devices  38.8 us (34%)
  waiting for transfers between devices  16.3 us (14%)
  Pallas kernels  5.09 us (4%)
  local copies, waits for them, and re-layouts  3.6 us (3%)
  other arithmetic  2.49 us (2%)
    all_to_all x1, blocking collectives, on_device(): lax.all_to_all(rows, ('band', 'dom'), 0, 0, tiled=True, axis_index_groups...  29.5 us
    all_to_all x1, blocking collectives, on_device(): lax.all_to_all(rotated.reshape(n_band, n_mine, nz), 'band', 0, 0, tiled=T...  18.4 us
    ppermute x1, starting transfers between devices, on_device(): own = lax.ppermute(own, ('dom', 'band'), turned)  10.9 us
    all_to_all x1, waiting for transfers between devices, on_device(): lax.all_to_all(many, 'band', 0, 0, tiled=True, axis_index_groups=lines)  7.77 us
    all_to_all x1, starting transfers between devices, on_device(): lax.all_to_all(many, 'band', 0, 0, tiled=True, axis_index_groups=lines)  7.68 us
    ppermute x2, starting transfers between devices, from_x(): return lax.ppermute(value, 'dom', pairs)  7.5 us
    ppermute x2, waiting for transfers between devices, from_x(): return lax.ppermute(value, 'dom', pairs)  5.97 us
    all_to_all x1, starting transfers between devices, on_device(): blocks = lax.all_to_all(blocks, 'dom', 0, 0, tiled=True)  5.06 us
  transfers between devices with their start and end apart: 8, of which 5 were waited for; matrix products, arithmetic and copies ran while one was open for 2% of the time, Pallas kernels for 2%

profile of v9, /device:TPU:8, one launch (start us, length us, event | category | flops | bytes accessed | tf_op | source)
XLA Modules:
  0.0 114.4 jit_solution(2023001255435780096)
XLA Ops:
  0.0 0.0 copy-start
  0.0 0.8 copy-done
  0.8 10.9 %collective-permute-start = (bf16[32,512]{1,0:T(8,128)(2,1)S(1)}, bf16[32,512]{1,0:T(8,128)(2,1)S(1)}, u32[]{:S(2)}, u32[]{:S(2)}) collective-permute-start(bf16[32,512]{1,0:T(8,128)(2,1)S(1)} %dynamic-slice_bitcast_fusion), channel_id=1, source_target_pairs={{256,0},{257,1},{258,2},{259,3},{260,4},{261,5},{262,6},{263,7},{2... | collective-permute-start | bytes 98312 | tf_op jit(solution)/shard_map/ppermute | solution.py:229
  11.8 1.6 %collective-permute-done = bf16[32,512]{1,0:T(8,128)(2,1)S(1)} collective-permute-done((bf16[32,512]{1,0:T(8,128)(2,1)S(1)}, bf16[32,512]{1,0:T(8,128)(2,1)S(1)}, u32[]{:S(2)}, u32[]{:S(2)}) %collective-permute-start) | collective-permute-done | bytes 32800 | tf_op jit(solution)/shard_map/ppermute | solution.py:229
  13.3 0.7 broadcast_in_dim.6
  14.1 0.0 copy-start.2
  14.1 7.7 %all-to-all-start = ((bf16[8,32,512]{2,1,0:T(8,128)(2,1)}), bf16[8,32,512]{2,1,0:T(8,128)(2,1)S(1)}, u32[]{:S(2)}, u32[]{:S(2)}) async-start(bf16[8,32,512]{2,1,0:T(8,128)(2,1)} %broadcast_in_dim.6), calls=%async_computation | async-start | bytes 524288 | tf_op jit(solution)/shard_map/all_to_all | solution.py:232
  21.8 0.0 copy-done.2
  21.8 0.0 copy-start.1
  21.8 0.9 copy-done.1
  22.7 0.8 pad_maximum_fusion.1
  23.5 7.8 %all-to-all-done = bf16[8,32,512]{2,1,0:T(8,128)(2,1)S(1)} async-done(((bf16[8,32,512]{2,1,0:T(8,128)(2,1)}), bf16[8,32,512]{2,1,0:T(8,128)(2,1)S(1)}, u32[]{:S(2)}, u32[]{:S(2)}) %all-to-all-start) | async-done | bytes 262176 | tf_op jit(solution)/shard_map/all_to_all | solution.py:232
  31.3 5.1 %all-to-all-start.1 = ((bf16[16,4,2,16,128]{4,3,2,1,0:T(8,128)(2,1)}), bf16[16,4,2,16,128]{4,3,2,1,0:T(8,128)(2,1)S(1)}, u32[]{:S(2)}, u32[]{:S(2)}) async-start(bf16[16,4,2,16,128]{4,3,2,1,0:T(8,128)(2,1)} %pad_maximum_fusion.1), calls=%async_computation.1 | async-start | bytes 1048576 | tf_op jit(solution)/shard_map/all_to_all | solution.py:203
  36.4 3.8 %collective-permute-start.3 = (bf16[256,512]{1,0:T(8,128)(2,1)S(1)}, bf16[256,512]{1,0:T(8,128)(2,1)S(1)}, u32[]{:S(2)}, u32[]{:S(2)}) collective-permute-start(bf16[256,512]{1,0:T(8,128)(2,1)S(1)} %bitcast.18), channel_id=1, source_target_pairs={{192,0},{224,32},{0,64},{32,96},{64,128},{96,160},{128,192},{160,2... | collective-permute-start | bytes 786440 | tf_op jit(solution)/shard_map/ppermute | solution.py:216
  40.2 3.4 %collective-permute-start.2 = (bf16[256,512]{1,0:T(8,128)(2,1)S(1)}, bf16[256,512]{1,0:T(8,128)(2,1)S(1)}, u32[]{:S(2)}, u32[]{:S(2)}) collective-permute-start(bf16[256,512]{1,0:T(8,128)(2,1)S(1)} %bitcast.19), channel_id=1, source_target_pairs={{0,256},{32,288},{64,320},{96,352},{128,384},{160,416},{192,448},{... | collective-permute-start | bytes 786440 | tf_op jit(solution)/shard_map/ppermute | solution.py:237
  43.6 3.7 %collective-permute-start.1 = (bf16[256,512]{1,0:T(8,128)(2,1)S(1)}, bf16[256,512]{1,0:T(8,128)(2,1)S(1)}, u32[]{:S(2)}, u32[]{:S(2)}) collective-permute-start(bf16[256,512]{1,0:T(8,128)(2,1)S(1)} %bitcast.20), channel_id=1, source_target_pairs={{64,0},{96,32},{128,64},{160,96},{192,128},{224,160},{0,192},{32,2... | collective-permute-start | bytes 786440 | tf_op jit(solution)/shard_map/ppermute | solution.py:216
  47.3 4.6 %collective-permute-done.3 = bf16[256,512]{1,0:T(8,128)(2,1)S(1)} collective-permute-done((bf16[256,512]{1,0:T(8,128)(2,1)S(1)}, bf16[256,512]{1,0:T(8,128)(2,1)S(1)}, u32[]{:S(2)}, u32[]{:S(2)}) %collective-permute-start.3) | collective-permute-done | bytes 262176 | tf_op jit(solution)/shard_map/ppermute | solution.py:216
  51.9 0.0 collective-permute-done.2
  51.9 1.3 %collective-permute-done.1 = bf16[256,512]{1,0:T(8,128)(2,1)S(1)} collective-permute-done((bf16[256,512]{1,0:T(8,128)(2,1)S(1)}, bf16[256,512]{1,0:T(8,128)(2,1)S(1)}, u32[]{:S(2)}, u32[]{:S(2)}) %collective-permute-start.1) | collective-permute-done | bytes 262176 | tf_op jit(solution)/shard_map/ppermute | solution.py:216
  53.3 1.1 pad_maximum_fusion.mine
  54.4 1.9 %collective-permute-start.4 = (bf16[4,256,512]{2,1,0:T(8,128)(2,1)}, bf16[4,256,512]{2,1,0:T(8,128)(2,1)}, u32[]{:S(2)}, u32[]{:S(2)}) collective-permute-start(bf16[4,256,512]{2,1,0:T(8,128)(2,1)} %pad_maximum_fusion.mine), channel_id=1, source_target_pairs={{0,32},{32,0},{64,96},{96,64},{128,160},{160,128},{192,224},{224,1... | collective-permute-start | bytes 3145736 | tf_op jit(solution)/shard_map/ppermute | solution.py:239
  56.3 0.0 all-to-all-done.1.blocks
  56.3 2.9 %chebyshev.1 = (bf16[512,128]{1,0:T(8,128)(2,1)S(1)}, bf16[512,128]{1,0:T(8,128)(2,1)S(1)}) custom-call(bf16[16,4,2,16,128]{4,3,2,1,0:T(8,128)(2,1)S(1)} %all-to-all-done.1.blocks), custom_call_target="tpu_custom_call" | custom-call | tf_op jit(solution)/shard_map/chebyshev/pallas_call | solution.py:204
  59.2 2.4 %collective-permute-start.5 = (bf16[512,128]{1,0:T(8,128)(2,1)S(1)}, bf16[512,128]{1,0:T(8,128)(2,1)S(1)}, u32[]{:S(2)}, u32[]{:S(2)}) collective-permute-start(bf16[512,128]{1,0:T(8,128)(2,1)S(1)} %get-tuple-element.8), channel_id=1, source_target_pairs={{0,32},{32,0},{64,96},{96,64},{128,160},{160,128},{192,224},{224,1... | collective-permute-start | bytes 393224 | tf_op jit(solution)/shard_map/ppermute | solution.py:242
  61.6 1.0 collective-permute-done.5
  62.5 0.5 maximum_select_fusion
  63.0 29.5 %all_to_all.20 = bf16[256,4,128]{2,1,0:T(4,128)(2,1)S(1)} all-to-all(bf16[256,4,128]{2,1,0:T(4,128)(2,1)S(1)} %maximum_select_fusion), channel_id=1, replica_groups={{0,64,128,192,256,320,384,448,1,65,129,193,257,321,385,449,2,66,130,194..., dimensions={0} | all-to-all | bytes 524288 | tf_op jit(solution)/shard_map/all_to_all | solution.py:252
  92.6 0.0 collective-permute-done.4.other
  92.6 2.2 %rotate.1 = bf16[1024,128]{1,0:T(8,128)(2,1)S(1)} custom-call(bf16[4,256,512]{2,1,0:T(8,128)(2,1)} %pad_maximum_fusion.mine, bf16[4,256,512]{2,1,0:T(8,128)(2,1)} %collective-permute-done.4.other, bf16[1024,128]{1,0:T(8,128)(2,1)S(1)} %bitcast.15), custom_call_target="tpu_custom_call" | custom-call | tf_op jit(solution)/shard_map/rotate/pallas_call | solution.py:256
  94.8 18.4 %all_to_all.21 = bf16[32,32,128]{2,1,0:T(8,128)(2,1)S(1)} all-to-all(bf16[32,32,128]{2,1,0:T(8,128)(2,1)S(1)} %bitcast.16), channel_id=1, replica_groups=mesh['dom'=16,'band'=32] {'band'}, dimensions={0} | all-to-all | bytes 524288 | tf_op jit(solution)/shard_map/all_to_all | solution.py:257
  113.2 0.1 convert_bitcast_fusion
  113.3 1.1 copy.4
  (4 shorter events, 0.1 us)
Async XLA Ops:
  0.0 0.8 copy-start
  0.8 12.5 %collective-permute-start = (bf16[32,512]{1,0:T(8,128)(2,1)S(1)}, bf16[32,512]{1,0:T(8,128)(2,1)S(1)}, u32[]{:S(2)}, u32[]{:S(2)}) collective-permute-start(bf16[32,512]{1,0:T(8,128)(2,1)S(1)} %dynamic-slice_bitcast_fusion), channel_id=1, source_target_pairs={{256,0},{257,1},{258,2},{259,3},{260,4},{261,5},{262,6},{263,7},{2... | collective-permute-start | bytes 98312 | tf_op jit(solution)/shard_map/ppermute | solution.py:229
  14.1 7.7 %copy-start.2 = (f32[1,2,16,128]{3,2,1,0:T(8,128)S(1)}, f32[1,2,16,128]{3,2,1,0:T(8,128)}, u32[]{:S(2)}) copy-start(f32[1,2,16,128]{3,2,1,0:T(8,128)} %param.4) | copy-start | bytes 49156
  14.1 17.2 %all-to-all-start = ((bf16[8,32,512]{2,1,0:T(8,128)(2,1)}), bf16[8,32,512]{2,1,0:T(8,128)(2,1)S(1)}, u32[]{:S(2)}, u32[]{:S(2)}) async-start(bf16[8,32,512]{2,1,0:T(8,128)(2,1)} %broadcast_in_dim.6), calls=%async_computation | async-start | bytes 524288 | tf_op jit(solution)/shard_map/all_to_all | solution.py:232
  21.8 1.0 copy-start.1
  31.3 25.0 %all-to-all-start.1 = ((bf16[16,4,2,16,128]{4,3,2,1,0:T(8,128)(2,1)}), bf16[16,4,2,16,128]{4,3,2,1,0:T(8,128)(2,1)S(1)}, u32[]{:S(2)}, u32[]{:S(2)}) async-start(bf16[16,4,2,16,128]{4,3,2,1,0:T(8,128)(2,1)} %pad_maximum_fusion.1), calls=%async_computation.1 | async-start | bytes 1048576 | tf_op jit(solution)/shard_map/all_to_all | solution.py:203
  36.4 15.5 %collective-permute-start.3 = (bf16[256,512]{1,0:T(8,128)(2,1)S(1)}, bf16[256,512]{1,0:T(8,128)(2,1)S(1)}, u32[]{:S(2)}, u32[]{:S(2)}) collective-permute-start(bf16[256,512]{1,0:T(8,128)(2,1)S(1)} %bitcast.18), channel_id=1, source_target_pairs={{192,0},{224,32},{0,64},{32,96},{64,128},{96,160},{128,192},{160,2... | collective-permute-start | bytes 786440 | tf_op jit(solution)/shard_map/ppermute | solution.py:216
  40.2 11.7 %collective-permute-start.2 = (bf16[256,512]{1,0:T(8,128)(2,1)S(1)}, bf16[256,512]{1,0:T(8,128)(2,1)S(1)}, u32[]{:S(2)}, u32[]{:S(2)}) collective-permute-start(bf16[256,512]{1,0:T(8,128)(2,1)S(1)} %bitcast.19), channel_id=1, source_target_pairs={{0,256},{32,288},{64,320},{96,352},{128,384},{160,416},{192,448},{... | collective-permute-start | bytes 786440 | tf_op jit(solution)/shard_map/ppermute | solution.py:237
  43.6 9.7 %collective-permute-start.1 = (bf16[256,512]{1,0:T(8,128)(2,1)S(1)}, bf16[256,512]{1,0:T(8,128)(2,1)S(1)}, u32[]{:S(2)}, u32[]{:S(2)}) collective-permute-start(bf16[256,512]{1,0:T(8,128)(2,1)S(1)} %bitcast.20), channel_id=1, source_target_pairs={{64,0},{96,32},{128,64},{160,96},{192,128},{224,160},{0,192},{32,2... | collective-permute-start | bytes 786440 | tf_op jit(solution)/shard_map/ppermute | solution.py:216
  54.4 38.2 %collective-permute-start.4 = (bf16[4,256,512]{2,1,0:T(8,128)(2,1)}, bf16[4,256,512]{2,1,0:T(8,128)(2,1)}, u32[]{:S(2)}, u32[]{:S(2)}) collective-permute-start(bf16[4,256,512]{2,1,0:T(8,128)(2,1)} %pad_maximum_fusion.mine), channel_id=1, source_target_pairs={{0,32},{32,0},{64,96},{96,64},{128,160},{160,128},{192,224},{224,1... | collective-permute-start | bytes 3145736 | tf_op jit(solution)/shard_map/ppermute | solution.py:239
  59.2 3.4 %collective-permute-start.5 = (bf16[512,128]{1,0:T(8,128)(2,1)S(1)}, bf16[512,128]{1,0:T(8,128)(2,1)S(1)}, u32[]{:S(2)}, u32[]{:S(2)}) collective-permute-start(bf16[512,128]{1,0:T(8,128)(2,1)S(1)} %get-tuple-element.8), channel_id=1, source_target_pairs={{0,32},{32,0},{64,96},{96,64},{128,160},{160,128},{192,224},{224,1... | collective-permute-start | bytes 393224 | tf_op jit(solution)/shard_map/ppermute | solution.py:242

commit v10 on v9

--- a/solution.py
+++ b/solution.py
@@ -149,6 +149,55 @@
     )
 
 
+def pack_kernel(n_dom, n_own, cx, cy, nz):
+    def body(bands, pot, out, parts, sems):
+        copies = [pltpu.make_async_copy(bands, out.at[:, 0:n_own], sems.at[n_dom])]
+        copies[0].start()
+        value = pot[...]
+        high = value.astype(jnp.bfloat16)
+        parts[0] = high
+        parts[1] = (value - high.astype(jnp.float32)).astype(jnp.bfloat16)
+        for d in range(n_dom):
+            copies.append(
+                pltpu.make_async_copy(parts, out.at[d, n_own : n_own + 2], sems.at[d])
+            )
+            copies[-1].start()
+        for copy in copies:
+            copy.wait()
+
+    return pl.pallas_call(
+        body,
+        out_shape=jax.ShapeDtypeStruct((n_dom, n_own + 2, cx, cy, nz), jnp.bfloat16),
+        in_specs=[pl.BlockSpec(memory_space=pl.ANY), pl.BlockSpec(memory_space=pltpu.VMEM)],
+        out_specs=pl.BlockSpec(memory_space=pl.ANY),
+        scratch_shapes=[
+            pltpu.VMEM((2, cx, cy, nz), jnp.bfloat16),
+            pltpu.SemaphoreType.DMA((n_dom + 1,)),
+        ],
+        name="pack",
+    )
+
+
+def unpack_kernel(n_line, n_mine, nz):
+    block = n_mine // 2
+
+    def body(lines, out):
+        first = pl.multiple_of(pl.program_id(0) * block, block)
+        for line in range(n_line):
+            value = lines[line, pl.ds(first, block), :].astype(jnp.float32)
+            for at in range(0, block, 8):
+                out[pl.ds(at * n_line + line, 8, stride=n_line), :] = value[at : at + 8]
+
+    return pl.pallas_call(
+        body,
+        grid=(n_mine // block,),
+        out_shape=jax.ShapeDtypeStruct((n_mine * n_line, nz), jnp.float32),
+        in_specs=[pl.BlockSpec(memory_space=pltpu.VMEM)],
+        out_specs=pl.BlockSpec((block * n_line, nz), lambda i: (i, 0)),
+        name="unpack",
+    )
+
+
 def rotate_kernel(n_all, n_x, nz):
     half, block = n_all // 2, n_all // n_x
 
@@ -194,12 +243,9 @@
     n_y = n_band // n_x
     core, _ = chip_place(n_x)
 
-    pot = potential[0]
-    high = lax.reduce_precision(pot, 8, 7)
-    parts = jnp.stack([high, pot - high]).astype(jnp.bfloat16)
-    parts = jnp.broadcast_to(parts[None], (n_dom, 2, cx, cy, nz))
-    blocks = orbitals.reshape(n_dom, n_own, cx, cy, nz)
-    blocks = jnp.concatenate([blocks, parts], axis=1)
+    blocks = pack_kernel(n_dom, n_own, cx, cy, nz)(
+        orbitals.reshape(n_dom, n_own, cx, cy, nz), potential[0]
+    )
     blocks = lax.all_to_all(blocks, "dom", 0, 0, tiled=True)
     kept, away = filter_kernel(n_dom, n_own, cx, cy, nz)(in_vmem(blocks))
 
@@ -243,11 +289,8 @@
     n_pair = n_dom // 2
     kept = kept.reshape(n_band * n_pair, n_own, nz)
     away = away.reshape(n_band * n_pair, n_own, nz)
-    rows = lax.select(
-        jnp.broadcast_to(core == 0, (n_band * n_pair, 2 * n_own, nz)),
-        jnp.concatenate([kept, away], axis=1),
-        jnp.concatenate([away, kept], axis=1),
-    )
+    lower = jnp.broadcast_to(core == 0, kept.shape)
+    rows = jnp.stack([lax.select(lower, kept, away), lax.select(lower, away, kept)], axis=1)
     group = [[b * n_dom + 2 * p + c for b in range(n_band) for p in range(n_pair)] for c in (0, 1)]
     rows = lax.all_to_all(
         rows, ("band", "dom"), 0, 0, tiled=True, axis_index_groups=group
@@ -255,7 +298,7 @@
 
     rotated = rotate_kernel(n_all, n_x, nz)(in_vmem(mine), in_vmem(other), in_vmem(rows))
     rotated = lax.all_to_all(rotated.reshape(n_band, n_mine, nz), "band", 0, 0, tiled=True)
-    rotated = rotated.transpose(1, 0, 2).astype(jnp.float32)
+    rotated = unpack_kernel(n_band, n_mine, nz)(in_vmem(rotated))
     return rotated.reshape(orbitals.shape)
 
 

time: 115 us -> 119 us (1.035)
  Pallas kernels: 5.09 us -> 15.9 us
  waiting for transfers between devices: 16.3 us -> 8.51 us
  blocking collectives: 47.9 us -> 52.2 us
  other arithmetic: 2.49 us -> 0.53 us
    pallas_call x0 -> x2, Pallas kernels: none -> 11.1 us  [the longest x1 9.93 us: on_device(): pack_kernel(n_dom, n_own, cx, cy, nz)]
    all_to_all x1, waiting for transfers between devices: 7.77 us -> 0.01 us  [on_device(): lax.all_to_all(many, 'band', 0, 0, tiled=True, axis_index_groups=lines)]
    all_to_all x1, blocking collectives: 29.5 us -> 33.8 us  [on_device(): lax.all_to_all(rows, ('band', 'dom'), 0, 0, tiled=True, axis_index_groups...]
  transfers between devices with their start and end apart: 8 -> 8, of which waited for: 5 -> 4; matrix products, arithmetic and copies ran while one was open for 2% -> 0% of each run, Pallas kernels for 2% -> 11%
where the time goes in v10:
time: 119 us
  blocking collectives  52.2 us (44%)
  starting transfers between devices  38.7 us (33%)
  Pallas kernels  15.9 us (13%)
  waiting for transfers between devices  8.51 us (7%)
  local copies, waits for them, and re-layouts  2.8 us (2%)
    all_to_all x1, blocking collectives, on_device(): lax.all_to_all(rows, ('band', 'dom'), 0, 0, tiled=True, axis_index_groups...  33.8 us
    all_to_all x1, blocking collectives, on_device(): lax.all_to_all(rotated.reshape(n_band, n_mine, nz), 'band', 0, 0, tiled=T...  18.4 us
    ppermute x1, starting transfers between devices, on_device(): own = lax.ppermute(own, ('dom', 'band'), turned)  10.9 us
    pallas_call x1, Pallas kernels, on_device(): pack_kernel(n_dom, n_own, cx, cy, nz)  9.93 us
    all_to_all x1, starting transfers between devices, on_device(): lax.all_to_all(many, 'band', 0, 0, tiled=True, axis_index_groups=lines)  7.55 us
    ppermute x2, starting transfers between devices, from_x(): return lax.ppermute(value, 'dom', pairs)  7.5 us
    ppermute x2, waiting for transfers between devices, from_x(): return lax.ppermute(value, 'dom', pairs)  5.97 us
    all_to_all x1, starting transfers between devices, on_device(): blocks = lax.all_to_all(blocks, 'dom', 0, 0, tiled=True)  5.07 us
  transfers between devices with their start and end apart: 8, of which 4 were waited for; matrix products, arithmetic and copies ran while one was open for 0% of the time, Pallas kernels for 11%

profile of v10, /device:TPU:8, one launch (start us, length us, event | category | flops | bytes accessed | tf_op | source)
XLA Modules:
  0.0 118.7 jit_solution(15159083761202171152)
XLA Ops:
  0.0 0.0 copy-start
  0.0 0.8 copy-done
  0.8 10.9 %collective-permute-start = (bf16[32,512]{1,0:T(8,128)(2,1)S(1)}, bf16[32,512]{1,0:T(8,128)(2,1)S(1)}, u32[]{:S(2)}, u32[]{:S(2)}) collective-permute-start(bf16[32,512]{1,0:T(8,128)(2,1)S(1)} %dynamic-slice_bitcast_fusion), channel_id=1, source_target_pairs={{256,0},{257,1},{258,2},{259,3},{260,4},{261,5},{262,6},{263,7},{2... | collective-permute-start | bytes 98312 | tf_op jit(solution)/shard_map/ppermute | solution.py:275
  11.8 1.6 %collective-permute-done = bf16[32,512]{1,0:T(8,128)(2,1)S(1)} collective-permute-done((bf16[32,512]{1,0:T(8,128)(2,1)S(1)}, bf16[32,512]{1,0:T(8,128)(2,1)S(1)}, u32[]{:S(2)}, u32[]{:S(2)}) %collective-permute-start) | collective-permute-done | bytes 32800 | tf_op jit(solution)/shard_map/ppermute | solution.py:275
  13.3 0.7 broadcast_in_dim.4
  14.1 7.5 %all-to-all-start = ((bf16[8,32,512]{2,1,0:T(8,128)(2,1)}), bf16[8,32,512]{2,1,0:T(8,128)(2,1)S(1)}, u32[]{:S(2)}, u32[]{:S(2)}) async-start(bf16[8,32,512]{2,1,0:T(8,128)(2,1)} %broadcast_in_dim.4), calls=%async_computation | async-start | bytes 524288 | tf_op jit(solution)/shard_map/all_to_all | solution.py:278
  21.6 9.9 %pack.1 = bf16[16,4,2,16,128]{4,3,2,1,0:T(8,128)(2,1)} custom-call(bf16[16,2,2,16,128]{4,3,2,1,0:T(8,128)(2,1)} %bitcast.28, f32[2,16,128]{2,1,0:T(8,128)} %bitcast.32), custom_call_target="tpu_custom_call" | custom-call | tf_op jit(solution)/shard_map/pack/pallas_call | solution.py:246
  31.6 0.0 all-to-all-done
  31.6 5.1 %all-to-all-start.1 = ((bf16[16,4,2,16,128]{4,3,2,1,0:T(8,128)(2,1)}), bf16[16,4,2,16,128]{4,3,2,1,0:T(8,128)(2,1)S(1)}, u32[]{:S(2)}, u32[]{:S(2)}) async-start(bf16[16,4,2,16,128]{4,3,2,1,0:T(8,128)(2,1)} %pack.1), calls=%async_computation.1 | async-start | bytes 1048576 | tf_op jit(solution)/shard_map/all_to_all | solution.py:249
  36.6 3.8 %collective-permute-start.3 = (bf16[256,512]{1,0:T(8,128)(2,1)S(1)}, bf16[256,512]{1,0:T(8,128)(2,1)S(1)}, u32[]{:S(2)}, u32[]{:S(2)}) collective-permute-start(bf16[256,512]{1,0:T(8,128)(2,1)S(1)} %bitcast.22), channel_id=1, source_target_pairs={{192,0},{224,32},{0,64},{32,96},{64,128},{96,160},{128,192},{160,2... | collective-permute-start | bytes 786440 | tf_op jit(solution)/shard_map/ppermute | solution.py:262
  40.5 3.4 %collective-permute-start.2 = (bf16[256,512]{1,0:T(8,128)(2,1)S(1)}, bf16[256,512]{1,0:T(8,128)(2,1)S(1)}, u32[]{:S(2)}, u32[]{:S(2)}) collective-permute-start(bf16[256,512]{1,0:T(8,128)(2,1)S(1)} %bitcast.23), channel_id=1, source_target_pairs={{0,256},{32,288},{64,320},{96,352},{128,384},{160,416},{192,448},{... | collective-permute-start | bytes 786440 | tf_op jit(solution)/shard_map/ppermute | solution.py:283
  43.9 3.7 %collective-permute-start.1 = (bf16[256,512]{1,0:T(8,128)(2,1)S(1)}, bf16[256,512]{1,0:T(8,128)(2,1)S(1)}, u32[]{:S(2)}, u32[]{:S(2)}) collective-permute-start(bf16[256,512]{1,0:T(8,128)(2,1)S(1)} %bitcast.24), channel_id=1, source_target_pairs={{64,0},{96,32},{128,64},{160,96},{192,128},{224,160},{0,192},{32,2... | collective-permute-start | bytes 786440 | tf_op jit(solution)/shard_map/ppermute | solution.py:262
  47.5 4.6 %collective-permute-done.3 = bf16[256,512]{1,0:T(8,128)(2,1)S(1)} collective-permute-done((bf16[256,512]{1,0:T(8,128)(2,1)S(1)}, bf16[256,512]{1,0:T(8,128)(2,1)S(1)}, u32[]{:S(2)}, u32[]{:S(2)}) %collective-permute-start.3) | collective-permute-done | bytes 262176 | tf_op jit(solution)/shard_map/ppermute | solution.py:262
  52.2 0.0 collective-permute-done.2
  52.2 1.3 %collective-permute-done.1 = bf16[256,512]{1,0:T(8,128)(2,1)S(1)} collective-permute-done((bf16[256,512]{1,0:T(8,128)(2,1)S(1)}, bf16[256,512]{1,0:T(8,128)(2,1)S(1)}, u32[]{:S(2)}, u32[]{:S(2)}) %collective-permute-start.1) | collective-permute-done | bytes 262176 | tf_op jit(solution)/shard_map/ppermute | solution.py:262
  53.5 0.1 pad_maximum_fusion.mine
  53.7 0.0 copy-start.1
  53.7 1.9 %collective-permute-start.4 = (bf16[4,256,512]{2,1,0:T(8,128)(2,1)S(1)}, bf16[4,256,512]{2,1,0:T(8,128)(2,1)}, u32[]{:S(2)}, u32[]{:S(2)}) collective-permute-start(bf16[4,256,512]{2,1,0:T(8,128)(2,1)S(1)} %pad_maximum_fusion.mine), channel_id=1, source_target_pairs={{0,32},{32,0},{64,96},{96,64},{128,160},{160,128},{192,224},{224,1... | collective-permute-start | bytes 3145736 | tf_op jit(solution)/shard_map/ppermute | solution.py:285
  55.6 0.0 all-to-all-done.1.blocks
  55.6 2.9 %chebyshev.1 = (bf16[512,128]{1,0:T(8,128)(2,1)S(1)}, bf16[512,128]{1,0:T(8,128)(2,1)S(1)}) custom-call(bf16[16,4,2,16,128]{4,3,2,1,0:T(8,128)(2,1)S(1)} %all-to-all-done.1.blocks), custom_call_target="tpu_custom_call" | custom-call | tf_op jit(solution)/shard_map/chebyshev/pallas_call | solution.py:250
  58.5 2.4 %collective-permute-start.5 = (bf16[512,128]{1,0:T(8,128)(2,1)S(1)}, bf16[512,128]{1,0:T(8,128)(2,1)S(1)}, u32[]{:S(2)}, u32[]{:S(2)}) collective-permute-start(bf16[512,128]{1,0:T(8,128)(2,1)S(1)} %get-tuple-element.8), channel_id=1, source_target_pairs={{0,32},{32,0},{64,96},{96,64},{128,160},{160,128},{192,224},{224,1... | collective-permute-start | bytes 393224 | tf_op jit(solution)/shard_map/ppermute | solution.py:288
  60.9 1.0 collective-permute-done.5
  61.9 0.4 pad_maximum_fusion.1
  62.3 33.8 %all_to_all.20 = bf16[256,2,2,128]{3,2,1,0:T(2,128)(2,1)S(1)} all-to-all(bf16[256,2,2,128]{3,2,1,0:T(2,128)(2,1)S(1)} %pad_maximum_fusion.1), channel_id=1, replica_groups={{0,64,128,192,256,320,384,448,1,65,129,193,257,321,385,449,2,66,130,194..., dimensions={0} | all-to-all | bytes 524288 | tf_op jit(solution)/shard_map/all_to_all | solution.py:295
  96.0 0.0 copy-done.1
  96.0 0.0 collective-permute-done.4.other
  96.0 0.0 copy-start.2
  96.0 1.2 %copy-done.2 = bf16[4,256,512]{2,1,0:T(8,128)(2,1)S(1)} copy-done((bf16[4,256,512]{2,1,0:T(8,128)(2,1)S(1)}, bf16[4,256,512]{2,1,0:T(8,128)(2,1)}, u32[]{:S(2)}) %copy-start.2) | copy-done | bytes 1048600
  97.2 1.9 %rotate.1 = bf16[1024,128]{1,0:T(8,128)(2,1)S(1)} custom-call(bf16[4,256,512]{2,1,0:T(8,128)(2,1)S(1)} %copy-done.2, bf16[4,256,512]{2,1,0:T(8,128)(2,1)} %collective-permute-done.4.other, bf16[1024,128]{1,0:T(8,128)(2,1)S(1)} %bitcast.20), custom_call_target="tpu_custom_call" | custom-call | tf_op jit(solution)/shard_map/rotate/pallas_call | solution.py:299
  99.2 18.4 %all_to_all.21.lines = bf16[32,32,128]{2,1,0:T(8,128)(2,1)S(1)} all-to-all(bf16[32,32,128]{2,1,0:T(8,128)(2,1)S(1)} %bitcast.21), channel_id=1, replica_groups=mesh['dom'=16,'band'=32] {'band'}, dimensions={0} | all-to-all | bytes 524288 | tf_op jit(solution)/shard_map/all_to_all | solution.py:300
  117.6 1.1 unpack.1
  (2 shorter events, 0.0 us)
Async XLA Ops:
  0.0 0.8 copy-start
  0.8 12.5 %collective-permute-start = (bf16[32,512]{1,0:T(8,128)(2,1)S(1)}, bf16[32,512]{1,0:T(8,128)(2,1)S(1)}, u32[]{:S(2)}, u32[]{:S(2)}) collective-permute-start(bf16[32,512]{1,0:T(8,128)(2,1)S(1)} %dynamic-slice_bitcast_fusion), channel_id=1, source_target_pairs={{256,0},{257,1},{258,2},{259,3},{260,4},{261,5},{262,6},{263,7},{2... | collective-permute-start | bytes 98312 | tf_op jit(solution)/shard_map/ppermute | solution.py:275
  14.1 17.5 %all-to-all-start = ((bf16[8,32,512]{2,1,0:T(8,128)(2,1)}), bf16[8,32,512]{2,1,0:T(8,128)(2,1)S(1)}, u32[]{:S(2)}, u32[]{:S(2)}) async-start(bf16[8,32,512]{2,1,0:T(8,128)(2,1)} %broadcast_in_dim.4), calls=%async_computation | async-start | bytes 524288 | tf_op jit(solution)/shard_map/all_to_all | solution.py:278
  31.6 24.0 %all-to-all-start.1 = ((bf16[16,4,2,16,128]{4,3,2,1,0:T(8,128)(2,1)}), bf16[16,4,2,16,128]{4,3,2,1,0:T(8,128)(2,1)S(1)}, u32[]{:S(2)}, u32[]{:S(2)}) async-start(bf16[16,4,2,16,128]{4,3,2,1,0:T(8,128)(2,1)} %pack.1), calls=%async_computation.1 | async-start | bytes 1048576 | tf_op jit(solution)/shard_map/all_to_all | solution.py:249
  36.6 15.5 %collective-permute-start.3 = (bf16[256,512]{1,0:T(8,128)(2,1)S(1)}, bf16[256,512]{1,0:T(8,128)(2,1)S(1)}, u32[]{:S(2)}, u32[]{:S(2)}) collective-permute-start(bf16[256,512]{1,0:T(8,128)(2,1)S(1)} %bitcast.22), channel_id=1, source_target_pairs={{192,0},{224,32},{0,64},{32,96},{64,128},{96,160},{128,192},{160,2... | collective-permute-start | bytes 786440 | tf_op jit(solution)/shard_map/ppermute | solution.py:262
  40.5 11.7 %collective-permute-start.2 = (bf16[256,512]{1,0:T(8,128)(2,1)S(1)}, bf16[256,512]{1,0:T(8,128)(2,1)S(1)}, u32[]{:S(2)}, u32[]{:S(2)}) collective-permute-start(bf16[256,512]{1,0:T(8,128)(2,1)S(1)} %bitcast.23), channel_id=1, source_target_pairs={{0,256},{32,288},{64,320},{96,352},{128,384},{160,416},{192,448},{... | collective-permute-start | bytes 786440 | tf_op jit(solution)/shard_map/ppermute | solution.py:283
  43.9 9.7 %collective-permute-start.1 = (bf16[256,512]{1,0:T(8,128)(2,1)S(1)}, bf16[256,512]{1,0:T(8,128)(2,1)S(1)}, u32[]{:S(2)}, u32[]{:S(2)}) collective-permute-start(bf16[256,512]{1,0:T(8,128)(2,1)S(1)} %bitcast.24), channel_id=1, source_target_pairs={{64,0},{96,32},{128,64},{160,96},{192,128},{224,160},{0,192},{32,2... | collective-permute-start | bytes 786440 | tf_op jit(solution)/shard_map/ppermute | solution.py:262
  53.7 42.4 %copy-start.1 = (bf16[4,256,512]{2,1,0:T(8,128)(2,1)}, bf16[4,256,512]{2,1,0:T(8,128)(2,1)S(1)}, u32[]{:S(2)}) copy-start(bf16[4,256,512]{2,1,0:T(8,128)(2,1)S(1)} %pad_maximum_fusion.mine) | copy-start | bytes 3145732
  53.7 42.4 %collective-permute-start.4 = (bf16[4,256,512]{2,1,0:T(8,128)(2,1)S(1)}, bf16[4,256,512]{2,1,0:T(8,128)(2,1)}, u32[]{:S(2)}, u32[]{:S(2)}) collective-permute-start(bf16[4,256,512]{2,1,0:T(8,128)(2,1)S(1)} %pad_maximum_fusion.mine), channel_id=1, source_target_pairs={{0,32},{32,0},{64,96},{96,64},{128,160},{160,128},{192,224},{224,1... | collective-permute-start | bytes 3145736 | tf_op jit(solution)/shard_map/ppermute | solution.py:285
  58.5 3.4 %collective-permute-start.5 = (bf16[512,128]{1,0:T(8,128)(2,1)S(1)}, bf16[512,128]{1,0:T(8,128)(2,1)S(1)}, u32[]{:S(2)}, u32[]{:S(2)}) collective-permute-start(bf16[512,128]{1,0:T(8,128)(2,1)S(1)} %get-tuple-element.8), channel_id=1, source_target_pairs={{0,32},{32,0},{64,96},{96,64},{128,160},{160,128},{192,224},{224,1... | collective-permute-start | bytes 393224 | tf_op jit(solution)/shard_map/ppermute | solution.py:288
  96.0 1.2 %copy-start.2 = (bf16[4,256,512]{2,1,0:T(8,128)(2,1)S(1)}, bf16[4,256,512]{2,1,0:T(8,128)(2,1)}, u32[]{:S(2)}) copy-start(bf16[4,256,512]{2,1,0:T(8,128)(2,1)} %copy-done.1) | copy-start | bytes 3145732

commit v11 on v9

--- a/solution.py
+++ b/solution.py
@@ -149,6 +149,26 @@
     )
 
 
+def pack_kernel(n_dom, n_own, cx, cy, nz):
+    def body(bands, pot, out):
+        value = pot[...]
+        high = value.astype(jnp.bfloat16)
+        low = (value - high.astype(jnp.float32)).astype(jnp.bfloat16)
+        for d in range(n_dom):
+            out[d, 0:n_own] = bands[d]
+            out[d, n_own] = high
+            out[d, n_own + 1] = low
+
+    vmem = pl.BlockSpec(memory_space=pltpu.VMEM)
+    return pl.pallas_call(
+        body,
+        out_shape=jax.ShapeDtypeStruct((n_dom, n_own + 2, cx, cy, nz), jnp.bfloat16),
+        in_specs=[vmem, vmem],
+        out_specs=vmem,
+        name="pack",
+    )
+
+
 def rotate_kernel(n_all, n_x, nz):
     half, block = n_all // 2, n_all // n_x
 
@@ -194,12 +214,9 @@
     n_y = n_band // n_x
     core, _ = chip_place(n_x)
 
-    pot = potential[0]
-    high = lax.reduce_precision(pot, 8, 7)
-    parts = jnp.stack([high, pot - high]).astype(jnp.bfloat16)
-    parts = jnp.broadcast_to(parts[None], (n_dom, 2, cx, cy, nz))
-    blocks = orbitals.reshape(n_dom, n_own, cx, cy, nz)
-    blocks = jnp.concatenate([blocks, parts], axis=1)
+    blocks = pack_kernel(n_dom, n_own, cx, cy, nz)(
+        orbitals.reshape(n_dom, n_own, cx, cy, nz), potential[0]
+    )
     blocks = lax.all_to_all(blocks, "dom", 0, 0, tiled=True)
     kept, away = filter_kernel(n_dom, n_own, cx, cy, nz)(in_vmem(blocks))
 
@@ -243,11 +260,8 @@
     n_pair = n_dom // 2
     kept = kept.reshape(n_band * n_pair, n_own, nz)
     away = away.reshape(n_band * n_pair, n_own, nz)
-    rows = lax.select(
-        jnp.broadcast_to(core == 0, (n_band * n_pair, 2 * n_own, nz)),
-        jnp.concatenate([kept, away], axis=1),
-        jnp.concatenate([away, kept], axis=1),
-    )
+    lower = jnp.broadcast_to(core == 0, kept.shape)
+    rows = jnp.stack([lax.select(lower, kept, away), lax.select(lower, away, kept)], axis=1)
     group = [[b * n_dom + 2 * p + c for b in range(n_band) for p in range(n_pair)] for c in (0, 1)]
     rows = lax.all_to_all(
         rows, ("band", "dom"), 0, 0, tiled=True, axis_index_groups=group

time: 115 us -> 115 us (level)
  other arithmetic: 2.49 us -> 0.58 us
  Pallas kernels: 5.09 us -> 6.57 us
    pallas_call x0 -> x1, Pallas kernels: none -> 1.79 us  [on_device(): pack_kernel(n_dom, n_own, cx, cy, nz)]
  transfers between devices with their start and end apart: 8 -> 8, of which waited for: 5 -> 5; matrix products, arithmetic and copies ran while one was open for 2% -> 0% of each run, Pallas kernels for 2% -> 4%
where the time goes in v11:
time: 115 us; the launch traced here: 114 us
  blocking collectives  47.9 us (42%)
  starting transfers between devices  38.7 us (34%)
  waiting for transfers between devices  16.3 us (14%)
  Pallas kernels  6.57 us (6%)
  local copies, waits for them, and re-layouts  3.9 us (3%)
    all_to_all x1, blocking collectives, on_device(): lax.all_to_all(rows, ('band', 'dom'), 0, 0, tiled=True, axis_index_groups...  29.5 us
    all_to_all x1, blocking collectives, on_device(): lax.all_to_all(rotated.reshape(n_band, n_mine, nz), 'band', 0, 0, tiled=T...  18.4 us
    ppermute x1, starting transfers between devices, on_device(): own = lax.ppermute(own, ('dom', 'band'), turned)  10.9 us
    all_to_all x1, waiting for transfers between devices, on_device(): lax.all_to_all(many, 'band', 0, 0, tiled=True, axis_index_groups=lines)  7.78 us
    all_to_all x1, starting transfers between devices, on_device(): lax.all_to_all(many, 'band', 0, 0, tiled=True, axis_index_groups=lines)  7.55 us
    ppermute x2, starting transfers between devices, from_x(): return lax.ppermute(value, 'dom', pairs)  7.5 us
    ppermute x2, waiting for transfers between devices, from_x(): return lax.ppermute(value, 'dom', pairs)  5.97 us
    all_to_all x1, starting transfers between devices, on_device(): blocks = lax.all_to_all(blocks, 'dom', 0, 0, tiled=True)  5.06 us
  transfers between devices with their start and end apart: 8, of which 5 were waited for; matrix products, arithmetic and copies ran while one was open for 0% of the time, Pallas kernels for 4%

profile of v11, /device:TPU:8, one launch (start us, length us, event | category | flops | bytes accessed | tf_op | source)
XLA Modules:
  0.0 114.1 jit_solution(13098350043721363884)
XLA Ops:
  0.0 0.0 copy-start
  0.0 0.8 copy-done
  0.8 10.9 %collective-permute-start = (bf16[32,512]{1,0:T(8,128)(2,1)S(1)}, bf16[32,512]{1,0:T(8,128)(2,1)S(1)}, u32[]{:S(2)}, u32[]{:S(2)}) collective-permute-start(bf16[32,512]{1,0:T(8,128)(2,1)S(1)} %dynamic-slice_bitcast_fusion), channel_id=1, source_target_pairs={{256,0},{257,1},{258,2},{259,3},{260,4},{261,5},{262,6},{263,7},{2... | collective-permute-start | bytes 98312 | tf_op jit(solution)/shard_map/ppermute | solution.py:246
  11.8 1.6 %collective-permute-done = bf16[32,512]{1,0:T(8,128)(2,1)S(1)} collective-permute-done((bf16[32,512]{1,0:T(8,128)(2,1)S(1)}, bf16[32,512]{1,0:T(8,128)(2,1)S(1)}, u32[]{:S(2)}, u32[]{:S(2)}) %collective-permute-start) | collective-permute-done | bytes 32800 | tf_op jit(solution)/shard_map/ppermute | solution.py:246
  13.3 0.7 broadcast_in_dim.4
  14.1 7.5 %all-to-all-start = ((bf16[8,32,512]{2,1,0:T(8,128)(2,1)}), bf16[8,32,512]{2,1,0:T(8,128)(2,1)S(1)}, u32[]{:S(2)}, u32[]{:S(2)}) async-start(bf16[8,32,512]{2,1,0:T(8,128)(2,1)} %broadcast_in_dim.4), calls=%async_computation | async-start | bytes 524288 | tf_op jit(solution)/shard_map/all_to_all | solution.py:249
  21.6 1.8 %pack.1 = bf16[16,4,2,16,128]{4,3,2,1,0:T(8,128)(2,1)} custom-call(bf16[16,2,2,16,128]{4,3,2,1,0:T(8,128)(2,1)} %bitcast.28, f32[2,16,128]{2,1,0:T(8,128)} %bitcast.32), custom_call_target="tpu_custom_call" | custom-call | tf_op jit(solution)/shard_map/pack/pallas_call | solution.py:217
  23.4 7.8 %all-to-all-done = bf16[8,32,512]{2,1,0:T(8,128)(2,1)S(1)} async-done(((bf16[8,32,512]{2,1,0:T(8,128)(2,1)}), bf16[8,32,512]{2,1,0:T(8,128)(2,1)S(1)}, u32[]{:S(2)}, u32[]{:S(2)}) %all-to-all-start) | async-done | bytes 262176 | tf_op jit(solution)/shard_map/all_to_all | solution.py:249
  31.2 5.1 %all-to-all-start.1 = ((bf16[16,4,2,16,128]{4,3,2,1,0:T(8,128)(2,1)}), bf16[16,4,2,16,128]{4,3,2,1,0:T(8,128)(2,1)S(1)}, u32[]{:S(2)}, u32[]{:S(2)}) async-start(bf16[16,4,2,16,128]{4,3,2,1,0:T(8,128)(2,1)} %pack.1), calls=%async_computation.1 | async-start | bytes 1048576 | tf_op jit(solution)/shard_map/all_to_all | solution.py:220
  36.3 3.8 %collective-permute-start.3 = (bf16[256,512]{1,0:T(8,128)(2,1)S(1)}, bf16[256,512]{1,0:T(8,128)(2,1)S(1)}, u32[]{:S(2)}, u32[]{:S(2)}) collective-permute-start(bf16[256,512]{1,0:T(8,128)(2,1)S(1)} %bitcast.22), channel_id=1, source_target_pairs={{192,0},{224,32},{0,64},{32,96},{64,128},{96,160},{128,192},{160,2... | collective-permute-start | bytes 786440 | tf_op jit(solution)/shard_map/ppermute | solution.py:233
  40.1 3.4 %collective-permute-start.2 = (bf16[256,512]{1,0:T(8,128)(2,1)S(1)}, bf16[256,512]{1,0:T(8,128)(2,1)S(1)}, u32[]{:S(2)}, u32[]{:S(2)}) collective-permute-start(bf16[256,512]{1,0:T(8,128)(2,1)S(1)} %bitcast.23), channel_id=1, source_target_pairs={{0,256},{32,288},{64,320},{96,352},{128,384},{160,416},{192,448},{... | collective-permute-start | bytes 786440 | tf_op jit(solution)/shard_map/ppermute | solution.py:254
  43.5 3.7 %collective-permute-start.1 = (bf16[256,512]{1,0:T(8,128)(2,1)S(1)}, bf16[256,512]{1,0:T(8,128)(2,1)S(1)}, u32[]{:S(2)}, u32[]{:S(2)}) collective-permute-start(bf16[256,512]{1,0:T(8,128)(2,1)S(1)} %bitcast.24), channel_id=1, source_target_pairs={{64,0},{96,32},{128,64},{160,96},{192,128},{224,160},{0,192},{32,2... | collective-permute-start | bytes 786440 | tf_op jit(solution)/shard_map/ppermute | solution.py:233
  47.2 4.6 %collective-permute-done.3 = bf16[256,512]{1,0:T(8,128)(2,1)S(1)} collective-permute-done((bf16[256,512]{1,0:T(8,128)(2,1)S(1)}, bf16[256,512]{1,0:T(8,128)(2,1)S(1)}, u32[]{:S(2)}, u32[]{:S(2)}) %collective-permute-start.3) | collective-permute-done | bytes 262176 | tf_op jit(solution)/shard_map/ppermute | solution.py:233
  51.8 0.0 collective-permute-done.2
  51.8 1.3 %collective-permute-done.1 = bf16[256,512]{1,0:T(8,128)(2,1)S(1)} collective-permute-done((bf16[256,512]{1,0:T(8,128)(2,1)S(1)}, bf16[256,512]{1,0:T(8,128)(2,1)S(1)}, u32[]{:S(2)}, u32[]{:S(2)}) %collective-permute-start.1) | collective-permute-done | bytes 262176 | tf_op jit(solution)/shard_map/ppermute | solution.py:233
  53.1 0.1 pad_maximum_fusion.mine
  53.3 0.0 copy-start.1
  53.3 1.9 %collective-permute-start.4 = (bf16[4,256,512]{2,1,0:T(8,128)(2,1)S(1)}, bf16[4,256,512]{2,1,0:T(8,128)(2,1)}, u32[]{:S(2)}, u32[]{:S(2)}) collective-permute-start(bf16[4,256,512]{2,1,0:T(8,128)(2,1)S(1)} %pad_maximum_fusion.mine), channel_id=1, source_target_pairs={{0,32},{32,0},{64,96},{96,64},{128,160},{160,128},{192,224},{224,1... | collective-permute-start | bytes 3145736 | tf_op jit(solution)/shard_map/ppermute | solution.py:256
  55.2 0.0 all-to-all-done.1.blocks
  55.2 2.9 %chebyshev.1 = (bf16[512,128]{1,0:T(8,128)(2,1)S(1)}, bf16[512,128]{1,0:T(8,128)(2,1)S(1)}) custom-call(bf16[16,4,2,16,128]{4,3,2,1,0:T(8,128)(2,1)S(1)} %all-to-all-done.1.blocks), custom_call_target="tpu_custom_call" | custom-call | tf_op jit(solution)/shard_map/chebyshev/pallas_call | solution.py:221
  58.1 2.4 %collective-permute-start.5 = (bf16[512,128]{1,0:T(8,128)(2,1)S(1)}, bf16[512,128]{1,0:T(8,128)(2,1)S(1)}, u32[]{:S(2)}, u32[]{:S(2)}) collective-permute-start(bf16[512,128]{1,0:T(8,128)(2,1)S(1)} %get-tuple-element.8), channel_id=1, source_target_pairs={{0,32},{32,0},{64,96},{96,64},{128,160},{160,128},{192,224},{224,1... | collective-permute-start | bytes 393224 | tf_op jit(solution)/shard_map/ppermute | solution.py:259
  60.5 1.0 collective-permute-done.5
  61.5 0.4 pad_maximum_fusion.1
  61.9 29.5 %all_to_all.20 = bf16[256,2,2,128]{3,2,1,0:T(2,128)(2,1)S(1)} all-to-all(bf16[256,2,2,128]{3,2,1,0:T(2,128)(2,1)S(1)} %pad_maximum_fusion.1), channel_id=1, replica_groups={{0,64,128,192,256,320,384,448,1,65,129,193,257,321,385,449,2,66,130,194..., dimensions={0} | all-to-all | bytes 524288 | tf_op jit(solution)/shard_map/all_to_all | solution.py:266
  91.4 0.0 copy-done.1
  91.4 0.0 collective-permute-done.4.other
  91.4 0.0 copy-start.2
  91.4 1.2 %copy-done.2 = bf16[4,256,512]{2,1,0:T(8,128)(2,1)S(1)} copy-done((bf16[4,256,512]{2,1,0:T(8,128)(2,1)S(1)}, bf16[4,256,512]{2,1,0:T(8,128)(2,1)}, u32[]{:S(2)}) %copy-start.2) | copy-done | bytes 1048600
  92.6 1.9 %rotate.1 = bf16[1024,128]{1,0:T(8,128)(2,1)S(1)} custom-call(bf16[4,256,512]{2,1,0:T(8,128)(2,1)S(1)} %copy-done.2, bf16[4,256,512]{2,1,0:T(8,128)(2,1)} %collective-permute-done.4.other, bf16[1024,128]{1,0:T(8,128)(2,1)S(1)} %bitcast.20), custom_call_target="tpu_custom_call" | custom-call | tf_op jit(solution)/shard_map/rotate/pallas_call | solution.py:270
  94.6 18.4 %all_to_all.21 = bf16[32,32,128]{2,1,0:T(8,128)(2,1)S(1)} all-to-all(bf16[32,32,128]{2,1,0:T(8,128)(2,1)S(1)} %bitcast.21), channel_id=1, replica_groups=mesh['dom'=16,'band'=32] {'band'}, dimensions={0} | all-to-all | bytes 524288 | tf_op jit(solution)/shard_map/all_to_all | solution.py:271
  113.0 0.1 convert_bitcast_fusion
  113.0 1.1 copy.6
  (2 shorter events, 0.0 us)
Async XLA Ops:
  0.0 0.8 copy-start
  0.8 12.5 %collective-permute-start = (bf16[32,512]{1,0:T(8,128)(2,1)S(1)}, bf16[32,512]{1,0:T(8,128)(2,1)S(1)}, u32[]{:S(2)}, u32[]{:S(2)}) collective-permute-start(bf16[32,512]{1,0:T(8,128)(2,1)S(1)} %dynamic-slice_bitcast_fusion), channel_id=1, source_target_pairs={{256,0},{257,1},{258,2},{259,3},{260,4},{261,5},{262,6},{263,7},{2... | collective-permute-start | bytes 98312 | tf_op jit(solution)/shard_map/ppermute | solution.py:246
  14.1 17.1 %all-to-all-start = ((bf16[8,32,512]{2,1,0:T(8,128)(2,1)}), bf16[8,32,512]{2,1,0:T(8,128)(2,1)S(1)}, u32[]{:S(2)}, u32[]{:S(2)}) async-start(bf16[8,32,512]{2,1,0:T(8,128)(2,1)} %broadcast_in_dim.4), calls=%async_computation | async-start | bytes 524288 | tf_op jit(solution)/shard_map/all_to_all | solution.py:249
  31.2 24.0 %all-to-all-start.1 = ((bf16[16,4,2,16,128]{4,3,2,1,0:T(8,128)(2,1)}), bf16[16,4,2,16,128]{4,3,2,1,0:T(8,128)(2,1)S(1)}, u32[]{:S(2)}, u32[]{:S(2)}) async-start(bf16[16,4,2,16,128]{4,3,2,1,0:T(8,128)(2,1)} %pack.1), calls=%async_computation.1 | async-start | bytes 1048576 | tf_op jit(solution)/shard_map/all_to_all | solution.py:220
  36.3 15.5 %collective-permute-start.3 = (bf16[256,512]{1,0:T(8,128)(2,1)S(1)}, bf16[256,512]{1,0:T(8,128)(2,1)S(1)}, u32[]{:S(2)}, u32[]{:S(2)}) collective-permute-start(bf16[256,512]{1,0:T(8,128)(2,1)S(1)} %bitcast.22), channel_id=1, source_target_pairs={{192,0},{224,32},{0,64},{32,96},{64,128},{96,160},{128,192},{160,2... | collective-permute-start | bytes 786440 | tf_op jit(solution)/shard_map/ppermute | solution.py:233
  40.1 11.7 %collective-permute-start.2 = (bf16[256,512]{1,0:T(8,128)(2,1)S(1)}, bf16[256,512]{1,0:T(8,128)(2,1)S(1)}, u32[]{:S(2)}, u32[]{:S(2)}) collective-permute-start(bf16[256,512]{1,0:T(8,128)(2,1)S(1)} %bitcast.23), channel_id=1, source_target_pairs={{0,256},{32,288},{64,320},{96,352},{128,384},{160,416},{192,448},{... | collective-permute-start | bytes 786440 | tf_op jit(solution)/shard_map/ppermute | solution.py:254
  43.5 9.7 %collective-permute-start.1 = (bf16[256,512]{1,0:T(8,128)(2,1)S(1)}, bf16[256,512]{1,0:T(8,128)(2,1)S(1)}, u32[]{:S(2)}, u32[]{:S(2)}) collective-permute-start(bf16[256,512]{1,0:T(8,128)(2,1)S(1)} %bitcast.24), channel_id=1, source_target_pairs={{64,0},{96,32},{128,64},{160,96},{192,128},{224,160},{0,192},{32,2... | collective-permute-start | bytes 786440 | tf_op jit(solution)/shard_map/ppermute | solution.py:233
  53.3 38.1 %copy-start.1 = (bf16[4,256,512]{2,1,0:T(8,128)(2,1)}, bf16[4,256,512]{2,1,0:T(8,128)(2,1)S(1)}, u32[]{:S(2)}) copy-start(bf16[4,256,512]{2,1,0:T(8,128)(2,1)S(1)} %pad_maximum_fusion.mine) | copy-start | bytes 3145732
  53.3 38.1 %collective-permute-start.4 = (bf16[4,256,512]{2,1,0:T(8,128)(2,1)S(1)}, bf16[4,256,512]{2,1,0:T(8,128)(2,1)}, u32[]{:S(2)}, u32[]{:S(2)}) collective-permute-start(bf16[4,256,512]{2,1,0:T(8,128)(2,1)S(1)} %pad_maximum_fusion.mine), channel_id=1, source_target_pairs={{0,32},{32,0},{64,96},{96,64},{128,160},{160,128},{192,224},{224,1... | collective-permute-start | bytes 3145736 | tf_op jit(solution)/shard_map/ppermute | solution.py:256
  58.1 3.4 %collective-permute-start.5 = (bf16[512,128]{1,0:T(8,128)(2,1)S(1)}, bf16[512,128]{1,0:T(8,128)(2,1)S(1)}, u32[]{:S(2)}, u32[]{:S(2)}) collective-permute-start(bf16[512,128]{1,0:T(8,128)(2,1)S(1)} %get-tuple-element.8), channel_id=1, source_target_pairs={{0,32},{32,0},{64,96},{96,64},{128,160},{160,128},{192,224},{224,1... | collective-permute-start | bytes 393224 | tf_op jit(solution)/shard_map/ppermute | solution.py:259
  91.4 1.2 %copy-start.2 = (bf16[4,256,512]{2,1,0:T(8,128)(2,1)S(1)}, bf16[4,256,512]{2,1,0:T(8,128)(2,1)}, u32[]{:S(2)}) copy-start(bf16[4,256,512]{2,1,0:T(8,128)(2,1)} %copy-done.1) | copy-start | bytes 3145732

commit v12 on v9

--- a/solution.py
+++ b/solution.py
@@ -157,12 +157,13 @@
         z_lo = lax.div(lax.axis_index("dom"), 2 * n_x)
         z_hi = lax.div(lax.axis_index("band"), lax.axis_size("band") // n_x)
         first = z_hi + x + 2 * z_lo
+        step = 1 + (n_x - 2) * lax.rem(x, 2)
         near = rows[pl.ds(pl.multiple_of(core * half, half), half), :]
         far = rows[pl.ds(pl.multiple_of((1 - core) * half, half), half), :]
         for r in range(n_x):
             sums = jnp.dot(mine[r], near, preferred_element_type=jnp.float32)
             sums = sums + jnp.dot(other[r], far, preferred_element_type=jnp.float32)
-            at = pl.multiple_of(lax.rem(first + r, n_x) * block, block)
+            at = pl.multiple_of(lax.rem(first + r * step, n_x) * block, block)
             out[pl.ds(at, block), :] = sums.astype(jnp.bfloat16)
 
     vmem = pl.BlockSpec(memory_space=pltpu.VMEM)
@@ -208,11 +209,11 @@
     def split(d):
         return d // (2 * n_x), d // 2 % n_x, d % 2
 
-    def from_x(value, step):
+    def beside_x(value, mask):
         pairs = []
         for d in range(n_dom):
             z, x, c = split(d)
-            pairs.append((z * 2 * n_x + (x + step) % n_x * 2 + c, d))
+            pairs.append((z * 2 * n_x + (x ^ mask) * 2 + c, d))
         return lax.ppermute(value, "dom", pairs)
 
     turned = []
@@ -231,8 +232,8 @@
     lines = [[z * n_y + y for y in range(n_y)] for z in range(n_x)]
     own = lax.all_to_all(many, "band", 0, 0, tiled=True, axis_index_groups=lines)
     own = own.reshape(n_y * n_mine, half)
-    after = from_x(own, 1)
-    before = from_x(own, -1)
+    after = beside_x(own, 1)
+    before = beside_x(own, n_x - 1)
     partner = [(d, (d + n_dom // 2) % n_dom) for d in range(n_dom)]
     far = lax.ppermute(own, "dom", partner)
     mine = jnp.stack([own, after, far, before])

time: 115 us -> 114 us (level)
  blocking collectives: 47.9 us -> 45.8 us
  waiting for transfers between devices: 16.3 us -> 17.8 us
    all_to_all x1, blocking collectives: 29.5 us -> 27.4 us  [on_device(): lax.all_to_all(rows, ('band', 'dom'), 0, 0, tiled=True, axis_index_groups...]
    ppermute x2, waiting for transfers between devices: 5.97 us -> 7.49 us  [beside_x(): return lax.ppermute(value, 'dom', pairs)]
  transfers between devices with their start and end apart: 8 -> 8, of which waited for: 5 -> 5; matrix products, arithmetic and copies ran while one was open for 2% -> 2% of each run, Pallas kernels for 2% -> 3%
where the time goes in v12:
time: 114 us; the launch traced here: 113 us
  blocking collectives  45.8 us (40%)
  starting transfers between devices  38.5 us (34%)
  waiting for transfers between devices  17.8 us (16%)
  Pallas kernels  5.09 us (4%)
  local copies, waits for them, and re-layouts  3.6 us (3%)
  other arithmetic  2.49 us (2%)
    all_to_all x1, blocking collectives, on_device(): lax.all_to_all(rows, ('band', 'dom'), 0, 0, tiled=True, axis_index_groups...  27.4 us
    all_to_all x1, blocking collectives, on_device(): lax.all_to_all(rotated.reshape(n_band, n_mine, nz), 'band', 0, 0, tiled=T...  18.4 us
    ppermute x1, starting transfers between devices, on_device(): own = lax.ppermute(own, ('dom', 'band'), turned)  10.9 us
    all_to_all x1, waiting for transfers between devices, on_device(): lax.all_to_all(many, 'band', 0, 0, tiled=True, axis_index_groups=lines)  7.77 us
    all_to_all x1, starting transfers between devices, on_device(): lax.all_to_all(many, 'band', 0, 0, tiled=True, axis_index_groups=lines)  7.68 us
    ppermute x2, waiting for transfers between devices, beside_x(): return lax.ppermute(value, 'dom', pairs)  7.49 us
    ppermute x2, starting transfers between devices, beside_x(): return lax.ppermute(value, 'dom', pairs)  7.19 us
    all_to_all x1, starting transfers between devices, on_device(): blocks = lax.all_to_all(blocks, 'dom', 0, 0, tiled=True)  5.06 us
  transfers between devices with their start and end apart: 8, of which 5 were waited for; matrix products, arithmetic and copies ran while one was open for 2% of the time, Pallas kernels for 3%

profile of v12, /device:TPU:8, one launch (start us, length us, event | category | flops | bytes accessed | tf_op | source)
XLA Modules:
  0.0 113.5 jit_solution(3651921170053375007)
XLA Ops:
  0.0 0.0 copy-start
  0.0 0.8 copy-done
  0.8 10.9 %collective-permute-start = (bf16[32,512]{1,0:T(8,128)(2,1)S(1)}, bf16[32,512]{1,0:T(8,128)(2,1)S(1)}, u32[]{:S(2)}, u32[]{:S(2)}) collective-permute-start(bf16[32,512]{1,0:T(8,128)(2,1)S(1)} %dynamic-slice_bitcast_fusion), channel_id=1, source_target_pairs={{256,0},{257,1},{258,2},{259,3},{260,4},{261,5},{262,6},{263,7},{2... | collective-permute-start | bytes 98312 | tf_op jit(solution)/shard_map/ppermute | solution.py:230
  11.8 1.6 %collective-permute-done = bf16[32,512]{1,0:T(8,128)(2,1)S(1)} collective-permute-done((bf16[32,512]{1,0:T(8,128)(2,1)S(1)}, bf16[32,512]{1,0:T(8,128)(2,1)S(1)}, u32[]{:S(2)}, u32[]{:S(2)}) %collective-permute-start) | collective-permute-done | bytes 32800 | tf_op jit(solution)/shard_map/ppermute | solution.py:230
  13.3 0.7 broadcast_in_dim.6
  14.1 0.0 copy-start.2
  14.1 7.7 %all-to-all-start = ((bf16[8,32,512]{2,1,0:T(8,128)(2,1)}), bf16[8,32,512]{2,1,0:T(8,128)(2,1)S(1)}, u32[]{:S(2)}, u32[]{:S(2)}) async-start(bf16[8,32,512]{2,1,0:T(8,128)(2,1)} %broadcast_in_dim.6), calls=%async_computation | async-start | bytes 524288 | tf_op jit(solution)/shard_map/all_to_all | solution.py:233
  21.8 0.0 copy-done.2
  21.8 0.0 copy-start.1
  21.8 0.9 copy-done.1
  22.7 0.8 pad_maximum_fusion.1
  23.5 7.8 %all-to-all-done = bf16[8,32,512]{2,1,0:T(8,128)(2,1)S(1)} async-done(((bf16[8,32,512]{2,1,0:T(8,128)(2,1)}), bf16[8,32,512]{2,1,0:T(8,128)(2,1)S(1)}, u32[]{:S(2)}, u32[]{:S(2)}) %all-to-all-start) | async-done | bytes 262176 | tf_op jit(solution)/shard_map/all_to_all | solution.py:233
  31.3 5.1 %all-to-all-start.1 = ((bf16[16,4,2,16,128]{4,3,2,1,0:T(8,128)(2,1)}), bf16[16,4,2,16,128]{4,3,2,1,0:T(8,128)(2,1)S(1)}, u32[]{:S(2)}, u32[]{:S(2)}) async-start(bf16[16,4,2,16,128]{4,3,2,1,0:T(8,128)(2,1)} %pad_maximum_fusion.1), calls=%async_computation.1 | async-start | bytes 1048576 | tf_op jit(solution)/shard_map/all_to_all | solution.py:204
  36.4 5.0 %collective-permute-start.3 = (bf16[256,512]{1,0:T(8,128)(2,1)S(1)}, bf16[256,512]{1,0:T(8,128)(2,1)S(1)}, u32[]{:S(2)}, u32[]{:S(2)}) collective-permute-start(bf16[256,512]{1,0:T(8,128)(2,1)S(1)} %bitcast.18), channel_id=1, source_target_pairs={{192,0},{224,32},{128,64},{160,96},{64,128},{96,160},{0,192},{32,2... | collective-permute-start | bytes 786440 | tf_op jit(solution)/shard_map/ppermute | solution.py:217
  41.4 3.4 %collective-permute-start.2 = (bf16[256,512]{1,0:T(8,128)(2,1)S(1)}, bf16[256,512]{1,0:T(8,128)(2,1)S(1)}, u32[]{:S(2)}, u32[]{:S(2)}) collective-permute-start(bf16[256,512]{1,0:T(8,128)(2,1)S(1)} %bitcast.19), channel_id=1, source_target_pairs={{0,256},{32,288},{64,320},{96,352},{128,384},{160,416},{192,448},{... | collective-permute-start | bytes 786440 | tf_op jit(solution)/shard_map/ppermute | solution.py:238
  44.8 2.2 %collective-permute-start.1 = (bf16[256,512]{1,0:T(8,128)(2,1)S(1)}, bf16[256,512]{1,0:T(8,128)(2,1)S(1)}, u32[]{:S(2)}, u32[]{:S(2)}) collective-permute-start(bf16[256,512]{1,0:T(8,128)(2,1)S(1)} %bitcast.20), channel_id=1, source_target_pairs={{64,0},{96,32},{0,64},{32,96},{192,128},{224,160},{128,192},{160,2... | collective-permute-start | bytes 786440 | tf_op jit(solution)/shard_map/ppermute | solution.py:217
  47.0 4.9 %collective-permute-done.3 = bf16[256,512]{1,0:T(8,128)(2,1)S(1)} collective-permute-done((bf16[256,512]{1,0:T(8,128)(2,1)S(1)}, bf16[256,512]{1,0:T(8,128)(2,1)S(1)}, u32[]{:S(2)}, u32[]{:S(2)}) %collective-permute-start.3) | collective-permute-done | bytes 262176 | tf_op jit(solution)/shard_map/ppermute | solution.py:217
  51.9 0.0 collective-permute-done.2
  51.9 2.5 %collective-permute-done.1 = bf16[256,512]{1,0:T(8,128)(2,1)S(1)} collective-permute-done((bf16[256,512]{1,0:T(8,128)(2,1)S(1)}, bf16[256,512]{1,0:T(8,128)(2,1)S(1)}, u32[]{:S(2)}, u32[]{:S(2)}) %collective-permute-start.1) | collective-permute-done | bytes 262176 | tf_op jit(solution)/shard_map/ppermute | solution.py:217
  54.5 1.1 pad_maximum_fusion.mine
  55.6 1.9 %collective-permute-start.4 = (bf16[4,256,512]{2,1,0:T(8,128)(2,1)}, bf16[4,256,512]{2,1,0:T(8,128)(2,1)}, u32[]{:S(2)}, u32[]{:S(2)}) collective-permute-start(bf16[4,256,512]{2,1,0:T(8,128)(2,1)} %pad_maximum_fusion.mine), channel_id=1, source_target_pairs={{0,32},{32,0},{64,96},{96,64},{128,160},{160,128},{192,224},{224,1... | collective-permute-start | bytes 3145736 | tf_op jit(solution)/shard_map/ppermute | solution.py:240
  57.5 0.0 all-to-all-done.1.blocks
  57.5 2.9 %chebyshev.1 = (bf16[512,128]{1,0:T(8,128)(2,1)S(1)}, bf16[512,128]{1,0:T(8,128)(2,1)S(1)}) custom-call(bf16[16,4,2,16,128]{4,3,2,1,0:T(8,128)(2,1)S(1)} %all-to-all-done.1.blocks), custom_call_target="tpu_custom_call" | custom-call | tf_op jit(solution)/shard_map/chebyshev/pallas_call | solution.py:205
  60.4 2.4 %collective-permute-start.5 = (bf16[512,128]{1,0:T(8,128)(2,1)S(1)}, bf16[512,128]{1,0:T(8,128)(2,1)S(1)}, u32[]{:S(2)}, u32[]{:S(2)}) collective-permute-start(bf16[512,128]{1,0:T(8,128)(2,1)S(1)} %get-tuple-element.8), channel_id=1, source_target_pairs={{0,32},{32,0},{64,96},{96,64},{128,160},{160,128},{192,224},{224,1... | collective-permute-start | bytes 393224 | tf_op jit(solution)/shard_map/ppermute | solution.py:243
  62.8 1.0 collective-permute-done.5
  63.8 0.5 maximum_select_fusion
  64.2 27.4 %all_to_all.20 = bf16[256,4,128]{2,1,0:T(4,128)(2,1)S(1)} all-to-all(bf16[256,4,128]{2,1,0:T(4,128)(2,1)S(1)} %maximum_select_fusion), channel_id=1, replica_groups={{0,64,128,192,256,320,384,448,1,65,129,193,257,321,385,449,2,66,130,194..., dimensions={0} | all-to-all | bytes 524288 | tf_op jit(solution)/shard_map/all_to_all | solution.py:253
  91.6 0.0 collective-permute-done.4.other
  91.6 2.2 %rotate.1 = bf16[1024,128]{1,0:T(8,128)(2,1)S(1)} custom-call(bf16[4,256,512]{2,1,0:T(8,128)(2,1)} %pad_maximum_fusion.mine, bf16[4,256,512]{2,1,0:T(8,128)(2,1)} %collective-permute-done.4.other, bf16[1024,128]{1,0:T(8,128)(2,1)S(1)} %bitcast.15), custom_call_target="tpu_custom_call" | custom-call | tf_op jit(solution)/shard_map/rotate/pallas_call | solution.py:257
  93.9 18.4 %all_to_all.21 = bf16[32,32,128]{2,1,0:T(8,128)(2,1)S(1)} all-to-all(bf16[32,32,128]{2,1,0:T(8,128)(2,1)S(1)} %bitcast.16), channel_id=1, replica_groups=mesh['dom'=16,'band'=32] {'band'}, dimensions={0} | all-to-all | bytes 524288 | tf_op jit(solution)/shard_map/all_to_all | solution.py:258
  112.3 0.1 convert_bitcast_fusion
  112.3 1.1 copy.4
  (4 shorter events, 0.1 us)
Async XLA Ops:
  0.0 0.8 copy-start
  0.8 12.5 %collective-permute-start = (bf16[32,512]{1,0:T(8,128)(2,1)S(1)}, bf16[32,512]{1,0:T(8,128)(2,1)S(1)}, u32[]{:S(2)}, u32[]{:S(2)}) collective-permute-start(bf16[32,512]{1,0:T(8,128)(2,1)S(1)} %dynamic-slice_bitcast_fusion), channel_id=1, source_target_pairs={{256,0},{257,1},{258,2},{259,3},{260,4},{261,5},{262,6},{263,7},{2... | collective-permute-start | bytes 98312 | tf_op jit(solution)/shard_map/ppermute | solution.py:230
  14.1 7.7 %copy-start.2 = (f32[1,2,16,128]{3,2,1,0:T(8,128)S(1)}, f32[1,2,16,128]{3,2,1,0:T(8,128)}, u32[]{:S(2)}) copy-start(f32[1,2,16,128]{3,2,1,0:T(8,128)} %param.4) | copy-start | bytes 49156
  14.1 17.2 %all-to-all-start = ((bf16[8,32,512]{2,1,0:T(8,128)(2,1)}), bf16[8,32,512]{2,1,0:T(8,128)(2,1)S(1)}, u32[]{:S(2)}, u32[]{:S(2)}) async-start(bf16[8,32,512]{2,1,0:T(8,128)(2,1)} %broadcast_in_dim.6), calls=%async_computation | async-start | bytes 524288 | tf_op jit(solution)/shard_map/all_to_all | solution.py:233
  21.8 1.0 copy-start.1
  31.3 26.2 %all-to-all-start.1 = ((bf16[16,4,2,16,128]{4,3,2,1,0:T(8,128)(2,1)}), bf16[16,4,2,16,128]{4,3,2,1,0:T(8,128)(2,1)S(1)}, u32[]{:S(2)}, u32[]{:S(2)}) async-start(bf16[16,4,2,16,128]{4,3,2,1,0:T(8,128)(2,1)} %pad_maximum_fusion.1), calls=%async_computation.1 | async-start | bytes 1048576 | tf_op jit(solution)/shard_map/all_to_all | solution.py:204
  36.4 15.5 %collective-permute-start.3 = (bf16[256,512]{1,0:T(8,128)(2,1)S(1)}, bf16[256,512]{1,0:T(8,128)(2,1)S(1)}, u32[]{:S(2)}, u32[]{:S(2)}) collective-permute-start(bf16[256,512]{1,0:T(8,128)(2,1)S(1)} %bitcast.18), channel_id=1, source_target_pairs={{192,0},{224,32},{128,64},{160,96},{64,128},{96,160},{0,192},{32,2... | collective-permute-start | bytes 786440 | tf_op jit(solution)/shard_map/ppermute | solution.py:217
  41.4 10.5 %collective-permute-start.2 = (bf16[256,512]{1,0:T(8,128)(2,1)S(1)}, bf16[256,512]{1,0:T(8,128)(2,1)S(1)}, u32[]{:S(2)}, u32[]{:S(2)}) collective-permute-start(bf16[256,512]{1,0:T(8,128)(2,1)S(1)} %bitcast.19), channel_id=1, source_target_pairs={{0,256},{32,288},{64,320},{96,352},{128,384},{160,416},{192,448},{... | collective-permute-start | bytes 786440 | tf_op jit(solution)/shard_map/ppermute | solution.py:238
  44.8 9.7 %collective-permute-start.1 = (bf16[256,512]{1,0:T(8,128)(2,1)S(1)}, bf16[256,512]{1,0:T(8,128)(2,1)S(1)}, u32[]{:S(2)}, u32[]{:S(2)}) collective-permute-start(bf16[256,512]{1,0:T(8,128)(2,1)S(1)} %bitcast.20), channel_id=1, source_target_pairs={{64,0},{96,32},{0,64},{32,96},{192,128},{224,160},{128,192},{160,2... | collective-permute-start | bytes 786440 | tf_op jit(solution)/shard_map/ppermute | solution.py:217
  55.6 36.1 %collective-permute-start.4 = (bf16[4,256,512]{2,1,0:T(8,128)(2,1)}, bf16[4,256,512]{2,1,0:T(8,128)(2,1)}, u32[]{:S(2)}, u32[]{:S(2)}) collective-permute-start(bf16[4,256,512]{2,1,0:T(8,128)(2,1)} %pad_maximum_fusion.mine), channel_id=1, source_target_pairs={{0,32},{32,0},{64,96},{96,64},{128,160},{160,128},{192,224},{224,1... | collective-permute-start | bytes 3145736 | tf_op jit(solution)/shard_map/ppermute | solution.py:240
  60.4 3.4 %collective-permute-start.5 = (bf16[512,128]{1,0:T(8,128)(2,1)S(1)}, bf16[512,128]{1,0:T(8,128)(2,1)S(1)}, u32[]{:S(2)}, u32[]{:S(2)}) collective-permute-start(bf16[512,128]{1,0:T(8,128)(2,1)S(1)} %get-tuple-element.8), channel_id=1, source_target_pairs={{0,32},{32,0},{64,96},{96,64},{128,160},{160,128},{192,224},{224,1... | collective-permute-start | bytes 393224 | tf_op jit(solution)/shard_map/ppermute | solution.py:243
